TPU v7x, 32 devices: a whole 2x2x4 slice. The times are simulated.
32 devices in a mesh: groups: 2 (over y), tile: 4 (over z), col: 2 (over x), rep: 2 (over core).
Axes of the slice: x: 2, y: 2, z: 4, core: 2. Of those that a mesh axis runs over, the one named last changes fastest.
Arguments:
- forcing: bfloat16 [4, 20, 32, 2048], P(('groups', 'rep'), 'tile', None, 'col'), parts along dimension 0, may hold values from -6 to 6
- member_kernel_weight: bfloat16 [20, 576, 64], P('tile'), may hold values from -0.25 to 0.25
- member_counts: int32 [4], P('tile'), may hold values from 1 to 5, 16 in all
- mixing_input_weight: bfloat16 [1280, 512], P('tile'), may hold values from -0.1875 to 0.1875
- depth_weight: float32 [9, 512], replicated, may hold values from -2 to 2
- mix_weight: bfloat16 [512, 512], replicated, may hold values from -0.25 to 0.25
- cotangent: bfloat16 [4, 32, 32, 512], P(('groups', 'rep'), 'tile', 'col'), parts along dimension 0, may hold values from -6 to 6
Outputs:
- adjusted: bfloat16 [4, 32, 32, 512], P(('groups', 'rep'), 'tile', 'col'), parts along dimension 0
- mix_grad: float32 [1024, 512], P(('groups', 'tile', 'col', 'rep')), parts along dimension 0
- depth_grad: float32 [18, 512], P('groups'), parts along dimension 0
- in_grad: float32 [2560, 512], P(('groups', 'tile')), parts along dimension 0
- group_grad: float32 [40, 576, 64], P(('groups', 'tile')), parts along dimension 0
There are 2 independent parts, one for each index of `groups`. A program takes and returns all parts, laid end to end along the dimension named above; an argument that names none is the same for every part. Nothing has to cross between parts.
Inputs may be any that keep to these rules, and one draw needn't show every extreme that they name: member_counts sums to 16; each index of tile holds at least one member and at least one holds 5.
All inputs are finite; a program needn't handle non-finite values. No bound on the sum of `member_counts` on one device may be relied on, other than what follows from the above.
Results may differ from a plain program's by a relative error of at most 0.011.
Values may be sent and summed in bfloat16 or wider, within the bound.
No kernel may reach another device: no remote copies, remote signals or barrier semaphores. Data moves between devices by JAX's collectives and lax.ppermute only.
A program may use at most 64 MiB of HBM per device.

v0:
```python
import functools
import math

import jax
import jax.numpy as jnp
from jax import lax
from jax.experimental import pallas as pl
from jax.experimental.pallas import tpu as pltpu
from jax.sharding import PartitionSpec as P


F32 = jnp.float32
BF16 = jnp.bfloat16
LANES = 128
ROWS = 8
VMEM = pl.BlockSpec(memory_space=pltpu.VMEM)
SMEM = pl.BlockSpec(memory_space=pltpu.SMEM)
HBM = pl.BlockSpec(memory_space=pltpu.HBM)


def swap(value, axis, step):
    return lax.ppermute(value, axis, [(i, i ^ step) for i in range(lax.axis_size(axis))])


def with_neighbours(values, axis):
    count = lax.axis_size(axis)
    received = []
    for first, value in enumerate(values):
        pairs = [(i, i + 1) for i in range(first, count - 1, 2)]
        received.append(lax.ppermute(value, axis, pairs + [(b, a) for a, b in pairs]))
    return received


def in_order(received, axis):
    even = lax.axis_index(axis) % 2 == 0
    near = received[0]
    far = received[1] if len(received) > 1 else jnp.zeros_like(near)
    return jnp.where(even, far, near), jnp.where(even, near, far)


def tree_sum(terms):
    while len(terms) > 1:
        terms = [a + b for a, b in zip(terms[::2], terms[1::2])] + terms[len(terms) & ~1 :]
    return terms[0]


def full_sum(keep, send):
    total = (keep.astype(F32) + swap(send, "rep", 1).astype(F32)).astype(BF16)
    step = 1
    while step < lax.axis_size("col"):
        total = (total.astype(F32) + swap(total, "col", step).astype(F32)).astype(BF16)
        step *= 2
    remote = swap(total, "rep", 1)
    first = lax.axis_index("rep") == 0
    return jnp.concatenate([jnp.where(first, total, remote), jnp.where(first, remote, total)], axis=0)


def silu_slope(value):
    sig = 1.0 / (1.0 + jnp.exp(-value))
    return sig * (1.0 + value * (1.0 - sig))


def lane_below(shape, bound):
    return lax.broadcasted_iota(jnp.int32, shape, len(shape) - 1) < bound


def interleave(first, second):
    half = LANES // 2
    low = lane_below(first.shape, half)
    axis = first.ndim - 1
    return (
        jnp.where(low, first, pltpu.roll(second, half, axis)),
        jnp.where(low, pltpu.roll(first, half, axis), second),
    )


def window_rows(field_ref, near, far, even, slot):
    left, right = jnp.where(even, far, near), jnp.where(even, near, far)
    whole = jnp.concatenate([left, field_ref[slot].astype(F32), right], axis=1)
    half = LANES // 2
    tiles = [whole[:, i : i + LANES] for i in range(0, whole.shape[1], LANES)]
    low = lane_below(tiles[0].shape, half)
    tiles = [pltpu.roll(t, half, 1) for t in tiles]
    middle = jnp.concatenate([jnp.where(low, a, b) for a, b in zip(tiles, tiles[1:])], axis=1)
    height = middle.shape[0]
    row = lax.broadcasted_iota(jnp.int32, middle.shape, 0)
    above = jnp.where(row == 0, 0.0, pltpu.roll(middle, 1, 0))
    below = jnp.where(row == height - 1, 0.0, pltpu.roll(middle, height - 1, 0))
    return above, middle, below


def pair_weight(kernel_ref, slot):
    weight = kernel_ref[slot].astype(F32)
    span = weight.shape[1] // 3
    parts = [weight[:, a * span : (a + 1) * span] for a in range(3)]
    blank = jnp.zeros((weight.shape[0], LANES // 2), F32)
    first = jnp.concatenate([x for part in parts for x in (part, blank)], axis=1)
    second = jnp.concatenate([x for part in parts for x in (blank, part)], axis=1)
    return jnp.concatenate([first, second], axis=0).astype(BF16)


def prepare_kernel(edges_out, field, kernel, weight, upstream, *refs):
    field_ref, pair_ref, weight_ref, upstream_ref = refs[:4]
    field_edges, refs = refs[4 : 4 + edges_out[0]], refs[4 + edges_out[0] :]
    upstream_edges, row_edges = refs[: edges_out[0]], refs[edges_out[0] : -2]
    kernel_ref, sems = refs[-2:]
    depth = weight.shape[0]
    copies = [
        pltpu.make_async_copy(source, target, sems.at[i])
        for i, (source, target) in enumerate(
            (
                (field, field_ref),
                (upstream, upstream_ref),
                (kernel, kernel_ref),
                (weight, weight_ref.at[pl.ds(0, depth), :]),
            )
        )
    ]
    for copy in copies:
        copy.start()
    if weight_ref.shape[0] > depth:
        weight_ref[depth:, :] = jnp.zeros((weight_ref.shape[0] - depth, weight_ref.shape[1]), BF16)
    even = lax.rem(lax.axis_index("col"), 2) == 0
    reach = field_edges[0].shape[2]
    copies[0].wait()
    low, high = field_ref[:, :, :reach], field_ref[:, :, field_ref.shape[2] - reach :]
    for i, ref in enumerate(field_edges):
        ref[...] = jnp.where(even, low, high) if i else jnp.where(even, high, low)
    copies[1].wait()
    cells = upstream_ref[...].astype(F32)
    low, high = cells[:, 0, :], cells[:, cells.shape[1] - 1, :]
    for i, ref in enumerate(upstream_edges):
        ref[...] = (jnp.where(even, low, high) if i else jnp.where(even, high, low)).astype(BF16)
    even = lax.rem(lax.axis_index("tile"), 2) == 0
    low, high = upstream_ref[0], upstream_ref[upstream_ref.shape[0] - 1]
    for i, ref in enumerate(row_edges):
        ref[...] = jnp.where(even, low, high) if i else jnp.where(even, high, low)
    copies[2].wait()
    for slot in range(kernel_ref.shape[0]):
        pair_ref[slot] = pair_weight(kernel_ref, slot)
    copies[3].wait()


def slot_inputs(field_ref, kernel_ref, halo_refs, slot):
    even = lax.rem(lax.axis_index("col"), 2) == 0
    near = halo_refs[0][slot].astype(F32)
    far = halo_refs[1][slot].astype(F32) if len(halo_refs) > 1 else jnp.zeros_like(near)
    return window_rows(field_ref, near, far, even, slot), kernel_ref[slot]


def gate_of(shifted, weight):
    shifted = [s.astype(BF16) for s in shifted]
    pairs = shifted[0].shape[1] // LANES - 1
    lhs = jnp.concatenate(
        [
            jnp.concatenate([s[:, p * LANES : (p + 2) * LANES] for s in shifted], axis=1)
            for p in range(pairs)
        ],
        axis=0,
    )
    gate = lax.dot_general(lhs, weight, (((1,), (1,)), ((), ())), preferred_element_type=F32)
    return gate.reshape(pairs, -1, LANES)


def features_kernel(tiles, count_ref, field_ref, kernel_ref, weight_ref, *refs):
    halo_refs, out_refs, store = refs[: -tiles - 1], refs[-tiles - 1 : -1], refs[-1]
    slots, height, lanes = field_ref.shape
    pairs = lanes // LANES + 2
    main = ROWS * pairs
    col = lax.axis_index("col")

    def values(slot):
        shifted, weight = slot_inputs(field_ref, kernel_ref, halo_refs, slot)
        gate = gate_of(shifted, weight)
        value = gate / (1.0 + jnp.exp(-gate))
        live = slot < count_ref[0]
        first = jnp.where(live & (col > 0), value[:1], 0.0)
        last = jnp.where(live & (col < lax.axis_size("col") - 1), value[-1:], 0.0)
        return jnp.concatenate([first, jnp.where(live, value[1:-1], 0.0), last], axis=0)

    def around(bands, j):
        none = jnp.zeros_like(bands[0])
        sub = lax.broadcasted_iota(jnp.int32, none.shape, 1)
        both = jnp.where(sub >= 4, bands[j - 1] if j else none, bands[j + 1] if j + 1 < len(bands) else none)
        packed = [
            jnp.where(sub[0] < 4, pltpu.roll(both[q], 2, 0), pltpu.roll(both[q + 1], 6, 0))
            for q in range(0, pairs, 2)
        ]
        return jnp.concatenate(packed, axis=0)

    def put(both, lane_tile):
        here = slice(lane_tile * LANES, (lane_tile + 1) * LANES)
        bands = [[v[:, ROWS * j : ROWS * (j + 1)] for j in range(height // ROWS)] for v in both]
        for j in range(height // ROWS):
            for half in range(2):
                rows = bands[half][j].reshape(main, LANES)
                store[j, half * main : (half + 1) * main, here] = rows.astype(BF16)
            halo = jnp.concatenate([around(bands[half], j) for half in range(2)], axis=0)
            store[j, 2 * main :, here] = halo.astype(BF16)

    for slot in range(0, slots - 1, 2):
        put(interleave(values(slot), values(slot + 1)), slot // 2)
    if slots % 2:
        last = values(slots - 1)
        put(interleave(last, jnp.zeros_like(last)), slots // 2)
    for step, out in enumerate(out_refs):
        band = lax.bitwise_xor(lax.axis_index("tile"), step)
        out[...] = jnp.dot(store[band], weight_ref[...], preferred_element_type=F32).astype(BF16)


def backward_inputs_kernel(count_ref, field_ref, kernel_ref, *refs):
    halo_refs, (patch_ref, own_ref) = refs[:-2], refs[-2:]
    slots, height, lanes = field_ref.shape
    pairs = lanes // LANES
    bands = height // ROWS

    def by_band(value):
        return jnp.concatenate([value[:, ROWS * j : ROWS * (j + 1)] for j in range(bands)], axis=0)

    def values(slot):
        shifted, weight = slot_inputs(field_ref, kernel_ref, halo_refs, slot)
        gate = gate_of(shifted, weight)[1:-1]
        live = slot < count_ref[0]
        slope = by_band(jnp.where(live, silu_slope(gate), 0.0))
        patch_ref[slot, :, 6 * LANES :] = slope.reshape(-1, LANES).astype(BF16)
        for a, s in enumerate(shifted):
            patch = jnp.concatenate(
                [
                    s[ROWS * j : ROWS * (j + 1), p * LANES : (p + 2) * LANES]
                    for j in range(bands)
                    for p in range(1, pairs + 1)
                ],
                axis=0,
            )
            patch_ref[slot, :, 2 * a * LANES : 2 * (a + 1) * LANES] = patch.astype(BF16)
        return jnp.where(live, gate / (1.0 + jnp.exp(-gate)), 0.0)

    def put(even, odd, lane_tile):
        span = ROWS * pairs
        for j in range(bands):
            for half, value in enumerate((even, odd)):
                rows = value[:, ROWS * j : ROWS * (j + 1)].reshape(span, LANES)
                own_ref[
                    (2 * j + half) * span : (2 * j + half + 1) * span,
                    lane_tile * LANES : (lane_tile + 1) * LANES,
                ] = rows.astype(BF16)

    for slot in range(0, slots - 1, 2):
        put(*interleave(values(slot), values(slot + 1)), slot // 2)
    if slots % 2:
        last = values(slots - 1)
        put(*interleave(last, jnp.zeros_like(last)), slots // 2)


def upstream_kernel(main_ref, left_ref, right_ref, top_ref, bottom_ref, mix_ref, grad_ref, rows_ref):
    width = grad_ref.shape[0] - 2
    cells, hidden = main_ref.shape
    rows_ref[...] = jnp.zeros_like(rows_ref)
    places = (0, cells, cells + 16, cells + 32, cells + 32 + width)
    for place, ref in zip(places, (main_ref, left_ref, right_ref, top_ref, bottom_ref)):
        rows_ref[place : place + ref.shape[0], :] = ref[...]
    shape = ((width + 2) * 16, rows_ref.shape[0])
    target = lax.broadcasted_iota(jnp.int32, shape, 0)
    source = lax.broadcasted_iota(jnp.int32, shape, 1)
    column, row = lax.shift_right_logical(target, 4), target & 15
    want = (row - 1) * width + (column - 1)
    want = jnp.where(row == 0, places[3] + column - 1, want)
    want = jnp.where(row == ROWS + 1, places[4] + column - 1, want)
    want = jnp.where(column == 0, places[1] + row, want)
    want = jnp.where(column == width + 1, places[2] + row, want)
    want = jnp.where(row > ROWS + 1, -1, want)
    pick = jnp.where(source == want, 1.0, 0.0).astype(BF16)
    picked = jnp.dot(pick, rows_ref[...], preferred_element_type=F32).astype(BF16)
    grad = jnp.dot(picked, mix_ref[...], preferred_element_type=F32)
    grad_ref[...] = grad.reshape(width + 2, 16, hidden)


TAPS = [(a, b) for a in range(3) for b in range(3)]


def middle_kernel(tiles, grad_ref, depth_ref, *refs):
    term_refs, (act_grad_ref, hidden_ref, act, inner) = refs[:tiles], refs[tiles:]
    width, hidden = grad_ref.shape[0] - 2, grad_ref.shape[2]
    pairs = width // 2 + 2
    main = ROWS * pairs
    chunks = [(n, slice(n * LANES, (n + 1) * LANES)) for n in range(hidden // LANES)]
    for n, here in chunks:
        total = tree_sum([ref[:, here].astype(F32) for ref in term_refs]).astype(BF16).astype(F32)
        for p in range(pairs):
            for half in range(2):
                start = half * main + ROWS * p
                act[n, 2 * p + half, 2 : 2 + ROWS, :] = total[start : start + ROWS]
                start = 2 * main + half * main // 2 + 4 * p
                act[n, 2 * p + half, 0:2, :] = total[start : start + 2]
                act[n, 2 * p + half, 2 + ROWS : 4 + ROWS, :] = total[start + 2 : start + 4]

    def forward(column, carry):
        for n, here in chunks:
            terms = [
                depth_ref[3 * a + b : 3 * a + b + 1, here] * act[n, column + b, a : a + ROWS + 2, :] for a, b in TAPS
            ]
            before = tree_sum(terms)
            sig = 1.0 / (1.0 + jnp.exp(-before))
            slope = sig * (1.0 + before * (1.0 - sig))
            grad = grad_ref[column, 0 : ROWS + 2, here] * slope
            inner[n, column, 0 : ROWS + 2, :] = grad.astype(BF16).astype(F32)
            hidden_ref[column, :, here] = (before * sig)[1 : ROWS + 1]
        return carry

    lax.fori_loop(0, width + 2, forward, 0)

    def backward(column, carry):
        place = lax.shift_right_logical(column, 1) + (column & 1) * (width // 2)
        for n, here in chunks:
            terms = [
                depth_ref[3 * a + b : 3 * a + b + 1, here] * inner[n, column + 2 - b, 2 - a : 2 - a + ROWS, :]
                for a, b in TAPS
            ]
            act_grad_ref[place, :, here] = tree_sum(terms).astype(BF16)
        return carry

    lax.fori_loop(0, width, backward, 0)


def finish_kernel(hidden_ref, upstream_ref, mix_ref, act, inner, adjusted_ref, keep_ref, send_ref, held):
    chunks, columns = act.shape[:2]
    width = columns - 4
    cells, hidden = upstream_ref.shape
    target = lax.broadcasted_iota(jnp.int32, (cells, cells), 0)
    source = lax.broadcasted_iota(jnp.int32, (cells, cells), 1)
    pick = (source & (ROWS - 1)) * width + lax.shift_right_logical(source, 3) == target
    pick = jnp.where(pick, 1.0, 0.0).astype(BF16)
    by_column = hidden_ref[1 : width + 1].reshape(cells, hidden).astype(BF16)
    value = jnp.dot(pick, by_column, preferred_element_type=F32).astype(BF16)
    adjusted_ref[...] = lax.dot_general(
        value, mix_ref[...], (((1,), (1,)), ((), ())), preferred_element_type=F32
    ).astype(BF16)
    held[...] = lax.dot_general(
        upstream_ref[...], value, (((0,), (0,)), ((), ())), preferred_element_type=F32
    ).astype(BF16)

    def add(column, sums):
        new = []
        for n in range(chunks):
            own = inner[n, column + 1, 1 : 1 + ROWS, :]
            for t, (a, b) in enumerate(TAPS):
                new.append(sums[n * 9 + t] + act[n, column + 1 + b, 1 + a : 1 + a + ROWS, :] * own)
        return tuple(new)

    zero = jnp.zeros((ROWS, LANES), F32)
    sums = lax.fori_loop(0, width, add, (zero,) * (9 * chunks))
    rows = []
    for n in range(chunks):
        taps = [jnp.sum(sums[n * 9 + t], axis=0, keepdims=True) for t in range(9)]
        rows.append(jnp.concatenate(taps + [jnp.zeros((7, LANES), F32)], axis=0))
    depth = jnp.concatenate(rows, axis=1).astype(BF16)
    rep = lax.axis_index("rep")
    block = hidden // (lax.axis_size("tile") * lax.axis_size("col") * lax.axis_size("rep"))
    for ref, which in ((keep_ref, rep), (send_ref, 1 - rep)):
        for g in range((keep_ref.shape[0] - 16) // block):
            start = pl.multiple_of(2 * g * block + which * block, 16)
            ref[g * block : (g + 1) * block, :] = held[pl.ds(start, block), :]
        ref[keep_ref.shape[0] - 16 :, :] = depth


def spread_kernel(axis, block, count, *refs):
    in_refs, out_refs, held = refs[:count], refs[count:-1], refs[-1]
    held[...] = tree_sum([ref[...].astype(F32) for ref in in_refs]).astype(BF16)
    rows = out_refs[0].shape[0] - 16
    size = len(out_refs)
    for step, out in enumerate(out_refs):
        part = lax.bitwise_xor(lax.axis_index(axis), step)
        for g in range(rows // block):
            start = pl.multiple_of(g * size * block + part * block, 16)
            out[g * block : (g + 1) * block, :] = held[pl.ds(start, block), :]
        out[rows:, :] = held[held.shape[0] - 16 :, :]


def total_kernel(count, *refs):
    in_refs, (mix_ref, depth_ref) = refs[:count], refs[count:]
    total = tree_sum([ref[...].astype(F32) for ref in in_refs])
    rows = mix_ref.shape[0]
    mix_ref[...] = total[:rows]
    depth_ref[...] = total[rows : rows + depth_ref.shape[0]]


def in_gradient_kernel(tiles, own_ref, *refs):
    grad_refs, (keep, send, whole, held) = refs[:tiles], refs[tiles:]
    cells = grad_refs[0].shape[0]
    for step, ref in enumerate(grad_refs):
        start = pl.multiple_of(lax.bitwise_xor(lax.axis_index("tile"), step) * cells, 16)
        whole[pl.ds(start, cells), :] = ref[...]
    term = lax.dot_general(own_ref[...], whole[...], (((0,), (0,)), ((), ())), preferred_element_type=F32)
    half = keep.shape[0]
    rep = lax.axis_index("rep")
    held[...] = term[: 2 * half].astype(BF16)
    keep[...] = held[pl.ds(pl.multiple_of(rep * half, 16), half), :]
    send[...] = held[pl.ds(pl.multiple_of((1 - rep) * half, 16), half), :]


def group_gradient_kernel(tiles, rows_ref, weight_ref, patch_ref, group_keep, group_send, group_term):
    slots, lanes = patch_ref.shape[0], 6 * LANES
    channels = LANES // 2
    rows = rows_ref[...]
    cells = rows.shape[0] // tiles
    rep = lax.axis_index("rep")
    feature_grad = lax.dot_general(rows, weight_ref[...], (((1,), (1,)), ((), ())), preferred_element_type=F32)
    feature_grad = feature_grad.astype(BF16).astype(F32)
    blank = slots * channels % LANES
    if blank:
        feature_grad = jnp.concatenate(
            [feature_grad, jnp.zeros((feature_grad.shape[0], LANES - blank), F32)], axis=1
        )
    part = cells // 2

    def halves(value):
        return [
            jnp.concatenate(
                [value[cells * j + part * h : cells * j + part * (h + 1)] for j in range(tiles)], axis=0
            )
            for h in range(2)
        ]

    for slot in range(0, slots, 2):
        tile = feature_grad[:, slot * channels : slot * channels + LANES]
        both = interleave(*halves(tile))
        for k in range(slot, min(slot + 2, slots)):
            inner = (both[k - slot] * patch_ref[k, :, lanes:].astype(F32)).astype(BF16)
            term = lax.dot_general(inner, patch_ref[k, :, :lanes], (((0,), (0,)), ((), ())), preferred_element_type=F32)
            quarter = lanes // 3
            use = 3 * channels
            low = jnp.concatenate([term[:channels, quarter * a : quarter * a + use] for a in range(3)], axis=1)
            high = jnp.concatenate(
                [term[channels:, quarter * a + channels : quarter * (a + 1)] for a in range(3)], axis=1
            )
            group_term[channels * k : channels * (k + 1), :] = (low + high).astype(BF16)
    half = group_keep.shape[0]
    group_keep[...] = group_term[pl.ds(pl.multiple_of(rep * half, 16), half), :]
    group_send[...] = group_term[pl.ds(pl.multiple_of((1 - rep) * half, 16), half), :]


def call(kernel, outs, operands, scratch=(), flops=1 << 24, specs=None):
    shapes = [jax.ShapeDtypeStruct(s, d) for s, d in outs]
    moved = sum(o.size * o.dtype.itemsize for o in list(operands) + shapes)
    held = sum(math.prod(r.shape) * 4 for r in scratch if len(r.shape) > 1)
    return pl.pallas_call(
        kernel,
        out_shape=shapes,
        in_specs=specs or [SMEM if jnp.issubdtype(o.dtype, jnp.integer) else VMEM for o in operands],
        out_specs=[VMEM] * len(shapes),
        scratch_shapes=list(scratch),
        cost_estimate=pl.CostEstimate(flops=flops, bytes_accessed=moved, transcendentals=0),
        compiler_params=pltpu.CompilerParams(vmem_limit_bytes=(8 << 20) + 2 * (moved + held)),
    )(*operands)


def program(
    forcing,
    member_kernel_weight,
    member_counts,
    mixing_input_weight,
    depth_weight,
    mix_weight,
    cotangent,
):
    channels = member_kernel_weight.shape[2]
    slots = forcing.shape[1]
    height = forcing.shape[2]
    width = forcing.shape[3] // channels
    hidden = mixing_input_weight.shape[1]
    tiles, cols, reps = (lax.axis_size(a) for a in ("tile", "col", "rep"))
    pairs = width // 2 + 2
    cells = ROWS * width
    assert height == ROWS * tiles and 2 * channels == LANES and pairs % 2 == 0
    lane_tiles = -(-slots // 2)
    rows = hidden // (tiles * cols * reps)

    sides, ends = (1 if count == 2 else 2 for count in (cols, tiles))
    field, kernel, weight, upstream, *edges = call(
        functools.partial(prepare_kernel, (sides, ends)),
        [
            (forcing.shape[1:], BF16),
            ((slots, LANES, 6 * LANES), BF16),
            ((lane_tiles * LANES, hidden), BF16),
            (cotangent.shape[1:], BF16),
        ]
        + [((slots, height, 4 * channels), BF16)] * sides
        + [((ROWS, hidden), BF16)] * sides
        + [((width, hidden), BF16)] * ends,
        [
            pltpu.with_memory_space_constraint(x, pltpu.HBM)
            for x in (forcing[0], jnp.swapaxes(member_kernel_weight, 1, 2), mixing_input_weight, cotangent[0])
        ],
        [pltpu.VMEM((slots, channels, 9 * channels), BF16), pltpu.SemaphoreType.DMA((4,))],
        specs=[HBM] * 4,
    )
    halos = with_neighbours(edges[:sides], "col")
    top, bottom = in_order(with_neighbours(edges[2 * sides :], "tile"), "tile")
    sent = call(
        functools.partial(features_kernel, tiles),
        [((3 * ROWS * pairs, hidden), BF16)] * tiles,
        [member_counts, field, kernel, weight, *halos],
        [pltpu.VMEM((tiles, 3 * ROWS * pairs, lane_tiles * LANES), BF16)],
        flops=1 << 28,
    )
    terms = [swap(sent[step], "tile", step) if step else sent[0] for step in range(tiles)]

    even = lax.axis_index("col") % 2 == 0
    columns = []
    for i, edge in enumerate(edges[sides : 2 * sides]):
        last = even if i == 0 else ~even
        corners = [jnp.where(last, row[-1:], row[:1]) for row in (top, bottom)]
        columns.append(jnp.concatenate([corners[0], edge, corners[1]], axis=0))
    left, right = in_order(with_neighbours(columns, "col"), "col")
    flat_upstream = upstream.reshape(cells, hidden)
    (hidden_grad,) = call(
        upstream_kernel,
        [((width + 2, 16, hidden), F32)],
        [flat_upstream, left, right, top, bottom, mix_weight],
        [pltpu.VMEM((2 * LANES, hidden), BF16)],
        flops=1 << 28,
    )
    patch, own_features = call(
        backward_inputs_kernel,
        [
            ((slots, cells // 2 * tiles, 7 * LANES), BF16),
            ((cells * tiles, lane_tiles * LANES), BF16),
        ],
        [member_counts, field, kernel, *halos],
        flops=1 << 28,
    )

    act_grad, hidden_act, act, inner = call(
        functools.partial(middle_kernel, tiles),
        [
            ((width, ROWS, hidden), BF16),
            ((width + 2, ROWS, hidden), F32),
            ((hidden // LANES, width + 4, 16, LANES), F32),
            ((hidden // LANES, width + 2, 16, LANES), F32),
        ],
        [hidden_grad, depth_weight, *terms],
    )
    act_grad = act_grad.reshape(cells, hidden)
    grads = [swap(act_grad, "tile", step) if step else act_grad for step in range(tiles)]

    part = ((tiles * cols * rows + 16, hidden), BF16)
    adjusted, keep, send = call(
        finish_kernel,
        [((cells, hidden), BF16), part, part],
        [hidden_act, flat_upstream, mix_weight, act, inner],
        [pltpu.VMEM((hidden, hidden), BF16)],
    )
    arrived = [keep, swap(send, "rep", 1)]
    blocks = tiles * cols
    for axis in ("col", "tile"):
        size = lax.axis_size(axis)
        blocks //= size
        dealt = call(
            functools.partial(spread_kernel, axis, rows, len(arrived)),
            [((blocks * rows + 16, hidden), BF16)] * size,
            arrived,
            [pltpu.VMEM(arrived[0].shape, BF16)],
        )
        arrived = [swap(dealt[step], axis, step) if step else dealt[0] for step in range(size)]
    mix_grad, depth_grad = call(
        functools.partial(total_kernel, tiles), [((rows, hidden), F32), ((9, hidden), F32)], arrived
    )

    half = slots * channels // 2
    in_keep, in_send, whole = call(
        functools.partial(in_gradient_kernel, tiles),
        [((half, hidden), BF16), ((half, hidden), BF16), ((cells * tiles, hidden), BF16)],
        [own_features, *grads],
        [pltpu.VMEM((2 * half, hidden), BF16)],
    )
    group_keep, group_send = call(
        functools.partial(group_gradient_kernel, tiles),
        [((half, 9 * channels), BF16), ((half, 9 * channels), BF16)],
        [whole, mixing_input_weight, patch],
        [pltpu.VMEM((2 * half, 9 * channels), BF16)],
        flops=1 << 28,
    )
    in_grad = full_sum(in_keep, in_send).astype(F32)
    group_grad = full_sum(group_keep, group_send).reshape(slots, channels, -1)
    group_grad = jnp.swapaxes(group_grad, 1, 2).astype(F32)
    return (adjusted.reshape(cotangent.shape), mix_grad, depth_grad, in_grad, group_grad)


def solution(mesh):
    in_specs = (
        P(("groups", "rep"), "tile", None, "col"),
        P("tile", None, None),
        P("tile"),
        P("tile", None),
        P(),
        P(),
        P(("groups", "rep"), "tile", "col", None),
    )
    out_specs = (
        P(("groups", "rep"), "tile", "col", None),
        P(("groups", "tile", "col", "rep"), None),
        P("groups", None),
        P(("groups", "tile"), None),
        P(("groups", "tile"), None, None),
    )
    return jax.shard_map(program, mesh=mesh, in_specs=in_specs, out_specs=out_specs, check_vma=False)
```

profile of v0, /device:TPU:0, one launch (start us, length us, event | category | flops | bytes accessed | tf_op | source)
XLA Modules:
  0.0 74.2 jit_solution(8602049592587145298)
XLA Ops:
  0.7 1.4 %shard_map.110 = (bf16[5,32,1024]{2,1,0:T(8,128)(2,1)S(1)}, bf16[5,128,768]{2,1,0:T(8,128)(2,1)S(1)}, bf16[384,512]{1,0:T(8,128)(2,1)S(1)}, bf16[8,16,512]{2,1,0...) custom-call(bf16[5,32,1024]{2,1,0:T(8,128)(2,1)} %bitcast.18, ...), custom_call_target="tpu_custom_call" | custom-call | flops 16777216 | bytes 3112960 | tf_op jit(solution)/shard_map/pallas_call | solution.py:446
  2.8 5.9 %collective-permute-start.1 = (bf16[16,512]{1,0:T(8,128)(2,1)S(1)}, bf16[16,512]{1,0:T(8,128)(2,1)S(1)}, u32[]{:S(2)}, u32[]{:S(2)}) collective-permute-start(bf16[16,512]{1,0:T(8,128)(2,1)S(1)} %get-tuple-element.41), channel_id=1, source_target_pairs={{0,4},{8,12},{4,0},{12,8},{1,5},{9,13},{5,1},{13,9},{2,6},{10,14},... | collective-permute-start | bytes 49160 | tf_op jit(solution)/shard_map/ppermute | solution.py:30
  8.7 1.5 %collective-permute-start.3 = (bf16[5,32,256]{2,1,0:T(8,128)(2,1)S(1)}, bf16[5,32,256]{2,1,0:T(8,128)(2,1)S(1)}, u32[]{:S(2)}, u32[]{:S(2)}) collective-permute-start(bf16[5,32,256]{2,1,0:T(8,128)(2,1)S(1)} %get-tuple-element.46), channel_id=1, source_target_pairs={{0,2},{2,0},{1,3},{3,1},{4,6},{6,4},{5,7},{7,5},{8,10},{10,8},{9,1... | collective-permute-start | bytes 245768 | tf_op jit(solution)/shard_map/ppermute | solution.py:30
  10.9 1.1 %collective-permute-start.2 = (bf16[10,512]{1,0:T(8,128)(2,1)S(1)}, bf16[10,512]{1,0:T(8,128)(2,1)S(1)}, u32[]{:S(2)}, u32[]{:S(2)}) collective-permute-start(bf16[10,512]{1,0:T(8,128)(2,1)S(1)} %pad_maximum_fusion.1), channel_id=1, source_target_pairs={{0,2},{2,0},{1,3},{3,1},{4,6},{6,4},{5,7},{7,5},{8,10},{10,8},{9,1... | collective-permute-start | bytes 30728 | tf_op jit(solution)/shard_map/ppermute | solution.py:30
  12.0 1.3 %collective-permute-done.3.refs_0_ = bf16[5,32,256]{2,1,0:T(8,128)(2,1)S(1)} collective-permute-done((bf16[5,32,256]{2,1,0:T(8,128)(2,1)S(1)}, bf16[5,32,256]{2,1,0:T(8,128)(2,1)S(1)}, u32[]{:S(2)}, u32[]{:S(2)}) %collective-permute-start.3) | collective-permute-done | bytes 81952 | tf_op jit(solution)/shard_map/ppermute | solution.py:30
  13.3 1.8 %shard_map.112 = (bf16[240,512]{1,0:T(8,128)(2,1)S(1)}, bf16[240,512]{1,0:T(8,128)(2,1)S(1)}, bf16[240,512]{1,0:T(8,128)(2,1)S(1)}, bf16[240,512]{1,0:T(8,128)(2,1)S(1)}) custom-call(s32[1]{0:T(128)S(6)} %copy.12.count_ref, bf16[5,32,1024]{2,1,0:T(8,128)(2,1)S(1)} %get-tuple-element.43.field_ref, bf16[5,128,768]{2,1,0:T(8,128)(2,1)S(1)} %get-tuple-element.44.kernel_ref, ...), custom_call_target="tpu_custom_call" | custom-call | flops 268435456 | bytes 2768900 | tf_op jit(solution)/shard_map/pallas_call | solution.py:446
  15.1 0.8 %collective-permute-start.4 = (bf16[240,512]{1,0:T(8,128)(2,1)S(1)}, bf16[240,512]{1,0:T(8,128)(2,1)S(1)}, u32[]{:S(2)}, u32[]{:S(2)}) collective-permute-start(bf16[240,512]{1,0:T(8,128)(2,1)S(1)} %get-tuple-element.48), channel_id=1, source_target_pairs={{0,4},{4,0},{8,12},{12,8},{1,5},{5,1},{9,13},{13,9},{2,6},{6,2},{1... | collective-permute-start | bytes 737288 | tf_op jit(solution)/shard_map/ppermute | solution.py:22
  15.9 1.2 %collective-permute-start.5 = (bf16[240,512]{1,0:T(8,128)(2,1)S(1)}, bf16[240,512]{1,0:T(8,128)(2,1)S(1)}, u32[]{:S(2)}, u32[]{:S(2)}) collective-permute-start(bf16[240,512]{1,0:T(8,128)(2,1)S(1)} %get-tuple-element.49), channel_id=1, source_target_pairs={{0,8},{4,12},{8,0},{12,4},{1,9},{5,13},{9,1},{13,5},{2,10},{6,14},... | collective-permute-start | bytes 737288 | tf_op jit(solution)/shard_map/ppermute | solution.py:22
  17.1 2.5 %collective-permute-start.6 = (bf16[240,512]{1,0:T(8,128)(2,1)S(1)}, bf16[240,512]{1,0:T(8,128)(2,1)S(1)}, u32[]{:S(2)}, u32[]{:S(2)}) collective-permute-start(bf16[240,512]{1,0:T(8,128)(2,1)S(1)} %get-tuple-element.50), channel_id=1, source_target_pairs={{0,12},{4,8},{8,4},{12,0},{1,13},{5,9},{9,5},{13,1},{2,14},{6,10},... | collective-permute-start | bytes 737288 | tf_op jit(solution)/shard_map/ppermute | solution.py:22
  20.1 5.4 %collective-permute-done.4.refs_1_ = bf16[240,512]{1,0:T(8,128)(2,1)S(1)} collective-permute-done((bf16[240,512]{1,0:T(8,128)(2,1)S(1)}, bf16[240,512]{1,0:T(8,128)(2,1)S(1)}, u32[]{:S(2)}, u32[]{:S(2)}) %collective-permute-start.4) | collective-permute-done | bytes 245792 | tf_op jit(solution)/shard_map/ppermute | solution.py:22
  25.5 9.7 %collective-permute-done.5.refs_2_ = bf16[240,512]{1,0:T(8,128)(2,1)S(1)} collective-permute-done((bf16[240,512]{1,0:T(8,128)(2,1)S(1)}, bf16[240,512]{1,0:T(8,128)(2,1)S(1)}, u32[]{:S(2)}, u32[]{:S(2)}) %collective-permute-start.5) | collective-permute-done | bytes 245792 | tf_op jit(solution)/shard_map/ppermute | solution.py:22
  35.2 1.4 %shard_map.113 = (bf16[16,8,512]{2,1,0:T(8,128)(2,1)S(1)}, f32[18,8,512]{2,1,0:T(8,128)S(1)}, f32[4,20,16,128]{3,2,1,0:T(8,128)S(1)}, f32[4,18,16,128]{3,2,1,0:T(8,128)S(1)}) custom-call(f32[18,16,512]{2,1,0:T(8,128)S(1)} %shard_map.111.grad_ref, f32[9,512]{1,0:T(8,128)S(1)} %copy-done.6, bf16[240,512]{1,0:T(8,128)(2,1)S(1)} %get-tuple-element.47.refs_0_, ...), custom_call_target="tpu_custom_call" | custom-call | flops 16777216 | bytes 3262464 | tf_op jit(solution)/shard_map/pallas_call | solution.py:446
  36.6 3.9 %collective-permute-start.12 = (bf16[128,512]{1,0:T(8,128)(2,1)S(1)}, bf16[128,512]{1,0:T(8,128)(2,1)S(1)}, u32[]{:S(2)}, u32[]{:S(2)}) collective-permute-start(bf16[128,512]{1,0:T(8,128)(2,1)S(1)} %bitcast.12), channel_id=1, source_target_pairs={{0,4},{4,0},{8,12},{12,8},{1,5},{5,1},{9,13},{13,9},{2,6},{6,2},{1... | collective-permute-start | bytes 393224 | tf_op jit(solution)/shard_map/ppermute | solution.py:22
  40.5 2.4 %collective-permute-start.14 = (bf16[128,512]{1,0:T(8,128)(2,1)S(1)}, bf16[128,512]{1,0:T(8,128)(2,1)S(1)}, u32[]{:S(2)}, u32[]{:S(2)}) collective-permute-start(bf16[128,512]{1,0:T(8,128)(2,1)S(1)} %bitcast.14), channel_id=1, source_target_pairs={{0,12},{4,8},{8,4},{12,0},{1,13},{5,9},{9,5},{13,1},{2,14},{6,10},... | collective-permute-start | bytes 393224 | tf_op jit(solution)/shard_map/ppermute | solution.py:22
  42.9 1.6 %shard_map.114 = (bf16[128,512]{1,0:T(8,128)(2,1)}, bf16[272,512]{1,0:T(8,128)(2,1)S(1)}, bf16[272,512]{1,0:T(8,128)(2,1)}) custom-call(f32[18,8,512]{2,1,0:T(8,128)S(1)} %get-tuple-element.51.hidden_ref, bf16[128,512]{1,0:T(8,128)(2,1)S(1)} %bitcast.11, bf16[512,512]{1,0:T(8,128)(2,1)S(1)} %copy-done, f32[4,20,16,128]{3,2,1,0:T(8,128)S(1)} %get-tuple-element.52.act, ...), custom_call_target="tpu_custom_call" | custom-call | flops 16777216 | bytes 2883584 | tf_op jit(solution)/shard_map/pallas_call | solution.py:446
  44.6 0.7 copy-done.4
  45.3 1.2 %shard_map.118 = (bf16[5,256,896]{2,1,0:T(8,128)(2,1)S(1)}, bf16[512,384]{1,0:T(8,128)(2,1)S(1)}) custom-call(s32[1]{0:T(128)S(6)} %copy.12.count_ref, bf16[5,32,1024]{2,1,0:T(8,128)(2,1)S(1)} %copy-done.3, bf16[5,128,768]{2,1,0:T(8,128)(2,1)S(1)} %get-tuple-element.44.kernel_ref, bf16[5,32,256]{2,1,0:T(8,128)(2,1)S(1)} %collective-permute-done.3.refs_0_), custom_call_target="tpu_custom_call" | custom-call | flops 268435456 | bytes 4079620 | tf_op jit(solution)/shard_map/pallas_call | solution.py:446
  46.5 4.3 %collective-permute-done.13.refs_2_ = bf16[128,512]{1,0:T(8,128)(2,1)S(1)} collective-permute-done((bf16[128,512]{1,0:T(8,128)(2,1)S(1)}, bf16[128,512]{1,0:T(8,128)(2,1)S(1)}, u32[]{:S(2)}, u32[]{:S(2)}) %collective-permute-start.13) | collective-permute-done | bytes 131104 | tf_op jit(solution)/shard_map/ppermute | solution.py:22
  51.4 1.0 %copy-done.1 = bf16[320,512]{1,0:T(8,128)(2,1)S(1)} copy-done((bf16[320,512]{1,0:T(8,128)(2,1)S(1)}, bf16[320,512]{1,0:T(8,128)(2,1)}, u32[]{:S(2)}) %copy-start.1) | copy-done | bytes 327704
  52.3 1.4 %shard_map.120 = (bf16[160,576]{1,0:T(8,128)(2,1)S(1)}, bf16[160,576]{1,0:T(8,128)(2,1)S(1)}) custom-call(bf16[512,512]{1,0:T(8,128)(2,1)S(1)} %get-tuple-element.69.rows_ref, bf16[320,512]{1,0:T(8,128)(2,1)S(1)} %copy-done.1, bf16[5,256,896]{2,1,0:T(8,128)(2,1)S(1)} %get-tuple-element.70.patch_ref), custom_call_target="tpu_custom_call" | custom-call | flops 268435456 | bytes 3514368 | tf_op jit(solution)/shard_map/pallas_call | solution.py:446
  54.3 1.1 %shard_map.115 = (bf16[144,512]{1,0:T(8,128)(2,1)S(1)}, bf16[144,512]{1,0:T(8,128)(2,1)S(1)}) custom-call(bf16[272,512]{1,0:T(8,128)(2,1)S(1)} %copy-done.5, bf16[272,512]{1,0:T(8,128)(2,1)} %collective-permute-done.7.refs_1_), custom_call_target="tpu_custom_call" | custom-call | flops 16777216 | bytes 851968 | tf_op jit(solution)/shard_map/pallas_call | solution.py:446
  55.4 1.1 %collective-permute-start.8 = (bf16[144,512]{1,0:T(8,128)(2,1)S(1)}, bf16[144,512]{1,0:T(8,128)(2,1)S(1)}, u32[]{:S(2)}, u32[]{:S(2)}) collective-permute-start(bf16[144,512]{1,0:T(8,128)(2,1)S(1)} %get-tuple-element.58), channel_id=1, source_target_pairs={{0,2},{2,0},{1,3},{3,1},{4,6},{6,4},{5,7},{7,5},{8,10},{10,8},{9,1... | collective-permute-start | bytes 442376 | tf_op jit(solution)/shard_map/ppermute | solution.py:22
  56.5 1.0 %add_convert_fusion.3 = bf16[160,512]{1,0:T(8,128)(2,1)S(1)} fusion(bf16[160,512]{1,0:T(8,128)(2,1)} %collective-permute-done.15, bf16[160,512]{1,0:T(8,128)(2,1)S(1)} %get-tuple-element.67), kind=kLoop, calls=%fused_computation.6 | loop fusion | flops 327680 | bytes 491520 | tf_op jit(solution)/shard_map/convert_element_type | solution.py:48
  57.5 1.0 %collective-permute-start.16 = (bf16[160,512]{1,0:T(8,128)(2,1)S(1)}, bf16[160,512]{1,0:T(8,128)(2,1)S(1)}, u32[]{:S(2)}, u32[]{:S(2)}) collective-permute-start(bf16[160,512]{1,0:T(8,128)(2,1)S(1)} %add_convert_fusion.3), channel_id=1, source_target_pairs={{0,2},{2,0},{1,3},{3,1},{4,6},{6,4},{5,7},{7,5},{8,10},{10,8},{9,1... | collective-permute-start | bytes 491528 | tf_op jit(solution)/shard_map/ppermute | solution.py:22
  58.6 1.1 %collective-permute-start.19 = (bf16[160,576]{1,0:T(8,128)(2,1)S(1)}, bf16[160,576]{1,0:T(8,128)(2,1)S(1)}, u32[]{:S(2)}, u32[]{:S(2)}) collective-permute-start(bf16[160,576]{1,0:T(8,128)(2,1)S(1)} %add_convert_fusion.1), channel_id=1, source_target_pairs={{0,2},{2,0},{1,3},{3,1},{4,6},{6,4},{5,7},{7,5},{8,10},{10,8},{9,1... | collective-permute-start | bytes 552968 | tf_op jit(solution)/shard_map/ppermute | solution.py:22
  59.7 2.5 %collective-permute-done.8.refs_1_ = bf16[144,512]{1,0:T(8,128)(2,1)S(1)} collective-permute-done((bf16[144,512]{1,0:T(8,128)(2,1)S(1)}, bf16[144,512]{1,0:T(8,128)(2,1)S(1)}, u32[]{:S(2)}, u32[]{:S(2)}) %collective-permute-start.8) | collective-permute-done | bytes 147488 | tf_op jit(solution)/shard_map/ppermute | solution.py:22
  62.3 2.7 %collective-permute-start.9 = (bf16[48,512]{1,0:T(8,128)(2,1)S(1)}, bf16[48,512]{1,0:T(8,128)(2,1)S(1)}, u32[]{:S(2)}, u32[]{:S(2)}) collective-permute-start(bf16[48,512]{1,0:T(8,128)(2,1)S(1)} %get-tuple-element.60), channel_id=1, source_target_pairs={{0,4},{4,0},{8,12},{12,8},{1,5},{5,1},{9,13},{13,9},{2,6},{6,2},{1... | collective-permute-start | bytes 147464 | tf_op jit(solution)/shard_map/ppermute | solution.py:22
  64.9 2.4 %collective-permute-start.11 = (bf16[48,512]{1,0:T(8,128)(2,1)S(1)}, bf16[48,512]{1,0:T(8,128)(2,1)S(1)}, u32[]{:S(2)}, u32[]{:S(2)}) collective-permute-start(bf16[48,512]{1,0:T(8,128)(2,1)S(1)} %get-tuple-element.62), channel_id=1, source_target_pairs={{0,12},{4,8},{8,4},{12,0},{1,13},{5,9},{9,5},{13,1},{2,14},{6,10},... | collective-permute-start | bytes 147464 | tf_op jit(solution)/shard_map/ppermute | solution.py:22
  68.0 1.9 %collective-permute-done.10.refs_2_ = bf16[48,512]{1,0:T(8,128)(2,1)S(1)} collective-permute-done((bf16[48,512]{1,0:T(8,128)(2,1)S(1)}, bf16[48,512]{1,0:T(8,128)(2,1)S(1)}, u32[]{:S(2)}, u32[]{:S(2)}) %collective-permute-start.10) | collective-permute-done | bytes 49184 | tf_op jit(solution)/shard_map/ppermute | solution.py:22
  70.0 1.0 %collective-permute-done.11.refs_3_ = bf16[48,512]{1,0:T(8,128)(2,1)S(1)} collective-permute-done((bf16[48,512]{1,0:T(8,128)(2,1)S(1)}, bf16[48,512]{1,0:T(8,128)(2,1)S(1)}, u32[]{:S(2)}, u32[]{:S(2)}) %collective-permute-start.11) | collective-permute-done | bytes 49184 | tf_op jit(solution)/shard_map/ppermute | solution.py:22
  71.8 0.9 %maximum_convert_fusion = f32[320,512]{1,0:T(8,128)} fusion(bf16[160,512]{1,0:T(8,128)(2,1)S(1)} %get-tuple-element.76, bf16[160,512]{1,0:T(8,128)(2,1)S(1)} %get-tuple-element.75), kind=kLoop, calls=%fused_computation.4 | loop fusion | flops 655360 | bytes 983040 | tf_op jit(solution)/shard_map/convert_element_type | solution.py:583
  73.3 0.9 %convert_bitcast_fusion = f32[5,576,64]{1,2,0:T(8,128)} fusion(bf16[5,64,576]{2,1,0:T(8,128)(2,1)S(1)} %bitcast.16), kind=kLoop, calls=%fused_computation | loop fusion | flops 184320 | bytes 1105920 | tf_op jit(solution)/shard_map/convert_element_type | solution.py:585
  (48 shorter events, 4.5 us)
Async XLA Ops:
  0.6 19.0 %copy-start = (bf16[512,512]{1,0:T(8,128)(2,1)S(1)}, bf16[512,512]{1,0:T(8,128)(2,1)}, u32[]{:S(2)}) copy-start(bf16[512,512]{1,0:T(8,128)(2,1)} %mix_ref.3) | copy-start | bytes 1572868
  0.6 34.5 %copy-start.6 = (f32[9,512]{1,0:T(8,128)S(1)}, f32[9,512]{1,0:T(8,128)}, u32[]{:S(2)}) copy-start(f32[9,512]{1,0:T(8,128)} %depth_ref.1) | copy-start | bytes 55300
  2.1 34.5 %copy-start.2 = (bf16[5,32,1024]{2,1,0:T(8,128)(2,1)}, bf16[5,32,1024]{2,1,0:T(8,128)(2,1)S(1)}, u32[]{:S(2)}) copy-start(bf16[5,32,1024]{2,1,0:T(8,128)(2,1)S(1)} %get-tuple-element.43.field_ref) | copy-start | bytes 983044
  2.1 8.8 %collective-permute-start = (bf16[16,512]{1,0:T(8,128)(2,1)S(1)}, bf16[16,512]{1,0:T(8,128)(2,1)S(1)}, u32[]{:S(2)}, u32[]{:S(2)}) collective-permute-start(bf16[16,512]{1,0:T(8,128)(2,1)S(1)} %get-tuple-element.40), channel_id=1, source_target_pairs={{4,8},{8,4},{5,9},{9,5},{6,10},{10,6},{7,11},{11,7},{20,24},{24,20... | collective-permute-start | bytes 49160 | tf_op jit(solution)/shard_map/ppermute | solution.py:30
  2.8 8.1 %collective-permute-start.1 = (bf16[16,512]{1,0:T(8,128)(2,1)S(1)}, bf16[16,512]{1,0:T(8,128)(2,1)S(1)}, u32[]{:S(2)}, u32[]{:S(2)}) collective-permute-start(bf16[16,512]{1,0:T(8,128)(2,1)S(1)} %get-tuple-element.41), channel_id=1, source_target_pairs={{0,4},{8,12},{4,0},{12,8},{1,5},{9,13},{5,1},{13,9},{2,6},{10,14},... | collective-permute-start | bytes 49160 | tf_op jit(solution)/shard_map/ppermute | solution.py:30
  8.7 4.6 %collective-permute-start.3 = (bf16[5,32,256]{2,1,0:T(8,128)(2,1)S(1)}, bf16[5,32,256]{2,1,0:T(8,128)(2,1)S(1)}, u32[]{:S(2)}, u32[]{:S(2)}) collective-permute-start(bf16[5,32,256]{2,1,0:T(8,128)(2,1)S(1)} %get-tuple-element.46), channel_id=1, source_target_pairs={{0,2},{2,0},{1,3},{3,1},{4,6},{6,4},{5,7},{7,5},{8,10},{10,8},{9,1... | collective-permute-start | bytes 245768 | tf_op jit(solution)/shard_map/ppermute | solution.py:30
  10.9 8.6 %collective-permute-start.2 = (bf16[10,512]{1,0:T(8,128)(2,1)S(1)}, bf16[10,512]{1,0:T(8,128)(2,1)S(1)}, u32[]{:S(2)}, u32[]{:S(2)}) collective-permute-start(bf16[10,512]{1,0:T(8,128)(2,1)S(1)} %pad_maximum_fusion.1), channel_id=1, source_target_pairs={{0,2},{2,0},{1,3},{3,1},{4,6},{6,4},{5,7},{7,5},{8,10},{10,8},{9,1... | collective-permute-start | bytes 30728 | tf_op jit(solution)/shard_map/ppermute | solution.py:30
  15.1 10.3 %collective-permute-start.4 = (bf16[240,512]{1,0:T(8,128)(2,1)S(1)}, bf16[240,512]{1,0:T(8,128)(2,1)S(1)}, u32[]{:S(2)}, u32[]{:S(2)}) collective-permute-start(bf16[240,512]{1,0:T(8,128)(2,1)S(1)} %get-tuple-element.48), channel_id=1, source_target_pairs={{0,4},{4,0},{8,12},{12,8},{1,5},{5,1},{9,13},{13,9},{2,6},{6,2},{1... | collective-permute-start | bytes 737288 | tf_op jit(solution)/shard_map/ppermute | solution.py:22
  15.9 19.3 %collective-permute-start.5 = (bf16[240,512]{1,0:T(8,128)(2,1)S(1)}, bf16[240,512]{1,0:T(8,128)(2,1)S(1)}, u32[]{:S(2)}, u32[]{:S(2)}) collective-permute-start(bf16[240,512]{1,0:T(8,128)(2,1)S(1)} %get-tuple-element.49), channel_id=1, source_target_pairs={{0,8},{4,12},{8,0},{12,4},{1,9},{5,13},{9,1},{13,5},{2,10},{6,14},... | collective-permute-start | bytes 737288 | tf_op jit(solution)/shard_map/ppermute | solution.py:22
  17.1 18.1 %collective-permute-start.6 = (bf16[240,512]{1,0:T(8,128)(2,1)S(1)}, bf16[240,512]{1,0:T(8,128)(2,1)S(1)}, u32[]{:S(2)}, u32[]{:S(2)}) collective-permute-start(bf16[240,512]{1,0:T(8,128)(2,1)S(1)} %get-tuple-element.50), channel_id=1, source_target_pairs={{0,12},{4,8},{8,4},{12,0},{1,13},{5,9},{9,5},{13,1},{2,14},{6,10},... | collective-permute-start | bytes 737288 | tf_op jit(solution)/shard_map/ppermute | solution.py:22
  36.6 8.7 %copy-start.3 = (bf16[5,32,1024]{2,1,0:T(8,128)(2,1)S(1)}, bf16[5,32,1024]{2,1,0:T(8,128)(2,1)}, u32[]{:S(2)}) copy-start(bf16[5,32,1024]{2,1,0:T(8,128)(2,1)} %copy-done.2) | copy-start | bytes 983044
  36.6 9.9 %collective-permute-start.12 = (bf16[128,512]{1,0:T(8,128)(2,1)S(1)}, bf16[128,512]{1,0:T(8,128)(2,1)S(1)}, u32[]{:S(2)}, u32[]{:S(2)}) collective-permute-start(bf16[128,512]{1,0:T(8,128)(2,1)S(1)} %bitcast.12), channel_id=1, source_target_pairs={{0,4},{4,0},{8,12},{12,8},{1,5},{5,1},{9,13},{13,9},{2,6},{6,2},{1... | collective-permute-start | bytes 393224 | tf_op jit(solution)/shard_map/ppermute | solution.py:22
  40.5 10.3 %collective-permute-start.13 = (bf16[128,512]{1,0:T(8,128)(2,1)S(1)}, bf16[128,512]{1,0:T(8,128)(2,1)S(1)}, u32[]{:S(2)}, u32[]{:S(2)}) collective-permute-start(bf16[128,512]{1,0:T(8,128)(2,1)S(1)} %bitcast.13), channel_id=1, source_target_pairs={{0,8},{4,12},{8,0},{12,4},{1,9},{5,13},{9,1},{13,5},{2,10},{6,14},... | collective-permute-start | bytes 393224 | tf_op jit(solution)/shard_map/ppermute | solution.py:22
  40.5 10.3 %collective-permute-start.14 = (bf16[128,512]{1,0:T(8,128)(2,1)S(1)}, bf16[128,512]{1,0:T(8,128)(2,1)S(1)}, u32[]{:S(2)}, u32[]{:S(2)}) collective-permute-start(bf16[128,512]{1,0:T(8,128)(2,1)S(1)} %bitcast.14), channel_id=1, source_target_pairs={{0,12},{4,8},{8,4},{12,0},{1,13},{5,9},{9,5},{13,1},{2,14},{6,10},... | collective-permute-start | bytes 393224 | tf_op jit(solution)/shard_map/ppermute | solution.py:22
  44.6 0.7 copy-start.4
  45.3 9.0 %collective-permute-start.7 = (bf16[272,512]{1,0:T(8,128)(2,1)}, bf16[272,512]{1,0:T(8,128)(2,1)}, u32[]{:S(2)}, u32[]{:S(2)}) collective-permute-start(bf16[272,512]{1,0:T(8,128)(2,1)} %get-tuple-element.56), channel_id=1, source_target_pairs={{0,1},{1,0},{2,3},{3,2},{4,5},{5,4},{6,7},{7,6},{8,9},{9,8},{10,11... | collective-permute-start | bytes 835592 | tf_op jit(solution)/shard_map/ppermute | solution.py:22
  46.5 7.8 %copy-start.5 = (bf16[272,512]{1,0:T(8,128)(2,1)S(1)}, bf16[272,512]{1,0:T(8,128)(2,1)}, u32[]{:S(2)}) copy-start(bf16[272,512]{1,0:T(8,128)(2,1)} %copy-done.4) | copy-start | bytes 835588
  51.3 5.2 %collective-permute-start.15 = (bf16[160,512]{1,0:T(8,128)(2,1)S(1)}, bf16[160,512]{1,0:T(8,128)(2,1)}, u32[]{:S(2)}, u32[]{:S(2)}) collective-permute-start(bf16[160,512]{1,0:T(8,128)(2,1)S(1)} %get-tuple-element.68), channel_id=1, source_target_pairs={{0,1},{1,0},{2,3},{3,2},{4,5},{5,4},{6,7},{7,6},{8,9},{9,8},{10,11... | collective-permute-start | bytes 491528 | tf_op jit(solution)/shard_map/ppermute | solution.py:22
  51.4 1.0 %copy-start.1 = (bf16[320,512]{1,0:T(8,128)(2,1)S(1)}, bf16[320,512]{1,0:T(8,128)(2,1)}, u32[]{:S(2)}) copy-start(bf16[320,512]{1,0:T(8,128)(2,1)} %weight_ref.1) | copy-start | bytes 983044
  53.7 4.8 %collective-permute-start.18 = (bf16[160,576]{1,0:T(8,128)(2,1)S(1)}, bf16[160,576]{1,0:T(8,128)(2,1)S(1)}, u32[]{:S(2)}, u32[]{:S(2)}) collective-permute-start(bf16[160,576]{1,0:T(8,128)(2,1)S(1)} %get-tuple-element.72), channel_id=1, source_target_pairs={{0,1},{1,0},{2,3},{3,2},{4,5},{5,4},{6,7},{7,6},{8,9},{9,8},{10,11... | collective-permute-start | bytes 552968 | tf_op jit(solution)/shard_map/ppermute | solution.py:22
  55.4 6.8 %collective-permute-start.8 = (bf16[144,512]{1,0:T(8,128)(2,1)S(1)}, bf16[144,512]{1,0:T(8,128)(2,1)S(1)}, u32[]{:S(2)}, u32[]{:S(2)}) collective-permute-start(bf16[144,512]{1,0:T(8,128)(2,1)S(1)} %get-tuple-element.58), channel_id=1, source_target_pairs={{0,2},{2,0},{1,3},{3,1},{4,6},{6,4},{5,7},{7,5},{8,10},{10,8},{9,1... | collective-permute-start | bytes 442376 | tf_op jit(solution)/shard_map/ppermute | solution.py:22
  57.5 9.9 %collective-permute-start.16 = (bf16[160,512]{1,0:T(8,128)(2,1)S(1)}, bf16[160,512]{1,0:T(8,128)(2,1)S(1)}, u32[]{:S(2)}, u32[]{:S(2)}) collective-permute-start(bf16[160,512]{1,0:T(8,128)(2,1)S(1)} %add_convert_fusion.3), channel_id=1, source_target_pairs={{0,2},{2,0},{1,3},{3,1},{4,6},{6,4},{5,7},{7,5},{8,10},{10,8},{9,1... | collective-permute-start | bytes 491528 | tf_op jit(solution)/shard_map/ppermute | solution.py:22
  58.6 13.0 %collective-permute-start.19 = (bf16[160,576]{1,0:T(8,128)(2,1)S(1)}, bf16[160,576]{1,0:T(8,128)(2,1)S(1)}, u32[]{:S(2)}, u32[]{:S(2)}) collective-permute-start(bf16[160,576]{1,0:T(8,128)(2,1)S(1)} %add_convert_fusion.1), channel_id=1, source_target_pairs={{0,2},{2,0},{1,3},{3,1},{4,6},{6,4},{5,7},{7,5},{8,10},{10,8},{9,1... | collective-permute-start | bytes 552968 | tf_op jit(solution)/shard_map/ppermute | solution.py:22
  62.3 5.8 %collective-permute-start.9 = (bf16[48,512]{1,0:T(8,128)(2,1)S(1)}, bf16[48,512]{1,0:T(8,128)(2,1)S(1)}, u32[]{:S(2)}, u32[]{:S(2)}) collective-permute-start(bf16[48,512]{1,0:T(8,128)(2,1)S(1)} %get-tuple-element.60), channel_id=1, source_target_pairs={{0,4},{4,0},{8,12},{12,8},{1,5},{5,1},{9,13},{13,9},{2,6},{6,2},{1... | collective-permute-start | bytes 147464 | tf_op jit(solution)/shard_map/ppermute | solution.py:22
  64.9 5.0 %collective-permute-start.10 = (bf16[48,512]{1,0:T(8,128)(2,1)S(1)}, bf16[48,512]{1,0:T(8,128)(2,1)S(1)}, u32[]{:S(2)}, u32[]{:S(2)}) collective-permute-start(bf16[48,512]{1,0:T(8,128)(2,1)S(1)} %get-tuple-element.61), channel_id=1, source_target_pairs={{0,8},{4,12},{8,0},{12,4},{1,9},{5,13},{9,1},{13,5},{2,10},{6,14},... | collective-permute-start | bytes 147464 | tf_op jit(solution)/shard_map/ppermute | solution.py:22
  64.9 6.0 %collective-permute-start.11 = (bf16[48,512]{1,0:T(8,128)(2,1)S(1)}, bf16[48,512]{1,0:T(8,128)(2,1)S(1)}, u32[]{:S(2)}, u32[]{:S(2)}) collective-permute-start(bf16[48,512]{1,0:T(8,128)(2,1)S(1)} %get-tuple-element.62), channel_id=1, source_target_pairs={{0,12},{4,8},{8,4},{12,0},{1,13},{5,9},{9,5},{13,1},{2,14},{6,10},... | collective-permute-start | bytes 147464 | tf_op jit(solution)/shard_map/ppermute | solution.py:22
  67.4 4.3 %collective-permute-start.17 = (bf16[160,512]{1,0:T(8,128)(2,1)S(1)}, bf16[160,512]{1,0:T(8,128)(2,1)S(1)}, u32[]{:S(2)}, u32[]{:S(2)}) collective-permute-start(bf16[160,512]{1,0:T(8,128)(2,1)S(1)} %add_convert_fusion.2), channel_id=1, source_target_pairs={{0,1},{1,0},{2,3},{3,2},{4,5},{5,4},{6,7},{7,6},{8,9},{9,8},{10,11... | collective-permute-start | bytes 491528 | tf_op jit(solution)/shard_map/ppermute | solution.py:22
  71.6 1.5 %collective-permute-start.20 = (bf16[160,576]{1,0:T(8,128)(2,1)S(1)}, bf16[160,576]{1,0:T(8,128)(2,1)S(1)}, u32[]{:S(2)}, u32[]{:S(2)}) collective-permute-start(bf16[160,576]{1,0:T(8,128)(2,1)S(1)} %add_convert_fusion), channel_id=1, source_target_pairs={{0,1},{1,0},{2,3},{3,2},{4,5},{5,4},{6,7},{7,6},{8,9},{9,8},{10,11... | collective-permute-start | bytes 552968 | tf_op jit(solution)/shard_map/ppermute | solution.py:22
where the time goes:
time: 74.5 us; the launch traced here: 74.2 us
  starting transfers between devices  29.1 us (39%)
  waiting for transfers between devices  27.2 us (37%)
  Pallas kernels  11.6 us (16%)
  other arithmetic  3.13 us (4%)
  local copies, waits for them, and re-layouts  1.7 us (2%)
  between operations  1.53 us (2%)
    ppermute x17, waiting for transfers between devices, swap(): lax.ppermute(value, axis, [(i, i ^ step) for i in range(lax.axis_size(axi...  25.9 us
    ppermute x17, starting transfers between devices, swap(): lax.ppermute(value, axis, [(i, i ^ step) for i in range(lax.axis_size(axi...  19.9 us
    pallas_call x11, Pallas kernels, call(): pl.pallas_call(kernel, out_shape=shapes, in_specs=specs or [SMEM if jnp.i...  11.6 us
    ppermute x4, starting transfers between devices, with_neighbours(): lax.ppermute(value, axis, pairs + [(b, a) for a, b in pairs])  9.19 us
    unnamed x14, local copies, waits for them, and re-layouts  1.7 us
  transfers between devices with their start and end apart: 21, of which 9 were waited for; matrix products, arithmetic and copies ran while one was open for 3% of the time, Pallas kernels for 12%

commit v1 on v0

--- a/solution.py
+++ b/solution.py
@@ -31,13 +31,6 @@
     return received
 
 
-def in_order(received, axis):
-    even = lax.axis_index(axis) % 2 == 0
-    near = received[0]
-    far = received[1] if len(received) > 1 else jnp.zeros_like(near)
-    return jnp.where(even, far, near), jnp.where(even, near, far)
-
-
 def tree_sum(terms):
     while len(terms) > 1:
         terms = [a + b for a, b in zip(terms[::2], terms[1::2])] + terms[len(terms) & ~1 :]
@@ -45,14 +38,22 @@
 
 
 def full_sum(keep, send):
+    rows, lanes = keep.shape
     total = (keep.astype(F32) + swap(send, "rep", 1).astype(F32)).astype(BF16)
     step = 1
     while step < lax.axis_size("col"):
         total = (total.astype(F32) + swap(total, "col", step).astype(F32)).astype(BF16)
         step *= 2
     remote = swap(total, "rep", 1)
-    first = lax.axis_index("rep") == 0
-    return jnp.concatenate([jnp.where(first, total, remote), jnp.where(first, remote, total)], axis=0)
+    (whole,) = call(join_kernel, [((2 * rows, lanes), F32)], [total, remote])
+    return whole
+
+
+def join_kernel(total_ref, remote_ref, out_ref):
+    rows = total_ref.shape[0]
+    rep = lax.axis_index("rep")
+    out_ref[pl.ds(pl.multiple_of(rep * rows, 16), rows), :] = total_ref[...].astype(F32)
+    out_ref[pl.ds(pl.multiple_of((1 - rep) * rows, 16), rows), :] = remote_ref[...].astype(F32)
 
 
 def silu_slope(value):
@@ -74,14 +75,22 @@
     )
 
 
-def window_rows(field_ref, near, far, even, slot):
+def window_rows(field_ref, halo_refs, slot, inner):
+    even = lax.rem(lax.axis_index("col"), 2) == 0
+    near = halo_refs[0][slot].astype(F32)
+    far = halo_refs[1][slot].astype(F32) if len(halo_refs) > 1 else jnp.zeros_like(near)
     left, right = jnp.where(even, far, near), jnp.where(even, near, far)
     whole = jnp.concatenate([left, field_ref[slot].astype(F32), right], axis=1)
     half = LANES // 2
     tiles = [whole[:, i : i + LANES] for i in range(0, whole.shape[1], LANES)]
     low = lane_below(tiles[0].shape, half)
     tiles = [pltpu.roll(t, half, 1) for t in tiles]
-    middle = jnp.concatenate([jnp.where(low, a, b) for a, b in zip(tiles, tiles[1:])], axis=1)
+    tiles = [jnp.where(low, a, b) for a, b in zip(tiles, tiles[1:])]
+    if inner:
+        tiles = tiles[1:-1]
+    elif len(halo_refs) == 1:
+        tiles = [jnp.where(even, b, a) for a, b in zip(tiles, tiles[1:])]
+    middle = jnp.concatenate(tiles, axis=1)
     height = middle.shape[0]
     row = lax.broadcasted_iota(jnp.int32, middle.shape, 0)
     above = jnp.where(row == 0, 0.0, pltpu.roll(middle, 1, 0))
@@ -141,13 +150,6 @@
     copies[3].wait()
 
 
-def slot_inputs(field_ref, kernel_ref, halo_refs, slot):
-    even = lax.rem(lax.axis_index("col"), 2) == 0
-    near = halo_refs[0][slot].astype(F32)
-    far = halo_refs[1][slot].astype(F32) if len(halo_refs) > 1 else jnp.zeros_like(near)
-    return window_rows(field_ref, near, far, even, slot), kernel_ref[slot]
-
-
 def gate_of(shifted, weight):
     shifted = [s.astype(BF16) for s in shifted]
     pairs = shifted[0].shape[1] // LANES - 1
@@ -162,41 +164,40 @@
     return gate.reshape(pairs, -1, LANES)
 
 
-def features_kernel(tiles, count_ref, field_ref, kernel_ref, weight_ref, *refs):
+def sent_pairs(width, cols):
+    return width // 2 + (1 if cols == 2 else 2)
+
+
+def features_kernel(tiles, pairs, count_ref, field_ref, kernel_ref, weight_ref, *refs):
     halo_refs, out_refs, store = refs[: -tiles - 1], refs[-tiles - 1 : -1], refs[-1]
-    slots, height, lanes = field_ref.shape
-    pairs = lanes // LANES + 2
+    slots, height, _ = field_ref.shape
     main = ROWS * pairs
     col = lax.axis_index("col")
 
     def values(slot):
-        shifted, weight = slot_inputs(field_ref, kernel_ref, halo_refs, slot)
-        gate = gate_of(shifted, weight)
+        gate = gate_of(window_rows(field_ref, halo_refs, slot, False), kernel_ref[slot])
         value = gate / (1.0 + jnp.exp(-gate))
         live = slot < count_ref[0]
+        if len(halo_refs) == 1:
+            return jnp.where(live, value, 0.0)
         first = jnp.where(live & (col > 0), value[:1], 0.0)
         last = jnp.where(live & (col < lax.axis_size("col") - 1), value[-1:], 0.0)
         return jnp.concatenate([first, jnp.where(live, value[1:-1], 0.0), last], axis=0)
 
-    def around(bands, j):
-        none = jnp.zeros_like(bands[0])
-        sub = lax.broadcasted_iota(jnp.int32, none.shape, 1)
-        both = jnp.where(sub >= 4, bands[j - 1] if j else none, bands[j + 1] if j + 1 < len(bands) else none)
-        packed = [
-            jnp.where(sub[0] < 4, pltpu.roll(both[q], 2, 0), pltpu.roll(both[q + 1], 6, 0))
-            for q in range(0, pairs, 2)
-        ]
-        return jnp.concatenate(packed, axis=0)
-
     def put(both, lane_tile):
         here = slice(lane_tile * LANES, (lane_tile + 1) * LANES)
         bands = [[v[:, ROWS * j : ROWS * (j + 1)] for j in range(height // ROWS)] for v in both]
+        none = jnp.zeros_like(bands[0][0])
+        sub = lax.broadcasted_iota(jnp.int32, none.shape, 1)
         for j in range(height // ROWS):
+            halo = []
             for half in range(2):
                 rows = bands[half][j].reshape(main, LANES)
                 store[j, half * main : (half + 1) * main, here] = rows.astype(BF16)
-            halo = jnp.concatenate([around(bands[half], j) for half in range(2)], axis=0)
-            store[j, 2 * main :, here] = halo.astype(BF16)
+                above = bands[half][j - 1] if j else none
+                below = bands[half][j + 1] if ROWS * (j + 1) < height else none
+                halo.append(pltpu.roll(jnp.where(sub >= 4, above, below), 2 + 4 * half, 1))
+            store[j, 2 * main :, here] = jnp.where(sub < 4, *halo).reshape(main, LANES).astype(BF16)
 
     for slot in range(0, slots - 1, 2):
         put(interleave(values(slot), values(slot + 1)), slot // 2)
@@ -218,8 +219,8 @@
         return jnp.concatenate([value[:, ROWS * j : ROWS * (j + 1)] for j in range(bands)], axis=0)
 
     def values(slot):
-        shifted, weight = slot_inputs(field_ref, kernel_ref, halo_refs, slot)
-        gate = gate_of(shifted, weight)[1:-1]
+        shifted = window_rows(field_ref, halo_refs, slot, True)
+        gate = gate_of(shifted, kernel_ref[slot])
         live = slot < count_ref[0]
         slope = by_band(jnp.where(live, silu_slope(gate), 0.0))
         patch_ref[slot, :, 6 * LANES :] = slope.reshape(-1, LANES).astype(BF16)
@@ -228,7 +229,7 @@
                 [
                     s[ROWS * j : ROWS * (j + 1), p * LANES : (p + 2) * LANES]
                     for j in range(bands)
-                    for p in range(1, pairs + 1)
+                    for p in range(pairs)
                 ],
                 axis=0,
             )
@@ -252,13 +253,18 @@
         put(*interleave(last, jnp.zeros_like(last)), slots // 2)
 
 
-def upstream_kernel(main_ref, left_ref, right_ref, top_ref, bottom_ref, mix_ref, grad_ref, rows_ref):
+def upstream_kernel(main_ref, top_ref, bottom_ref, mix_ref, *refs):
+    column_refs, (grad_ref, rows_ref) = refs[:-2], refs[-2:]
     width = grad_ref.shape[0] - 2
     cells, hidden = main_ref.shape
     rows_ref[...] = jnp.zeros_like(rows_ref)
+    even = lax.rem(lax.axis_index("col"), 2) == 0
+    near = column_refs[0][...]
+    far = column_refs[1][...] if len(column_refs) > 1 else jnp.zeros_like(near)
     places = (0, cells, cells + 16, cells + 32, cells + 32 + width)
-    for place, ref in zip(places, (main_ref, left_ref, right_ref, top_ref, bottom_ref)):
-        rows_ref[place : place + ref.shape[0], :] = ref[...]
+    values = (main_ref[...], jnp.where(even, far, near), jnp.where(even, near, far), top_ref[...], bottom_ref[...])
+    for place, value in zip(places, values):
+        rows_ref[place : place + value.shape[0], :] = value
     shape = ((width + 2) * 16, rows_ref.shape[0])
     target = lax.broadcasted_iota(jnp.int32, shape, 0)
     source = lax.broadcasted_iota(jnp.int32, shape, 1)
@@ -281,18 +287,24 @@
 def middle_kernel(tiles, grad_ref, depth_ref, *refs):
     term_refs, (act_grad_ref, hidden_ref, act, inner) = refs[:tiles], refs[tiles:]
     width, hidden = grad_ref.shape[0] - 2, grad_ref.shape[2]
-    pairs = width // 2 + 2
+    cols = lax.axis_size("col")
+    pairs = sent_pairs(width, cols)
     main = ROWS * pairs
+    before_block = jnp.where(lax.axis_index("col") == 0, 2, 0) if cols == 2 else 0
     chunks = [(n, slice(n * LANES, (n + 1) * LANES)) for n in range(hidden // LANES)]
     for n, here in chunks:
         total = tree_sum([ref[:, here].astype(F32) for ref in term_refs]).astype(BF16).astype(F32)
         for p in range(pairs):
             for half in range(2):
+                column = before_block + 2 * p + half
                 start = half * main + ROWS * p
-                act[n, 2 * p + half, 2 : 2 + ROWS, :] = total[start : start + ROWS]
-                start = 2 * main + half * main // 2 + 4 * p
-                act[n, 2 * p + half, 0:2, :] = total[start : start + 2]
-                act[n, 2 * p + half, 2 + ROWS : 4 + ROWS, :] = total[start + 2 : start + 4]
+                act[n, column, 2 : 2 + ROWS, :] = total[start : start + ROWS]
+                start = 2 * main + ROWS * p + 4 * half
+                act[n, column, 0:2, :] = total[start : start + 2]
+                act[n, column, 2 + ROWS : 4 + ROWS, :] = total[start + 2 : start + 4]
+        if cols == 2:
+            for half in range(2):
+                act[n, lax.rem(before_block + width + 2, width + 4) + half] = jnp.zeros(act.shape[2:], F32)
 
     def forward(column, carry):
         for n, here in chunks:
@@ -384,6 +396,27 @@
     depth_ref[...] = total[rows : rows + depth_ref.shape[0]]
 
 
+def corner_kernel(ends, sides, *refs):
+    row_refs, edge_refs, (top_ref, bottom_ref), out_refs = (
+        refs[:ends],
+        refs[ends : ends + sides],
+        refs[ends + sides : ends + sides + 2],
+        refs[ends + sides + 2 :],
+    )
+    even = lax.rem(lax.axis_index("tile"), 2) == 0
+    near = row_refs[0][...].astype(F32)
+    far = row_refs[1][...].astype(F32) if ends > 1 else jnp.zeros_like(near)
+    top, bottom = jnp.where(even, far, near), jnp.where(even, near, far)
+    top_ref[...] = top.astype(BF16)
+    bottom_ref[...] = bottom.astype(BF16)
+    last = lax.rem(lax.axis_index("col"), 2) == 0
+    for i, (edge, out) in enumerate(zip(edge_refs, out_refs)):
+        pick = last if i == 0 else ~last
+        ends_of = [jnp.where(pick, row[-1:], row[:1]) for row in (top, bottom)]
+        blank = jnp.zeros((16 - ROWS - 2, top.shape[1]), F32)
+        out[...] = jnp.concatenate([ends_of[0], edge[...].astype(F32), ends_of[1], blank], axis=0).astype(BF16)
+
+
 def in_gradient_kernel(tiles, own_ref, *refs):
     grad_refs, (keep, send, whole, held) = refs[:tiles], refs[tiles:]
     cells = grad_refs[0].shape[0]
@@ -469,9 +502,9 @@
     width = forcing.shape[3] // channels
     hidden = mixing_input_weight.shape[1]
     tiles, cols, reps = (lax.axis_size(a) for a in ("tile", "col", "rep"))
-    pairs = width // 2 + 2
+    pairs = sent_pairs(width, cols)
     cells = ROWS * width
-    assert height == ROWS * tiles and 2 * channels == LANES and pairs % 2 == 0
+    assert height == ROWS * tiles and 2 * channels == LANES
     lane_tiles = -(-slots // 2)
     rows = hidden // (tiles * cols * reps)
 
@@ -495,9 +528,9 @@
         specs=[HBM] * 4,
     )
     halos = with_neighbours(edges[:sides], "col")
-    top, bottom = in_order(with_neighbours(edges[2 * sides :], "tile"), "tile")
+    rows_near = with_neighbours(edges[2 * sides :], "tile")
     sent = call(
-        functools.partial(features_kernel, tiles),
+        functools.partial(features_kernel, tiles, pairs),
         [((3 * ROWS * pairs, hidden), BF16)] * tiles,
         [member_counts, field, kernel, weight, *halos],
         [pltpu.VMEM((tiles, 3 * ROWS * pairs, lane_tiles * LANES), BF16)],
@@ -505,18 +538,17 @@
     )
     terms = [swap(sent[step], "tile", step) if step else sent[0] for step in range(tiles)]
 
-    even = lax.axis_index("col") % 2 == 0
-    columns = []
-    for i, edge in enumerate(edges[sides : 2 * sides]):
-        last = even if i == 0 else ~even
-        corners = [jnp.where(last, row[-1:], row[:1]) for row in (top, bottom)]
-        columns.append(jnp.concatenate([corners[0], edge, corners[1]], axis=0))
-    left, right = in_order(with_neighbours(columns, "col"), "col")
+    top, bottom, *columns = call(
+        functools.partial(corner_kernel, ends, sides),
+        [((width, hidden), BF16)] * 2 + [((16, hidden), BF16)] * sides,
+        [*rows_near, *edges[sides : 2 * sides]],
+    )
+    columns = with_neighbours(columns, "col")
     flat_upstream = upstream.reshape(cells, hidden)
     (hidden_grad,) = call(
         upstream_kernel,
         [((width + 2, 16, hidden), F32)],
-        [flat_upstream, left, right, top, bottom, mix_weight],
+        [flat_upstream, top, bottom, mix_weight, *columns],
         [pltpu.VMEM((2 * LANES, hidden), BF16)],
         flops=1 << 28,
     )
@@ -580,9 +612,9 @@
         [pltpu.VMEM((2 * half, 9 * channels), BF16)],
         flops=1 << 28,
     )
-    in_grad = full_sum(in_keep, in_send).astype(F32)
+    in_grad = full_sum(in_keep, in_send)
     group_grad = full_sum(group_keep, group_send).reshape(slots, channels, -1)
-    group_grad = jnp.swapaxes(group_grad, 1, 2).astype(F32)
+    group_grad = jnp.swapaxes(group_grad, 1, 2)
     return (adjusted.reshape(cotangent.shape), mix_grad, depth_grad, in_grad, group_grad)
 
 

time: 74.5 us -> 77.6 us (1.042)
  waiting for transfers between devices: 27.2 us -> 33.6 us
  other arithmetic: 3.13 us -> 0.2 us
  local copies, waits for them, and re-layouts: 1.7 us -> 0.01 us
  starting transfers between devices: 29.1 us -> 30 us
    ppermute x4, waiting for transfers between devices: 1.3 us -> 13.3 us  [with_neighbours(): lax.ppermute(value, axis, pairs + [(b, a) for a, b in pairs])]
    ppermute x17, waiting for transfers between devices: 25.9 us -> 20.3 us  [swap(): lax.ppermute(value, axis, [(i, i ^ step) for i in range(lax.axis_size(axi...]
    ppermute x17, starting transfers between devices: 19.9 us -> 23.8 us  [swap(): lax.ppermute(value, axis, [(i, i ^ step) for i in range(lax.axis_size(axi...]
    ppermute x4, starting transfers between devices: 9.19 us -> 6.14 us  [with_neighbours(): lax.ppermute(value, axis, pairs + [(b, a) for a, b in pairs])]
    convert_element_type x2 -> x0, other arithmetic: 1.86 us -> none  [the longest x1 0.95 us: program(): group_grad = jnp.swapaxes(group_grad, 1, 2).astype(F32)]
    unnamed x14 -> x6, local copies, waits for them, and re-layouts: 1.7 us -> 0.01 us
    convert_element_type x2, other arithmetic: 1.01 us -> 0.1 us  [full_sum(): total = (keep.astype(F32) + swap(send, 'rep', 1).astype(F32)).astype(BF16)]
    pallas_call x11 -> x14, Pallas kernels: 11.6 us -> 12.2 us  [call(): pl.pallas_call(kernel, out_shape=shapes, in_specs=specs or [SMEM if jnp.i...]
  transfers between devices with their start and end apart: 21 -> 21, of which waited for: 9 -> 8; matrix products, arithmetic and copies ran while one was open for 3% -> 0% of each run, Pallas kernels for 12% -> 9%
where the time goes in v1:
time: 77.6 us; the launch traced here: 77.4 us
  waiting for transfers between devices  33.6 us (43%)
  starting transfers between devices  30 us (39%)
  Pallas kernels  12.2 us (16%)
  between operations  1.46 us (2%)
    ppermute x17, starting transfers between devices, swap(): lax.ppermute(value, axis, [(i, i ^ step) for i in range(lax.axis_size(axi...  23.8 us
    ppermute x17, waiting for transfers between devices, swap(): lax.ppermute(value, axis, [(i, i ^ step) for i in range(lax.axis_size(axi...  20.3 us
    ppermute x4, waiting for transfers between devices, with_neighbours(): lax.ppermute(value, axis, pairs + [(b, a) for a, b in pairs])  13.3 us
    pallas_call x14, Pallas kernels, call(): pl.pallas_call(kernel, out_shape=shapes, in_specs=specs or [SMEM if jnp.i...  12.2 us
    ppermute x4, starting transfers between devices, with_neighbours(): lax.ppermute(value, axis, pairs + [(b, a) for a, b in pairs])  6.14 us
  transfers between devices with their start and end apart: 21, of which 8 were waited for; matrix products, arithmetic and copies ran while one was open for 0% of the time, Pallas kernels for 9%

profile of v1, /device:TPU:0, one launch (start us, length us, event | category | flops | bytes accessed | tf_op | source)
XLA Modules:
  0.0 77.4 jit_solution(9289466899453588098)
XLA Ops:
  0.7 1.4 %shard_map.110 = (bf16[5,32,1024]{2,1,0:T(8,128)(2,1)S(1)}, bf16[5,128,768]{2,1,0:T(8,128)(2,1)S(1)}, bf16[384,512]{1,0:T(8,128)(2,1)S(1)}, bf16[8,16,512]{2,1,0...) custom-call(bf16[5,32,1024]{2,1,0:T(8,128)(2,1)} %bitcast.17, ...), custom_call_target="tpu_custom_call" | custom-call | flops 16777216 | bytes 3112960 | tf_op jit(solution)/shard_map/pallas_call | solution.py:479
  2.1 3.0 %collective-permute-start.3 = (bf16[5,32,256]{2,1,0:T(8,128)(2,1)S(1)}, bf16[5,32,256]{2,1,0:T(8,128)(2,1)S(1)}, u32[]{:S(2)}, u32[]{:S(2)}) collective-permute-start(bf16[5,32,256]{2,1,0:T(8,128)(2,1)S(1)} %get-tuple-element.52), channel_id=1, source_target_pairs={{0,2},{2,0},{1,3},{3,1},{4,6},{6,4},{5,7},{7,5},{8,10},{10,8},{9,1... | collective-permute-start | bytes 245768 | tf_op jit(solution)/shard_map/ppermute | solution.py:30
  5.8 1.8 %collective-permute-done.3.refs_0_ = bf16[5,32,256]{2,1,0:T(8,128)(2,1)S(1)} collective-permute-done((bf16[5,32,256]{2,1,0:T(8,128)(2,1)S(1)}, bf16[5,32,256]{2,1,0:T(8,128)(2,1)S(1)}, u32[]{:S(2)}, u32[]{:S(2)}) %collective-permute-start.3) | collective-permute-done | bytes 81952 | tf_op jit(solution)/shard_map/ppermute | solution.py:30
  7.6 1.7 %shard_map.113 = (bf16[216,512]{1,0:T(8,128)(2,1)S(1)}, bf16[216,512]{1,0:T(8,128)(2,1)S(1)}, bf16[216,512]{1,0:T(8,128)(2,1)S(1)}, bf16[216,512]{1,0:T(8,128)(2,1)S(1)}) custom-call(s32[1]{0:T(128)S(6)} %copy.12.count_ref, bf16[5,32,1024]{2,1,0:T(8,128)(2,1)S(1)} %get-tuple-element.49.field_ref, bf16[5,128,768]{2,1,0:T(8,128)(2,1)S(1)} %get-tuple-element.50.kernel_ref, ...), custom_call_target="tpu_custom_call" | custom-call | flops 268435456 | bytes 2670596 | tf_op jit(solution)/shard_map/pallas_call | solution.py:479
  9.2 2.2 %collective-permute-start.4 = (bf16[216,512]{1,0:T(8,128)(2,1)S(1)}, bf16[216,512]{1,0:T(8,128)(2,1)S(1)}, u32[]{:S(2)}, u32[]{:S(2)}) collective-permute-start(bf16[216,512]{1,0:T(8,128)(2,1)S(1)} %get-tuple-element.54), channel_id=1, source_target_pairs={{0,4},{4,0},{8,12},{12,8},{1,5},{5,1},{9,13},{13,9},{2,6},{6,2},{1... | collective-permute-start | bytes 663560 | tf_op jit(solution)/shard_map/ppermute | solution.py:22
  11.4 2.6 %collective-permute-start.5 = (bf16[216,512]{1,0:T(8,128)(2,1)S(1)}, bf16[216,512]{1,0:T(8,128)(2,1)S(1)}, u32[]{:S(2)}, u32[]{:S(2)}) collective-permute-start(bf16[216,512]{1,0:T(8,128)(2,1)S(1)} %get-tuple-element.55), channel_id=1, source_target_pairs={{0,8},{4,12},{8,0},{12,4},{1,9},{5,13},{9,1},{13,5},{2,10},{6,14},... | collective-permute-start | bytes 663560 | tf_op jit(solution)/shard_map/ppermute | solution.py:22
  14.0 0.9 %collective-permute-start = (bf16[16,512]{1,0:T(8,128)(2,1)S(1)}, bf16[16,512]{1,0:T(8,128)(2,1)S(1)}, u32[]{:S(2)}, u32[]{:S(2)}) collective-permute-start(bf16[16,512]{1,0:T(8,128)(2,1)S(1)} %get-tuple-element.43), channel_id=1, source_target_pairs={{0,4},{8,12},{4,0},{12,8},{1,5},{9,13},{5,1},{13,9},{2,6},{10,14},... | collective-permute-start | bytes 49160 | tf_op jit(solution)/shard_map/ppermute | solution.py:30
  14.9 0.7 collective-permute-start.1
  15.6 9.3 %collective-permute-done.refs_0_ = bf16[16,512]{1,0:T(8,128)(2,1)S(1)} collective-permute-done((bf16[16,512]{1,0:T(8,128)(2,1)S(1)}, bf16[16,512]{1,0:T(8,128)(2,1)S(1)}, u32[]{:S(2)}, u32[]{:S(2)}) %collective-permute-start) | collective-permute-done | bytes 16416 | tf_op jit(solution)/shard_map/ppermute | solution.py:30
  24.9 1.6 %collective-permute-start.2 = (bf16[16,512]{1,0:T(8,128)(2,1)S(1)}, bf16[16,512]{1,0:T(8,128)(2,1)S(1)}, u32[]{:S(2)}, u32[]{:S(2)}) collective-permute-start(bf16[16,512]{1,0:T(8,128)(2,1)S(1)} %get-tuple-element.48), channel_id=1, source_target_pairs={{0,2},{2,0},{1,3},{3,1},{4,6},{6,4},{5,7},{7,5},{8,10},{10,8},{9,1... | collective-permute-start | bytes 49160 | tf_op jit(solution)/shard_map/ppermute | solution.py:30
  26.4 2.2 %collective-permute-done.2.refs_0_ = bf16[16,512]{1,0:T(8,128)(2,1)S(1)} collective-permute-done((bf16[16,512]{1,0:T(8,128)(2,1)S(1)}, bf16[16,512]{1,0:T(8,128)(2,1)S(1)}, u32[]{:S(2)}, u32[]{:S(2)}) %collective-permute-start.2) | collective-permute-done | bytes 16416 | tf_op jit(solution)/shard_map/ppermute | solution.py:30
  29.1 0.8 %collective-permute-done.5.refs_2_ = bf16[216,512]{1,0:T(8,128)(2,1)S(1)} collective-permute-done((bf16[216,512]{1,0:T(8,128)(2,1)S(1)}, bf16[216,512]{1,0:T(8,128)(2,1)S(1)}, u32[]{:S(2)}, u32[]{:S(2)}) %collective-permute-start.5) | collective-permute-done | bytes 221216 | tf_op jit(solution)/shard_map/ppermute | solution.py:22
  30.0 1.5 %shard_map.114 = (bf16[16,8,512]{2,1,0:T(8,128)(2,1)S(1)}, f32[18,8,512]{2,1,0:T(8,128)S(1)}, f32[4,20,16,128]{3,2,1,0:T(8,128)S(1)}, f32[4,18,16,128]{3,2,1,0:T(8,128)S(1)}) custom-call(f32[18,16,512]{2,1,0:T(8,128)S(1)} %shard_map.112.grad_ref, f32[9,512]{1,0:T(8,128)S(1)} %copy-done.2, bf16[216,512]{1,0:T(8,128)(2,1)S(1)} %get-tuple-element.53.refs_0_, ...), custom_call_target="tpu_custom_call" | custom-call | flops 16777216 | bytes 3164160 | tf_op jit(solution)/shard_map/pallas_call | solution.py:479
  31.4 7.7 %collective-permute-start.12 = (bf16[128,512]{1,0:T(8,128)(2,1)S(1)}, bf16[128,512]{1,0:T(8,128)(2,1)S(1)}, u32[]{:S(2)}, u32[]{:S(2)}) collective-permute-start(bf16[128,512]{1,0:T(8,128)(2,1)S(1)} %bitcast.11), channel_id=1, source_target_pairs={{0,4},{4,0},{8,12},{12,8},{1,5},{5,1},{9,13},{13,9},{2,6},{6,2},{1... | collective-permute-start | bytes 393224 | tf_op jit(solution)/shard_map/ppermute | solution.py:22
  39.1 1.1 %collective-permute-start.13 = (bf16[128,512]{1,0:T(8,128)(2,1)S(1)}, bf16[128,512]{1,0:T(8,128)(2,1)S(1)}, u32[]{:S(2)}, u32[]{:S(2)}) collective-permute-start(bf16[128,512]{1,0:T(8,128)(2,1)S(1)} %bitcast.12), channel_id=1, source_target_pairs={{0,8},{4,12},{8,0},{12,4},{1,9},{5,13},{9,1},{13,5},{2,10},{6,14},... | collective-permute-start | bytes 393224 | tf_op jit(solution)/shard_map/ppermute | solution.py:22
  40.2 1.4 %collective-permute-start.14 = (bf16[128,512]{1,0:T(8,128)(2,1)S(1)}, bf16[128,512]{1,0:T(8,128)(2,1)S(1)}, u32[]{:S(2)}, u32[]{:S(2)}) collective-permute-start(bf16[128,512]{1,0:T(8,128)(2,1)S(1)} %bitcast.13), channel_id=1, source_target_pairs={{0,12},{4,8},{8,4},{12,0},{1,13},{5,9},{9,5},{13,1},{2,14},{6,10},... | collective-permute-start | bytes 393224 | tf_op jit(solution)/shard_map/ppermute | solution.py:22
  41.6 1.5 %shard_map.115 = (bf16[128,512]{1,0:T(8,128)(2,1)}, bf16[272,512]{1,0:T(8,128)(2,1)S(1)}, bf16[272,512]{1,0:T(8,128)(2,1)S(1)}) custom-call(f32[18,8,512]{2,1,0:T(8,128)S(1)} %get-tuple-element.57.hidden_ref, bf16[128,512]{1,0:T(8,128)(2,1)S(1)} %bitcast.10, bf16[512,512]{1,0:T(8,128)(2,1)S(1)} %copy-done, f32[4,20,16,128]{3,2,1,0:T(8,128)S(1)} %get-tuple-element.58.act, ...), custom_call_target="tpu_custom_call" | custom-call | flops 16777216 | bytes 2883584 | tf_op jit(solution)/shard_map/pallas_call | solution.py:479
  43.1 1.1 %shard_map.119 = (bf16[5,256,896]{2,1,0:T(8,128)(2,1)S(1)}, bf16[512,384]{1,0:T(8,128)(2,1)S(1)}) custom-call(s32[1]{0:T(128)S(6)} %copy.12.count_ref, bf16[5,32,1024]{2,1,0:T(8,128)(2,1)S(1)} %get-tuple-element.49.field_ref, bf16[5,128,768]{2,1,0:T(8,128)(2,1)S(1)} %get-tuple-element.50.kernel_ref, bf16[5,32,256]{2,1,0:T(8,128)(2,1)S(1)} %collective-permute-done.3.refs_0_), custom_call_target="tpu_custom_call" | custom-call | flops 268435456 | bytes 4079620 | tf_op jit(solution)/shard_map/pallas_call | solution.py:479
  44.2 4.9 %collective-permute-done.13.refs_2_ = bf16[128,512]{1,0:T(8,128)(2,1)S(1)} collective-permute-done((bf16[128,512]{1,0:T(8,128)(2,1)S(1)}, bf16[128,512]{1,0:T(8,128)(2,1)S(1)}, u32[]{:S(2)}, u32[]{:S(2)}) %collective-permute-start.13) | collective-permute-done | bytes 131104 | tf_op jit(solution)/shard_map/ppermute | solution.py:22
  49.6 1.4 %shard_map.122 = (bf16[160,576]{1,0:T(8,128)(2,1)S(1)}, bf16[160,576]{1,0:T(8,128)(2,1)S(1)}) custom-call(bf16[512,512]{1,0:T(8,128)(2,1)S(1)} %get-tuple-element.75.rows_ref, bf16[320,512]{1,0:T(8,128)(2,1)S(1)} %copy-done.1, bf16[5,256,896]{2,1,0:T(8,128)(2,1)S(1)} %get-tuple-element.76.patch_ref), custom_call_target="tpu_custom_call" | custom-call | flops 268435456 | bytes 3514368 | tf_op jit(solution)/shard_map/pallas_call | solution.py:479
  51.7 1.6 %collective-permute-start.8 = (bf16[144,512]{1,0:T(8,128)(2,1)S(1)}, bf16[144,512]{1,0:T(8,128)(2,1)S(1)}, u32[]{:S(2)}, u32[]{:S(2)}) collective-permute-start(bf16[144,512]{1,0:T(8,128)(2,1)S(1)} %get-tuple-element.64), channel_id=1, source_target_pairs={{0,2},{2,0},{1,3},{3,1},{4,6},{6,4},{5,7},{7,5},{8,10},{10,8},{9,1... | collective-permute-start | bytes 442376 | tf_op jit(solution)/shard_map/ppermute | solution.py:22
  53.3 0.8 %collective-permute-start.19 = (bf16[160,576]{1,0:T(8,128)(2,1)S(1)}, bf16[160,576]{1,0:T(8,128)(2,1)S(1)}, u32[]{:S(2)}, u32[]{:S(2)}) collective-permute-start(bf16[160,576]{1,0:T(8,128)(2,1)S(1)} %add_convert_fusion.1), channel_id=1, source_target_pairs={{0,2},{2,0},{1,3},{3,1},{4,6},{6,4},{5,7},{7,5},{8,10},{10,8},{9,1... | collective-permute-start | bytes 552968 | tf_op jit(solution)/shard_map/ppermute | solution.py:22
  54.2 1.4 %collective-permute-start.16 = (bf16[160,512]{1,0:T(8,128)(2,1)S(1)}, bf16[160,512]{1,0:T(8,128)(2,1)S(1)}, u32[]{:S(2)}, u32[]{:S(2)}) collective-permute-start(bf16[160,512]{1,0:T(8,128)(2,1)S(1)} %add_convert_fusion.3), channel_id=1, source_target_pairs={{0,2},{2,0},{1,3},{3,1},{4,6},{6,4},{5,7},{7,5},{8,10},{10,8},{9,1... | collective-permute-start | bytes 491528 | tf_op jit(solution)/shard_map/ppermute | solution.py:22
  55.5 7.3 %collective-permute-done.19 = bf16[160,576]{1,0:T(8,128)(2,1)S(1)} collective-permute-done((bf16[160,576]{1,0:T(8,128)(2,1)S(1)}, bf16[160,576]{1,0:T(8,128)(2,1)S(1)}, u32[]{:S(2)}, u32[]{:S(2)}) %collective-permute-start.19) | collective-permute-done | bytes 184352 | tf_op jit(solution)/shard_map/ppermute | solution.py:22
  63.0 2.5 %collective-permute-done.16 = bf16[160,512]{1,0:T(8,128)(2,1)S(1)} collective-permute-done((bf16[160,512]{1,0:T(8,128)(2,1)S(1)}, bf16[160,512]{1,0:T(8,128)(2,1)S(1)}, u32[]{:S(2)}, u32[]{:S(2)}) %collective-permute-start.16) | collective-permute-done | bytes 163872 | tf_op jit(solution)/shard_map/ppermute | solution.py:22
  65.7 2.0 %collective-permute-start.9 = (bf16[48,512]{1,0:T(8,128)(2,1)S(1)}, bf16[48,512]{1,0:T(8,128)(2,1)S(1)}, u32[]{:S(2)}, u32[]{:S(2)}) collective-permute-start(bf16[48,512]{1,0:T(8,128)(2,1)S(1)} %get-tuple-element.66), channel_id=1, source_target_pairs={{0,4},{4,0},{8,12},{12,8},{1,5},{5,1},{9,13},{13,9},{2,6},{6,2},{1... | collective-permute-start | bytes 147464 | tf_op jit(solution)/shard_map/ppermute | solution.py:22
  67.7 1.1 %collective-permute-start.10 = (bf16[48,512]{1,0:T(8,128)(2,1)S(1)}, bf16[48,512]{1,0:T(8,128)(2,1)S(1)}, u32[]{:S(2)}, u32[]{:S(2)}) collective-permute-start(bf16[48,512]{1,0:T(8,128)(2,1)S(1)} %get-tuple-element.67), channel_id=1, source_target_pairs={{0,8},{4,12},{8,0},{12,4},{1,9},{5,13},{9,1},{13,5},{2,10},{6,14},... | collective-permute-start | bytes 147464 | tf_op jit(solution)/shard_map/ppermute | solution.py:22
  68.8 1.4 %collective-permute-start.11 = (bf16[48,512]{1,0:T(8,128)(2,1)S(1)}, bf16[48,512]{1,0:T(8,128)(2,1)S(1)}, u32[]{:S(2)}, u32[]{:S(2)}) collective-permute-start(bf16[48,512]{1,0:T(8,128)(2,1)S(1)} %get-tuple-element.68), channel_id=1, source_target_pairs={{0,12},{4,8},{8,4},{12,0},{1,13},{5,9},{9,5},{13,1},{2,14},{6,10},... | collective-permute-start | bytes 147464 | tf_op jit(solution)/shard_map/ppermute | solution.py:22
  70.2 4.7 %collective-permute-done.10.refs_2_ = bf16[48,512]{1,0:T(8,128)(2,1)S(1)} collective-permute-done((bf16[48,512]{1,0:T(8,128)(2,1)S(1)}, bf16[48,512]{1,0:T(8,128)(2,1)S(1)}, u32[]{:S(2)}, u32[]{:S(2)}) %collective-permute-start.10) | collective-permute-done | bytes 49184 | tf_op jit(solution)/shard_map/ppermute | solution.py:22
  74.9 0.7 shard_map.118
  75.6 0.9 %shard_map.121 = f32[320,512]{1,0:T(8,128)} custom-call(bf16[160,512]{1,0:T(8,128)(2,1)S(1)} %add_convert_fusion.2.total_ref, bf16[160,512]{1,0:T(8,128)(2,1)S(1)} %collective-permute-done.17.remote_ref), custom_call_target="tpu_custom_call" | custom-call | flops 16777216 | bytes 983040 | tf_op jit(solution)/shard_map/pallas_call | solution.py:479
  76.5 1.0 %shard_map.123 = f32[320,576]{1,0:T(8,128)} custom-call(bf16[160,576]{1,0:T(8,128)(2,1)S(1)} %add_convert_fusion.total_ref, bf16[160,576]{1,0:T(8,128)(2,1)S(1)} %collective-permute-done.20.remote_ref), custom_call_target="tpu_custom_call" | custom-call | flops 16777216 | bytes 1105920 | tf_op jit(solution)/shard_map/pallas_call | solution.py:479
  (34 shorter events, 2.1 us)
Async XLA Ops:
  0.6 28.0 %copy-start = (bf16[512,512]{1,0:T(8,128)(2,1)S(1)}, bf16[512,512]{1,0:T(8,128)(2,1)}, u32[]{:S(2)}) copy-start(bf16[512,512]{1,0:T(8,128)(2,1)} %mix_ref.3) | copy-start | bytes 1572868
  0.6 29.3 %copy-start.2 = (f32[9,512]{1,0:T(8,128)S(1)}, f32[9,512]{1,0:T(8,128)}, u32[]{:S(2)}) copy-start(f32[9,512]{1,0:T(8,128)} %depth_ref.1) | copy-start | bytes 55300
  2.1 5.5 %collective-permute-start.3 = (bf16[5,32,256]{2,1,0:T(8,128)(2,1)S(1)}, bf16[5,32,256]{2,1,0:T(8,128)(2,1)S(1)}, u32[]{:S(2)}, u32[]{:S(2)}) collective-permute-start(bf16[5,32,256]{2,1,0:T(8,128)(2,1)S(1)} %get-tuple-element.52), channel_id=1, source_target_pairs={{0,2},{2,0},{1,3},{3,1},{4,6},{6,4},{5,7},{7,5},{8,10},{10,8},{9,1... | collective-permute-start | bytes 245768 | tf_op jit(solution)/shard_map/ppermute | solution.py:30
  9.2 19.9 %collective-permute-start.4 = (bf16[216,512]{1,0:T(8,128)(2,1)S(1)}, bf16[216,512]{1,0:T(8,128)(2,1)S(1)}, u32[]{:S(2)}, u32[]{:S(2)}) collective-permute-start(bf16[216,512]{1,0:T(8,128)(2,1)S(1)} %get-tuple-element.54), channel_id=1, source_target_pairs={{0,4},{4,0},{8,12},{12,8},{1,5},{5,1},{9,13},{13,9},{2,6},{6,2},{1... | collective-permute-start | bytes 663560 | tf_op jit(solution)/shard_map/ppermute | solution.py:22
  11.4 18.5 %collective-permute-start.5 = (bf16[216,512]{1,0:T(8,128)(2,1)S(1)}, bf16[216,512]{1,0:T(8,128)(2,1)S(1)}, u32[]{:S(2)}, u32[]{:S(2)}) collective-permute-start(bf16[216,512]{1,0:T(8,128)(2,1)S(1)} %get-tuple-element.55), channel_id=1, source_target_pairs={{0,8},{4,12},{8,0},{12,4},{1,9},{5,13},{9,1},{13,5},{2,10},{6,14},... | collective-permute-start | bytes 663560 | tf_op jit(solution)/shard_map/ppermute | solution.py:22
  14.0 16.0 %collective-permute-start.6 = (bf16[216,512]{1,0:T(8,128)(2,1)S(1)}, bf16[216,512]{1,0:T(8,128)(2,1)S(1)}, u32[]{:S(2)}, u32[]{:S(2)}) collective-permute-start(bf16[216,512]{1,0:T(8,128)(2,1)S(1)} %get-tuple-element.56), channel_id=1, source_target_pairs={{0,12},{4,8},{8,4},{12,0},{1,13},{5,9},{9,5},{13,1},{2,14},{6,10},... | collective-permute-start | bytes 663560 | tf_op jit(solution)/shard_map/ppermute | solution.py:22
  14.0 10.8 %collective-permute-start = (bf16[16,512]{1,0:T(8,128)(2,1)S(1)}, bf16[16,512]{1,0:T(8,128)(2,1)S(1)}, u32[]{:S(2)}, u32[]{:S(2)}) collective-permute-start(bf16[16,512]{1,0:T(8,128)(2,1)S(1)} %get-tuple-element.43), channel_id=1, source_target_pairs={{0,4},{8,12},{4,0},{12,8},{1,5},{9,13},{5,1},{13,9},{2,6},{10,14},... | collective-permute-start | bytes 49160 | tf_op jit(solution)/shard_map/ppermute | solution.py:30
  14.9 9.9 %collective-permute-start.1 = (bf16[16,512]{1,0:T(8,128)(2,1)S(1)}, bf16[16,512]{1,0:T(8,128)(2,1)S(1)}, u32[]{:S(2)}, u32[]{:S(2)}) collective-permute-start(bf16[16,512]{1,0:T(8,128)(2,1)S(1)} %get-tuple-element.44), channel_id=1, source_target_pairs={{4,8},{8,4},{5,9},{9,5},{6,10},{10,6},{7,11},{11,7},{20,24},{24,20... | collective-permute-start | bytes 49160 | tf_op jit(solution)/shard_map/ppermute | solution.py:30
  24.9 3.8 %collective-permute-start.2 = (bf16[16,512]{1,0:T(8,128)(2,1)S(1)}, bf16[16,512]{1,0:T(8,128)(2,1)S(1)}, u32[]{:S(2)}, u32[]{:S(2)}) collective-permute-start(bf16[16,512]{1,0:T(8,128)(2,1)S(1)} %get-tuple-element.48), channel_id=1, source_target_pairs={{0,2},{2,0},{1,3},{3,1},{4,6},{6,4},{5,7},{7,5},{8,10},{10,8},{9,1... | collective-permute-start | bytes 49160 | tf_op jit(solution)/shard_map/ppermute | solution.py:30
  31.4 18.1 %copy-start.1 = (bf16[320,512]{1,0:T(8,128)(2,1)S(1)}, bf16[320,512]{1,0:T(8,128)(2,1)}, u32[]{:S(2)}) copy-start(bf16[320,512]{1,0:T(8,128)(2,1)} %weight_ref.1) | copy-start | bytes 983044
  31.4 12.7 %collective-permute-start.12 = (bf16[128,512]{1,0:T(8,128)(2,1)S(1)}, bf16[128,512]{1,0:T(8,128)(2,1)S(1)}, u32[]{:S(2)}, u32[]{:S(2)}) collective-permute-start(bf16[128,512]{1,0:T(8,128)(2,1)S(1)} %bitcast.11), channel_id=1, source_target_pairs={{0,4},{4,0},{8,12},{12,8},{1,5},{5,1},{9,13},{13,9},{2,6},{6,2},{1... | collective-permute-start | bytes 393224 | tf_op jit(solution)/shard_map/ppermute | solution.py:22
  39.1 10.0 %collective-permute-start.13 = (bf16[128,512]{1,0:T(8,128)(2,1)S(1)}, bf16[128,512]{1,0:T(8,128)(2,1)S(1)}, u32[]{:S(2)}, u32[]{:S(2)}) collective-permute-start(bf16[128,512]{1,0:T(8,128)(2,1)S(1)} %bitcast.12), channel_id=1, source_target_pairs={{0,8},{4,12},{8,0},{12,4},{1,9},{5,13},{9,1},{13,5},{2,10},{6,14},... | collective-permute-start | bytes 393224 | tf_op jit(solution)/shard_map/ppermute | solution.py:22
  40.2 8.9 %collective-permute-start.14 = (bf16[128,512]{1,0:T(8,128)(2,1)S(1)}, bf16[128,512]{1,0:T(8,128)(2,1)S(1)}, u32[]{:S(2)}, u32[]{:S(2)}) collective-permute-start(bf16[128,512]{1,0:T(8,128)(2,1)S(1)} %bitcast.13), channel_id=1, source_target_pairs={{0,12},{4,8},{8,4},{12,0},{1,13},{5,9},{9,5},{13,1},{2,14},{6,10},... | collective-permute-start | bytes 393224 | tf_op jit(solution)/shard_map/ppermute | solution.py:22
  43.1 8.5 %collective-permute-start.7 = (bf16[272,512]{1,0:T(8,128)(2,1)S(1)}, bf16[272,512]{1,0:T(8,128)(2,1)S(1)}, u32[]{:S(2)}, u32[]{:S(2)}) collective-permute-start(bf16[272,512]{1,0:T(8,128)(2,1)S(1)} %get-tuple-element.62), channel_id=1, source_target_pairs={{0,1},{1,0},{2,3},{3,2},{4,5},{5,4},{6,7},{7,6},{8,9},{9,8},{10,11... | collective-permute-start | bytes 835592 | tf_op jit(solution)/shard_map/ppermute | solution.py:22
  51.0 2.3 %collective-permute-start.18 = (bf16[160,576]{1,0:T(8,128)(2,1)S(1)}, bf16[160,576]{1,0:T(8,128)(2,1)S(1)}, u32[]{:S(2)}, u32[]{:S(2)}) collective-permute-start(bf16[160,576]{1,0:T(8,128)(2,1)S(1)} %get-tuple-element.78), channel_id=1, source_target_pairs={{0,1},{1,0},{2,3},{3,2},{4,5},{5,4},{6,7},{7,6},{8,9},{9,8},{10,11... | collective-permute-start | bytes 552968 | tf_op jit(solution)/shard_map/ppermute | solution.py:22
  51.1 3.1 %collective-permute-start.15 = (bf16[160,512]{1,0:T(8,128)(2,1)S(1)}, bf16[160,512]{1,0:T(8,128)(2,1)S(1)}, u32[]{:S(2)}, u32[]{:S(2)}) collective-permute-start(bf16[160,512]{1,0:T(8,128)(2,1)S(1)} %get-tuple-element.74), channel_id=1, source_target_pairs={{0,1},{1,0},{2,3},{3,2},{4,5},{5,4},{6,7},{7,6},{8,9},{9,8},{10,11... | collective-permute-start | bytes 491528 | tf_op jit(solution)/shard_map/ppermute | solution.py:22
  51.7 13.9 %collective-permute-start.8 = (bf16[144,512]{1,0:T(8,128)(2,1)S(1)}, bf16[144,512]{1,0:T(8,128)(2,1)S(1)}, u32[]{:S(2)}, u32[]{:S(2)}) collective-permute-start(bf16[144,512]{1,0:T(8,128)(2,1)S(1)} %get-tuple-element.64), channel_id=1, source_target_pairs={{0,2},{2,0},{1,3},{3,1},{4,6},{6,4},{5,7},{7,5},{8,10},{10,8},{9,1... | collective-permute-start | bytes 442376 | tf_op jit(solution)/shard_map/ppermute | solution.py:22
  53.3 9.5 %collective-permute-start.19 = (bf16[160,576]{1,0:T(8,128)(2,1)S(1)}, bf16[160,576]{1,0:T(8,128)(2,1)S(1)}, u32[]{:S(2)}, u32[]{:S(2)}) collective-permute-start(bf16[160,576]{1,0:T(8,128)(2,1)S(1)} %add_convert_fusion.1), channel_id=1, source_target_pairs={{0,2},{2,0},{1,3},{3,1},{4,6},{6,4},{5,7},{7,5},{8,10},{10,8},{9,1... | collective-permute-start | bytes 552968 | tf_op jit(solution)/shard_map/ppermute | solution.py:22
  54.2 11.3 %collective-permute-start.16 = (bf16[160,512]{1,0:T(8,128)(2,1)S(1)}, bf16[160,512]{1,0:T(8,128)(2,1)S(1)}, u32[]{:S(2)}, u32[]{:S(2)}) collective-permute-start(bf16[160,512]{1,0:T(8,128)(2,1)S(1)} %add_convert_fusion.3), channel_id=1, source_target_pairs={{0,2},{2,0},{1,3},{3,1},{4,6},{6,4},{5,7},{7,5},{8,10},{10,8},{9,1... | collective-permute-start | bytes 491528 | tf_op jit(solution)/shard_map/ppermute | solution.py:22
  62.9 13.5 %collective-permute-start.20 = (bf16[160,576]{1,0:T(8,128)(2,1)S(1)}, bf16[160,576]{1,0:T(8,128)(2,1)S(1)}, u32[]{:S(2)}, u32[]{:S(2)}) collective-permute-start(bf16[160,576]{1,0:T(8,128)(2,1)S(1)} %add_convert_fusion.total_ref), channel_id=1, source_target_pairs={{0,1},{1,0},{2,3},{3,2},{4,5},{5,4},{6,7},{7,6},{8,9},{9,8},{10,11... | collective-permute-start | bytes 552968 | tf_op jit(solution)/shard_map/ppermute | solution.py:22
  65.6 10.0 %collective-permute-start.17 = (bf16[160,512]{1,0:T(8,128)(2,1)S(1)}, bf16[160,512]{1,0:T(8,128)(2,1)S(1)}, u32[]{:S(2)}, u32[]{:S(2)}) collective-permute-start(bf16[160,512]{1,0:T(8,128)(2,1)S(1)} %add_convert_fusion.2.total_ref), channel_id=1, source_target_pairs={{0,1},{1,0},{2,3},{3,2},{4,5},{5,4},{6,7},{7,6},{8,9},{9,8},{10,11... | collective-permute-start | bytes 491528 | tf_op jit(solution)/shard_map/ppermute | solution.py:22
  65.7 4.5 %collective-permute-start.9 = (bf16[48,512]{1,0:T(8,128)(2,1)S(1)}, bf16[48,512]{1,0:T(8,128)(2,1)S(1)}, u32[]{:S(2)}, u32[]{:S(2)}) collective-permute-start(bf16[48,512]{1,0:T(8,128)(2,1)S(1)} %get-tuple-element.66), channel_id=1, source_target_pairs={{0,4},{4,0},{8,12},{12,8},{1,5},{5,1},{9,13},{13,9},{2,6},{6,2},{1... | collective-permute-start | bytes 147464 | tf_op jit(solution)/shard_map/ppermute | solution.py:22
  67.7 7.2 %collective-permute-start.10 = (bf16[48,512]{1,0:T(8,128)(2,1)S(1)}, bf16[48,512]{1,0:T(8,128)(2,1)S(1)}, u32[]{:S(2)}, u32[]{:S(2)}) collective-permute-start(bf16[48,512]{1,0:T(8,128)(2,1)S(1)} %get-tuple-element.67), channel_id=1, source_target_pairs={{0,8},{4,12},{8,0},{12,4},{1,9},{5,13},{9,1},{13,5},{2,10},{6,14},... | collective-permute-start | bytes 147464 | tf_op jit(solution)/shard_map/ppermute | solution.py:22
  68.8 6.1 %collective-permute-start.11 = (bf16[48,512]{1,0:T(8,128)(2,1)S(1)}, bf16[48,512]{1,0:T(8,128)(2,1)S(1)}, u32[]{:S(2)}, u32[]{:S(2)}) collective-permute-start(bf16[48,512]{1,0:T(8,128)(2,1)S(1)} %get-tuple-element.68), channel_id=1, source_target_pairs={{0,12},{4,8},{8,4},{12,0},{1,13},{5,9},{9,5},{13,1},{2,14},{6,10},... | collective-permute-start | bytes 147464 | tf_op jit(solution)/shard_map/ppermute | solution.py:22

commit v2 on v1

--- a/solution.py
+++ b/solution.py
@@ -38,22 +38,27 @@
 
 
 def full_sum(keep, send):
-    rows, lanes = keep.shape
     total = (keep.astype(F32) + swap(send, "rep", 1).astype(F32)).astype(BF16)
     step = 1
     while step < lax.axis_size("col"):
         total = (total.astype(F32) + swap(total, "col", step).astype(F32)).astype(BF16)
         step *= 2
     remote = swap(total, "rep", 1)
-    (whole,) = call(join_kernel, [((2 * rows, lanes), F32)], [total, remote])
-    return whole
-
-
-def join_kernel(total_ref, remote_ref, out_ref):
-    rows = total_ref.shape[0]
+    return total, remote
+
+
+def join_kernel(parts, *refs):
+    in_refs, (in_out, group_out) = refs[:-2], refs[-2:]
+    rows = in_refs[0].shape[0]
     rep = lax.axis_index("rep")
-    out_ref[pl.ds(pl.multiple_of(rep * rows, 16), rows), :] = total_ref[...].astype(F32)
-    out_ref[pl.ds(pl.multiple_of((1 - rep) * rows, 16), rows), :] = remote_ref[...].astype(F32)
+    for i in range(parts):
+        for ref, which in ((in_refs[2 * i], rep), (in_refs[2 * i + 1], 1 - rep)):
+            here = pl.ds(pl.multiple_of(which * rows, 16), rows)
+            wide = in_refs[0].shape[1] if i < parts - 1 else in_out.shape[1] - i * in_refs[0].shape[1]
+            at = in_out.shape[1] - wide if i == parts - 1 else i * wide
+            in_out[here, at : at + wide] = ref[:, :wide].astype(F32)
+            if i == parts - 1:
+                group_out[here, :] = ref[:, wide : wide + group_out.shape[1]].astype(F32)
 
 
 def silu_slope(value):
@@ -168,8 +173,9 @@
     return width // 2 + (1 if cols == 2 else 2)
 
 
-def features_kernel(tiles, pairs, count_ref, field_ref, kernel_ref, weight_ref, *refs):
-    halo_refs, out_refs, store = refs[: -tiles - 1], refs[-tiles - 1 : -1], refs[-1]
+def features_kernel(tiles, pairs, parts, count_ref, field_ref, kernel_ref, weight_ref, *refs):
+    outs = tiles * parts
+    halo_refs, out_refs, store = refs[: -outs - 1], refs[-outs - 1 : -1], refs[-1]
     slots, height, _ = field_ref.shape
     main = ROWS * pairs
     col = lax.axis_index("col")
@@ -204,9 +210,12 @@
     if slots % 2:
         last = values(slots - 1)
         put(interleave(last, jnp.zeros_like(last)), slots // 2)
-    for step, out in enumerate(out_refs):
+    for step in range(tiles):
         band = lax.bitwise_xor(lax.axis_index("tile"), step)
-        out[...] = jnp.dot(store[band], weight_ref[...], preferred_element_type=F32).astype(BF16)
+        term = jnp.dot(store[band], weight_ref[...], preferred_element_type=F32).astype(BF16)
+        for part in range(parts):
+            out = out_refs[part * tiles + step]
+            out[...] = term[:, part * out.shape[1] : (part + 1) * out.shape[1]]
 
 
 def backward_inputs_kernel(count_ref, field_ref, kernel_ref, *refs):
@@ -284,15 +293,18 @@
 TAPS = [(a, b) for a in range(3) for b in range(3)]
 
 
-def middle_kernel(tiles, grad_ref, depth_ref, *refs):
+def middle_kernel(tiles, lane, grad_ref, depth_ref, *refs):
     term_refs, (act_grad_ref, hidden_ref, act, inner) = refs[:tiles], refs[tiles:]
-    width, hidden = grad_ref.shape[0] - 2, grad_ref.shape[2]
+    width = grad_ref.shape[0] - 2
     cols = lax.axis_size("col")
     pairs = sent_pairs(width, cols)
     main = ROWS * pairs
     before_block = jnp.where(lax.axis_index("col") == 0, 2, 0) if cols == 2 else 0
-    chunks = [(n, slice(n * LANES, (n + 1) * LANES)) for n in range(hidden // LANES)]
-    for n, here in chunks:
+    chunks = [
+        (n, slice(n * LANES, (n + 1) * LANES), slice(lane + n * LANES, lane + (n + 1) * LANES))
+        for n in range(act.shape[0])
+    ]
+    for n, here, _ in chunks:
         total = tree_sum([ref[:, here].astype(F32) for ref in term_refs]).astype(BF16).astype(F32)
         for p in range(pairs):
             for half in range(2):
@@ -307,14 +319,14 @@
                 act[n, lax.rem(before_block + width + 2, width + 4) + half] = jnp.zeros(act.shape[2:], F32)
 
     def forward(column, carry):
-        for n, here in chunks:
+        for n, here, whole in chunks:
             terms = [
-                depth_ref[3 * a + b : 3 * a + b + 1, here] * act[n, column + b, a : a + ROWS + 2, :] for a, b in TAPS
+                depth_ref[3 * a + b : 3 * a + b + 1, whole] * act[n, column + b, a : a + ROWS + 2, :] for a, b in TAPS
             ]
             before = tree_sum(terms)
             sig = 1.0 / (1.0 + jnp.exp(-before))
             slope = sig * (1.0 + before * (1.0 - sig))
-            grad = grad_ref[column, 0 : ROWS + 2, here] * slope
+            grad = grad_ref[column, 0 : ROWS + 2, whole] * slope
             inner[n, column, 0 : ROWS + 2, :] = grad.astype(BF16).astype(F32)
             hidden_ref[column, :, here] = (before * sig)[1 : ROWS + 1]
         return carry
@@ -323,9 +335,9 @@
 
     def backward(column, carry):
         place = lax.shift_right_logical(column, 1) + (column & 1) * (width // 2)
-        for n, here in chunks:
+        for n, here, whole in chunks:
             terms = [
-                depth_ref[3 * a + b : 3 * a + b + 1, here] * inner[n, column + 2 - b, 2 - a : 2 - a + ROWS, :]
+                depth_ref[3 * a + b : 3 * a + b + 1, whole] * inner[n, column + 2 - b, 2 - a : 2 - a + ROWS, :]
                 for a, b in TAPS
             ]
             act_grad_ref[place, :, here] = tree_sum(terms).astype(BF16)
@@ -334,15 +346,20 @@
     lax.fori_loop(0, width, backward, 0)
 
 
-def finish_kernel(hidden_ref, upstream_ref, mix_ref, act, inner, adjusted_ref, keep_ref, send_ref, held):
-    chunks, columns = act.shape[:2]
+def finish_kernel(parts, upstream_ref, mix_ref, *refs):
+    hidden_refs, acts, inners = (refs[parts * i : parts * (i + 1)] for i in range(3))
+    adjusted_ref, keep_ref, send_ref, held = refs[3 * parts :]
+    own, columns = acts[0].shape[:2]
+    chunks = own * parts
     width = columns - 4
     cells, hidden = upstream_ref.shape
     target = lax.broadcasted_iota(jnp.int32, (cells, cells), 0)
     source = lax.broadcasted_iota(jnp.int32, (cells, cells), 1)
     pick = (source & (ROWS - 1)) * width + lax.shift_right_logical(source, 3) == target
     pick = jnp.where(pick, 1.0, 0.0).astype(BF16)
-    by_column = hidden_ref[1 : width + 1].reshape(cells, hidden).astype(BF16)
+    by_column = jnp.concatenate(
+        [ref[1 : width + 1].reshape(cells, -1).astype(BF16) for ref in hidden_refs], axis=1
+    )
     value = jnp.dot(pick, by_column, preferred_element_type=F32).astype(BF16)
     adjusted_ref[...] = lax.dot_general(
         value, mix_ref[...], (((1,), (1,)), ((), ())), preferred_element_type=F32
@@ -354,9 +371,9 @@
     def add(column, sums):
         new = []
         for n in range(chunks):
-            own = inner[n, column + 1, 1 : 1 + ROWS, :]
+            act, grad = acts[n // own], inners[n // own][n % own, column + 1, 1 : 1 + ROWS, :]
             for t, (a, b) in enumerate(TAPS):
-                new.append(sums[n * 9 + t] + act[n, column + 1 + b, 1 + a : 1 + a + ROWS, :] * own)
+                new.append(sums[n * 9 + t] + act[n % own, column + 1 + b, 1 + a : 1 + a + ROWS, :] * grad)
         return tuple(new)
 
     zero = jnp.zeros((ROWS, LANES), F32)
@@ -417,12 +434,16 @@
         out[...] = jnp.concatenate([ends_of[0], edge[...].astype(F32), ends_of[1], blank], axis=0).astype(BF16)
 
 
-def in_gradient_kernel(tiles, own_ref, *refs):
-    grad_refs, (keep, send, whole, held) = refs[:tiles], refs[tiles:]
+def by_band(grad_refs, whole):
     cells = grad_refs[0].shape[0]
     for step, ref in enumerate(grad_refs):
         start = pl.multiple_of(lax.bitwise_xor(lax.axis_index("tile"), step) * cells, 16)
         whole[pl.ds(start, cells), :] = ref[...]
+
+
+def in_gradient_kernel(tiles, own_ref, *refs):
+    grad_refs, (keep, send, whole, held) = refs[:tiles], refs[tiles:]
+    by_band(grad_refs, whole)
     term = lax.dot_general(own_ref[...], whole[...], (((0,), (0,)), ((), ())), preferred_element_type=F32)
     half = keep.shape[0]
     rep = lax.axis_index("rep")
@@ -431,13 +452,27 @@
     send[...] = held[pl.ds(pl.multiple_of((1 - rep) * half, 16), half), :]
 
 
-def group_gradient_kernel(tiles, rows_ref, weight_ref, patch_ref, group_keep, group_send, group_term):
+def group_gradient_kernel(tiles, parts, own_ref, weight_ref, patch_ref, *refs):
+    whole_refs, grad_refs = refs[: parts - 1], refs[parts - 1 : parts - 1 + tiles]
+    group_keep, group_send, last, group_term = refs[parts - 1 + tiles :]
     slots, lanes = patch_ref.shape[0], 6 * LANES
     channels = LANES // 2
-    rows = rows_ref[...]
+    by_band(grad_refs, last)
+    rows = last[...]
+    wide = rows.shape[1]
     cells = rows.shape[0] // tiles
     rep = lax.axis_index("rep")
-    feature_grad = lax.dot_general(rows, weight_ref[...], (((1,), (1,)), ((), ())), preferred_element_type=F32)
+    term = lax.dot_general(own_ref[...], rows, (((0,), (0,)), ((), ())), preferred_element_type=F32)
+    group_term[:, :wide] = term[: slots * channels].astype(BF16)
+    feature_grad = None
+    for i, ref in enumerate((*whole_refs, last)):
+        term = lax.dot_general(
+            ref[...],
+            weight_ref[:, i * wide : (i + 1) * wide],
+            (((1,), (1,)), ((), ())),
+            preferred_element_type=F32,
+        )
+        feature_grad = term if feature_grad is None else feature_grad + term
     feature_grad = feature_grad.astype(BF16).astype(F32)
     blank = slots * channels % LANES
     if blank:
@@ -466,7 +501,10 @@
             high = jnp.concatenate(
                 [term[channels:, quarter * a + channels : quarter * (a + 1)] for a in range(3)], axis=1
             )
-            group_term[channels * k : channels * (k + 1), :] = (low + high).astype(BF16)
+            blank = jnp.zeros((channels, -9 * channels % LANES), F32)
+            group_term[channels * k : channels * (k + 1), wide:] = jnp.concatenate(
+                [low + high, blank], axis=1
+            ).astype(BF16)
     half = group_keep.shape[0]
     group_keep[...] = group_term[pl.ds(pl.multiple_of(rep * half, 16), half), :]
     group_send[...] = group_term[pl.ds(pl.multiple_of((1 - rep) * half, 16), half), :]
@@ -507,6 +545,8 @@
     assert height == ROWS * tiles and 2 * channels == LANES
     lane_tiles = -(-slots // 2)
     rows = hidden // (tiles * cols * reps)
+    parts = 2
+    wide = hidden // parts
 
     sides, ends = (1 if count == 2 else 2 for count in (cols, tiles))
     field, kernel, weight, upstream, *edges = call(
@@ -530,13 +570,16 @@
     halos = with_neighbours(edges[:sides], "col")
     rows_near = with_neighbours(edges[2 * sides :], "tile")
     sent = call(
-        functools.partial(features_kernel, tiles, pairs),
-        [((3 * ROWS * pairs, hidden), BF16)] * tiles,
+        functools.partial(features_kernel, tiles, pairs, parts),
+        [((3 * ROWS * pairs, wide), BF16)] * (tiles * parts),
         [member_counts, field, kernel, weight, *halos],
         [pltpu.VMEM((tiles, 3 * ROWS * pairs, lane_tiles * LANES), BF16)],
         flops=1 << 28,
     )
-    terms = [swap(sent[step], "tile", step) if step else sent[0] for step in range(tiles)]
+    terms = [
+        [swap(term, "tile", step) if step else term for step, term in enumerate(sent[h * tiles : (h + 1) * tiles])]
+        for h in range(parts)
+    ]
 
     top, bottom, *columns = call(
         functools.partial(corner_kernel, ends, sides),
@@ -562,24 +605,27 @@
         flops=1 << 28,
     )
 
-    act_grad, hidden_act, act, inner = call(
-        functools.partial(middle_kernel, tiles),
-        [
-            ((width, ROWS, hidden), BF16),
-            ((width + 2, ROWS, hidden), F32),
-            ((hidden // LANES, width + 4, 16, LANES), F32),
-            ((hidden // LANES, width + 2, 16, LANES), F32),
-        ],
-        [hidden_grad, depth_weight, *terms],
-    )
-    act_grad = act_grad.reshape(cells, hidden)
-    grads = [swap(act_grad, "tile", step) if step else act_grad for step in range(tiles)]
+    middles, grads = [], []
+    for h in range(parts):
+        act_grad, *rest = call(
+            functools.partial(middle_kernel, tiles, h * wide),
+            [
+                ((width, ROWS, wide), BF16),
+                ((width + 2, ROWS, wide), F32),
+                ((wide // LANES, width + 4, 16, LANES), F32),
+                ((wide // LANES, width + 2, 16, LANES), F32),
+            ],
+            [hidden_grad, depth_weight, *terms[h]],
+        )
+        act_grad = act_grad.reshape(cells, wide)
+        grads.append([swap(act_grad, "tile", step) if step else act_grad for step in range(tiles)])
+        middles.append(rest)
 
     part = ((tiles * cols * rows + 16, hidden), BF16)
     adjusted, keep, send = call(
-        finish_kernel,
+        functools.partial(finish_kernel, parts),
         [((cells, hidden), BF16), part, part],
-        [hidden_act, flat_upstream, mix_weight, act, inner],
+        [flat_upstream, mix_weight, *(middles[h][i] for i in range(3) for h in range(parts))],
         [pltpu.VMEM((hidden, hidden), BF16)],
     )
     arrived = [keep, swap(send, "rep", 1)]
@@ -599,22 +645,29 @@
     )
 
     half = slots * channels // 2
-    in_keep, in_send, whole = call(
-        functools.partial(in_gradient_kernel, tiles),
-        [((half, hidden), BF16), ((half, hidden), BF16), ((cells * tiles, hidden), BF16)],
-        [own_features, *grads],
-        [pltpu.VMEM((2 * half, hidden), BF16)],
-    )
-    group_keep, group_send = call(
-        functools.partial(group_gradient_kernel, tiles),
-        [((half, 9 * channels), BF16), ((half, 9 * channels), BF16)],
-        [whole, mixing_input_weight, patch],
-        [pltpu.VMEM((2 * half, 9 * channels), BF16)],
+    joined, wholes = [], []
+    for h in range(parts - 1):
+        keep, send, whole = call(
+            functools.partial(in_gradient_kernel, tiles),
+            [((half, wide), BF16), ((half, wide), BF16), ((cells * tiles, wide), BF16)],
+            [own_features, *grads[h]],
+            [pltpu.VMEM((2 * half, wide), BF16)],
+        )
+        wholes.append(whole)
+        joined += full_sum(keep, send)
+    lanes = wide + 9 * channels + -9 * channels % LANES
+    keep, send = call(
+        functools.partial(group_gradient_kernel, tiles, parts),
+        [((half, lanes), BF16), ((half, lanes), BF16)],
+        [own_features, mixing_input_weight, patch, *wholes, *grads[-1]],
+        [pltpu.VMEM((cells * tiles, wide), BF16), pltpu.VMEM((2 * half, lanes), BF16)],
         flops=1 << 28,
     )
-    in_grad = full_sum(in_keep, in_send)
-    group_grad = full_sum(group_keep, group_send).reshape(slots, channels, -1)
-    group_grad = jnp.swapaxes(group_grad, 1, 2)
+    joined += full_sum(keep, send)
+    in_grad, group_grad = call(
+        functools.partial(join_kernel, parts), [((2 * half, hidden), F32), ((2 * half, 9 * channels), F32)], joined
+    )
+    group_grad = jnp.swapaxes(group_grad.reshape(slots, channels, -1), 1, 2)
     return (adjusted.reshape(cotangent.shape), mix_grad, depth_grad, in_grad, group_grad)
 
 

time: 77.6 us -> 78.3 us (level)
  starting transfers between devices: 30 us -> 42 us
  waiting for transfers between devices: 33.6 us -> 22.3 us
    ppermute x17 -> x23, starting transfers between devices: 23.8 us -> 35.8 us  [swap(): lax.ppermute(value, axis, [(i, i ^ step) for i in range(lax.axis_size(axi...]
    ppermute x4, waiting for transfers between devices: 13.3 us -> 5.01 us  [with_neighbours(): lax.ppermute(value, axis, pairs + [(b, a) for a, b in pairs])]
    ppermute x17 -> x23, waiting for transfers between devices: 20.3 us -> 17.3 us  [swap(): lax.ppermute(value, axis, [(i, i ^ step) for i in range(lax.axis_size(axi...]
  transfers between devices with their start and end apart: 21 -> 27, of which waited for: 8 -> 11; matrix products, arithmetic and copies ran while one was open for 0% -> 0% of each run, Pallas kernels for 9% -> 8%
where the time goes in v2:
time: 78.3 us; the launch traced here: 78.1 us
  starting transfers between devices  42 us (54%)
  waiting for transfers between devices  22.3 us (28%)
  Pallas kernels  12.1 us (15%)
  between operations  1.49 us (2%)
    ppermute x23, starting transfers between devices, swap(): lax.ppermute(value, axis, [(i, i ^ step) for i in range(lax.axis_size(axi...  35.8 us
    ppermute x23, waiting for transfers between devices, swap(): lax.ppermute(value, axis, [(i, i ^ step) for i in range(lax.axis_size(axi...  17.3 us
    pallas_call x14, Pallas kernels, call(): pl.pallas_call(kernel, out_shape=shapes, in_specs=specs or [SMEM if jnp.i...  12.1 us
    ppermute x4, starting transfers between devices, with_neighbours(): lax.ppermute(value, axis, pairs + [(b, a) for a, b in pairs])  6.19 us
    ppermute x4, waiting for transfers between devices, with_neighbours(): lax.ppermute(value, axis, pairs + [(b, a) for a, b in pairs])  5.01 us
  transfers between devices with their start and end apart: 27, of which 11 were waited for; matrix products, arithmetic and copies ran while one was open for 0% of the time, Pallas kernels for 8%

profile of v2, /device:TPU:0, one launch (start us, length us, event | category | flops | bytes accessed | tf_op | source)
XLA Modules:
  0.0 78.1 jit_solution(17559068522576578644)
XLA Ops:
  0.7 1.4 %shard_map.110 = (bf16[5,32,1024]{2,1,0:T(8,128)(2,1)S(1)}, bf16[5,128,768]{2,1,0:T(8,128)(2,1)S(1)}, bf16[384,512]{1,0:T(8,128)(2,1)S(1)}, bf16[8,16,512]{2,1,0...) custom-call(bf16[5,32,1024]{2,1,0:T(8,128)(2,1)} %bitcast.21, ...), custom_call_target="tpu_custom_call" | custom-call | flops 16777216 | bytes 3112960 | tf_op jit(solution)/shard_map/pallas_call | solution.py:517
  2.1 3.0 %collective-permute-start.3 = (bf16[5,32,256]{2,1,0:T(8,128)(2,1)S(1)}, bf16[5,32,256]{2,1,0:T(8,128)(2,1)S(1)}, u32[]{:S(2)}, u32[]{:S(2)}) collective-permute-start(bf16[5,32,256]{2,1,0:T(8,128)(2,1)S(1)} %get-tuple-element.62), channel_id=1, source_target_pairs={{0,2},{2,0},{1,3},{3,1},{4,6},{6,4},{5,7},{7,5},{8,10},{10,8},{9,1... | collective-permute-start | bytes 245768 | tf_op jit(solution)/shard_map/ppermute | solution.py:30
  5.8 1.8 %collective-permute-done.3.refs_0_ = bf16[5,32,256]{2,1,0:T(8,128)(2,1)S(1)} collective-permute-done((bf16[5,32,256]{2,1,0:T(8,128)(2,1)S(1)}, bf16[5,32,256]{2,1,0:T(8,128)(2,1)S(1)}, u32[]{:S(2)}, u32[]{:S(2)}) %collective-permute-start.3) | collective-permute-done | bytes 81952 | tf_op jit(solution)/shard_map/ppermute | solution.py:30
  7.6 1.7 %shard_map.113 = (bf16[216,256]{1,0:T(8,128)(2,1)S(1)}, bf16[216,256]{1,0:T(8,128)(2,1)S(1)}, bf16[216,256]{1,0:T(8,128)(2,1)S(1)}, bf16[216,256]{1,0:T(8,128)(2...) custom-call(s32[1]{0:T(128)S(6)} %copy.12.count_ref, ...), custom_call_target="tpu_custom_call" | custom-call | flops 268435456 | bytes 2670596 | tf_op jit(solution)/shard_map/pallas_call | solution.py:517
  9.3 2.2 %collective-permute-start.4 = (bf16[216,256]{1,0:T(8,128)(2,1)S(1)}, bf16[216,256]{1,0:T(8,128)(2,1)S(1)}, u32[]{:S(2)}, u32[]{:S(2)}) collective-permute-start(bf16[216,256]{1,0:T(8,128)(2,1)S(1)} %get-tuple-element.64), channel_id=1, source_target_pairs={{0,4},{4,0},{8,12},{12,8},{1,5},{5,1},{9,13},{13,9},{2,6},{6,2},{1... | collective-permute-start | bytes 331784 | tf_op jit(solution)/shard_map/ppermute | solution.py:22
  11.4 2.6 %collective-permute-start.5 = (bf16[216,256]{1,0:T(8,128)(2,1)S(1)}, bf16[216,256]{1,0:T(8,128)(2,1)S(1)}, u32[]{:S(2)}, u32[]{:S(2)}) collective-permute-start(bf16[216,256]{1,0:T(8,128)(2,1)S(1)} %get-tuple-element.65), channel_id=1, source_target_pairs={{0,8},{4,12},{8,0},{12,4},{1,9},{5,13},{9,1},{13,5},{2,10},{6,14},... | collective-permute-start | bytes 331784 | tf_op jit(solution)/shard_map/ppermute | solution.py:22
  15.6 3.2 %collective-permute-done.refs_0_ = bf16[16,512]{1,0:T(8,128)(2,1)S(1)} collective-permute-done((bf16[16,512]{1,0:T(8,128)(2,1)S(1)}, bf16[16,512]{1,0:T(8,128)(2,1)S(1)}, u32[]{:S(2)}, u32[]{:S(2)}) %collective-permute-start) | collective-permute-done | bytes 16416 | tf_op jit(solution)/shard_map/ppermute | solution.py:30
  18.8 1.6 %collective-permute-start.2 = (bf16[16,512]{1,0:T(8,128)(2,1)S(1)}, bf16[16,512]{1,0:T(8,128)(2,1)S(1)}, u32[]{:S(2)}, u32[]{:S(2)}) collective-permute-start(bf16[16,512]{1,0:T(8,128)(2,1)S(1)} %get-tuple-element.58), channel_id=1, source_target_pairs={{0,2},{2,0},{1,3},{3,1},{4,6},{6,4},{5,7},{7,5},{8,10},{10,8},{9,1... | collective-permute-start | bytes 49160 | tf_op jit(solution)/shard_map/ppermute | solution.py:30
  20.4 4.9 %collective-permute-start.7 = (bf16[216,256]{1,0:T(8,128)(2,1)S(1)}, bf16[216,256]{1,0:T(8,128)(2,1)S(1)}, u32[]{:S(2)}, u32[]{:S(2)}) collective-permute-start(bf16[216,256]{1,0:T(8,128)(2,1)S(1)} %get-tuple-element.69), channel_id=1, source_target_pairs={{0,4},{4,0},{8,12},{12,8},{1,5},{5,1},{9,13},{13,9},{2,6},{6,2},{1... | collective-permute-start | bytes 331784 | tf_op jit(solution)/shard_map/ppermute | solution.py:22
  25.3 3.3 %collective-permute-start.8 = (bf16[216,256]{1,0:T(8,128)(2,1)S(1)}, bf16[216,256]{1,0:T(8,128)(2,1)S(1)}, u32[]{:S(2)}, u32[]{:S(2)}) collective-permute-start(bf16[216,256]{1,0:T(8,128)(2,1)S(1)} %get-tuple-element.70), channel_id=1, source_target_pairs={{0,8},{4,12},{8,0},{12,4},{1,9},{5,13},{9,1},{13,5},{2,10},{6,14},... | collective-permute-start | bytes 331784 | tf_op jit(solution)/shard_map/ppermute | solution.py:22
  28.6 1.4 %collective-permute-start.9 = (bf16[216,256]{1,0:T(8,128)(2,1)S(1)}, bf16[216,256]{1,0:T(8,128)(2,1)S(1)}, u32[]{:S(2)}, u32[]{:S(2)}) collective-permute-start(bf16[216,256]{1,0:T(8,128)(2,1)S(1)} %get-tuple-element.71), channel_id=1, source_target_pairs={{0,12},{4,8},{8,4},{12,0},{1,13},{5,9},{9,5},{13,1},{2,14},{6,10},... | collective-permute-start | bytes 331784 | tf_op jit(solution)/shard_map/ppermute | solution.py:22
  31.6 3.0 %collective-permute-start.16 = (bf16[128,256]{1,0:T(8,128)(2,1)S(1)}, bf16[128,256]{1,0:T(8,128)(2,1)S(1)}, u32[]{:S(2)}, u32[]{:S(2)}) collective-permute-start(bf16[128,256]{1,0:T(8,128)(2,1)S(1)} %bitcast.17), channel_id=1, source_target_pairs={{0,8},{4,12},{8,0},{12,4},{1,9},{5,13},{9,1},{13,5},{2,10},{6,14},... | collective-permute-start | bytes 196616 | tf_op jit(solution)/shard_map/ppermute | solution.py:22
  34.6 1.4 %collective-permute-start.17 = (bf16[128,256]{1,0:T(8,128)(2,1)S(1)}, bf16[128,256]{1,0:T(8,128)(2,1)S(1)}, u32[]{:S(2)}, u32[]{:S(2)}) collective-permute-start(bf16[128,256]{1,0:T(8,128)(2,1)S(1)} %bitcast.18), channel_id=1, source_target_pairs={{0,12},{4,8},{8,4},{12,0},{1,13},{5,9},{9,5},{13,1},{2,14},{6,10},... | collective-permute-start | bytes 196616 | tf_op jit(solution)/shard_map/ppermute | solution.py:22
  35.9 1.2 %collective-permute-done.8.refs_2_ = bf16[216,256]{1,0:T(8,128)(2,1)S(1)} collective-permute-done((bf16[216,256]{1,0:T(8,128)(2,1)S(1)}, bf16[216,256]{1,0:T(8,128)(2,1)S(1)}, u32[]{:S(2)}, u32[]{:S(2)}) %collective-permute-start.8) | collective-permute-done | bytes 110624 | tf_op jit(solution)/shard_map/ppermute | solution.py:22
  38.2 5.8 %collective-permute-start.21 = (bf16[128,256]{1,0:T(8,128)(2,1)S(1)}, bf16[128,256]{1,0:T(8,128)(2,1)S(1)}, u32[]{:S(2)}, u32[]{:S(2)}) collective-permute-start(bf16[128,256]{1,0:T(8,128)(2,1)S(1)} %bitcast.12), channel_id=1, source_target_pairs={{0,4},{4,0},{8,12},{12,8},{1,5},{5,1},{9,13},{13,9},{2,6},{6,2},{1... | collective-permute-start | bytes 196616 | tf_op jit(solution)/shard_map/ppermute | solution.py:22
  44.8 1.7 %collective-permute-start.23 = (bf16[128,256]{1,0:T(8,128)(2,1)S(1)}, bf16[128,256]{1,0:T(8,128)(2,1)S(1)}, u32[]{:S(2)}, u32[]{:S(2)}) collective-permute-start(bf16[128,256]{1,0:T(8,128)(2,1)S(1)} %bitcast.14), channel_id=1, source_target_pairs={{0,12},{4,8},{8,4},{12,0},{1,13},{5,9},{9,5},{13,1},{2,14},{6,10},... | collective-permute-start | bytes 196616 | tf_op jit(solution)/shard_map/ppermute | solution.py:22
  46.4 1.1 %shard_map.120 = (bf16[5,256,896]{2,1,0:T(8,128)(2,1)S(1)}, bf16[512,384]{1,0:T(8,128)(2,1)S(1)}) custom-call(s32[1]{0:T(128)S(6)} %copy.12.count_ref, bf16[5,32,1024]{2,1,0:T(8,128)(2,1)S(1)} %get-tuple-element.59.field_ref, bf16[5,128,768]{2,1,0:T(8,128)(2,1)S(1)} %get-tuple-element.60.kernel_ref, bf16[5,32,256]{2,1,0:T(8,128)(2,1)S(1)} %collective-permute-done.3.refs_0_), custom_call_target="tpu_custom_call" | custom-call | flops 268435456 | bytes 4079620 | tf_op jit(solution)/shard_map/pallas_call | solution.py:517
  47.8 1.9 %collective-permute-done.22.refs_3_ = bf16[128,256]{1,0:T(8,128)(2,1)S(1)} collective-permute-done((bf16[128,256]{1,0:T(8,128)(2,1)S(1)}, bf16[128,256]{1,0:T(8,128)(2,1)S(1)}, u32[]{:S(2)}, u32[]{:S(2)}) %collective-permute-start.22) | collective-permute-done | bytes 65568 | tf_op jit(solution)/shard_map/ppermute | solution.py:22
  49.8 1.1 %collective-permute-done.23.refs_4_ = bf16[128,256]{1,0:T(8,128)(2,1)S(1)} collective-permute-done((bf16[128,256]{1,0:T(8,128)(2,1)S(1)}, bf16[128,256]{1,0:T(8,128)(2,1)S(1)}, u32[]{:S(2)}, u32[]{:S(2)}) %collective-permute-start.23) | collective-permute-done | bytes 65568 | tf_op jit(solution)/shard_map/ppermute | solution.py:22
  50.9 1.6 %shard_map.122 = (bf16[160,896]{1,0:T(8,128)(2,1)S(1)}, bf16[160,896]{1,0:T(8,128)(2,1)S(1)}) custom-call(bf16[512,384]{1,0:T(8,128)(2,1)S(1)} %get-tuple-element.88.own_ref, bf16[320,512]{1,0:T(8,128)(2,1)S(1)} %copy-done.1, bf16[5,256,896]{2,1,0:T(8,128)(2,1)S(1)} %get-tuple-element.92.patch_ref, bf16[512,256]{1,0:T(8,128)(2,1)S(1)} %get-tuple-element.93.refs_0_, ...), custom_call_target="tpu_custom_call" | custom-call | flops 268435456 | bytes 4112384 | tf_op jit(solution)/shard_map/pallas_call | solution.py:517
  53.1 1.1 %collective-permute-done.24 = bf16[160,896]{1,0:T(8,128)(2,1)S(1)} collective-permute-done((bf16[160,896]{1,0:T(8,128)(2,1)S(1)}, bf16[160,896]{1,0:T(8,128)(2,1)S(1)}, u32[]{:S(2)}, u32[]{:S(2)}) %collective-permute-start.24) | collective-permute-done | bytes 286752 | tf_op jit(solution)/shard_map/ppermute | solution.py:22
  54.7 1.5 %shard_map.116 = (bf16[128,512]{1,0:T(8,128)(2,1)}, bf16[272,512]{1,0:T(8,128)(2,1)S(1)}, bf16[272,512]{1,0:T(8,128)(2,1)S(1)}) custom-call(bf16[128,512]{1,0:T(8,128)(2,1)S(1)} %bitcast.11, bf16[512,512]{1,0:T(8,128)(2,1)S(1)} %copy-done, f32[18,8,256]{2,1,0:T(8,128)S(1)} %get-tuple-element.67.refs_0_, f32[18,8,256]{2,1,0:T(8,128)S(1)} %get-tuple-element.72.refs_1_, ...), custom_call_target="tpu_custom_call" | custom-call | flops 16777216 | bytes 2883584 | tf_op jit(solution)/shard_map/pallas_call | solution.py:517
  56.3 1.6 %collective-permute-start.19 = (bf16[160,256]{1,0:T(8,128)(2,1)S(1)}, bf16[160,256]{1,0:T(8,128)(2,1)S(1)}, u32[]{:S(2)}, u32[]{:S(2)}) collective-permute-start(bf16[160,256]{1,0:T(8,128)(2,1)S(1)} %add_convert_fusion.3), channel_id=1, source_target_pairs={{0,2},{2,0},{1,3},{3,1},{4,6},{6,4},{5,7},{7,5},{8,10},{10,8},{9,1... | collective-permute-start | bytes 245768 | tf_op jit(solution)/shard_map/ppermute | solution.py:22
  58.0 1.5 %collective-permute-start.11 = (bf16[144,512]{1,0:T(8,128)(2,1)S(1)}, bf16[144,512]{1,0:T(8,128)(2,1)S(1)}, u32[]{:S(2)}, u32[]{:S(2)}) collective-permute-start(bf16[144,512]{1,0:T(8,128)(2,1)S(1)} %get-tuple-element.81), channel_id=1, source_target_pairs={{0,2},{2,0},{1,3},{3,1},{4,6},{6,4},{5,7},{7,5},{8,10},{10,8},{9,1... | collective-permute-start | bytes 442376 | tf_op jit(solution)/shard_map/ppermute | solution.py:22
  59.6 4.4 %collective-permute-done.25 = bf16[160,896]{1,0:T(8,128)(2,1)S(1)} collective-permute-done((bf16[160,896]{1,0:T(8,128)(2,1)S(1)}, bf16[160,896]{1,0:T(8,128)(2,1)S(1)}, u32[]{:S(2)}, u32[]{:S(2)}) %collective-permute-start.25) | collective-permute-done | bytes 286752 | tf_op jit(solution)/shard_map/ppermute | solution.py:22
  64.1 1.6 %collective-permute-done.19 = bf16[160,256]{1,0:T(8,128)(2,1)S(1)} collective-permute-done((bf16[160,256]{1,0:T(8,128)(2,1)S(1)}, bf16[160,256]{1,0:T(8,128)(2,1)S(1)}, u32[]{:S(2)}, u32[]{:S(2)}) %collective-permute-start.19) | collective-permute-done | bytes 81952 | tf_op jit(solution)/shard_map/ppermute | solution.py:22
  65.8 2.2 %collective-permute-done.11.refs_1_ = bf16[144,512]{1,0:T(8,128)(2,1)S(1)} collective-permute-done((bf16[144,512]{1,0:T(8,128)(2,1)S(1)}, bf16[144,512]{1,0:T(8,128)(2,1)S(1)}, u32[]{:S(2)}, u32[]{:S(2)}) %collective-permute-start.11) | collective-permute-done | bytes 147488 | tf_op jit(solution)/shard_map/ppermute | solution.py:22
  69.0 1.4 %collective-permute-start.13 = (bf16[48,512]{1,0:T(8,128)(2,1)S(1)}, bf16[48,512]{1,0:T(8,128)(2,1)S(1)}, u32[]{:S(2)}, u32[]{:S(2)}) collective-permute-start(bf16[48,512]{1,0:T(8,128)(2,1)S(1)} %get-tuple-element.84), channel_id=1, source_target_pairs={{0,8},{4,12},{8,0},{12,4},{1,9},{5,13},{9,1},{13,5},{2,10},{6,14},... | collective-permute-start | bytes 147464 | tf_op jit(solution)/shard_map/ppermute | solution.py:22
  70.4 2.2 %collective-permute-start.14 = (bf16[48,512]{1,0:T(8,128)(2,1)S(1)}, bf16[48,512]{1,0:T(8,128)(2,1)S(1)}, u32[]{:S(2)}, u32[]{:S(2)}) collective-permute-start(bf16[48,512]{1,0:T(8,128)(2,1)S(1)} %get-tuple-element.85), channel_id=1, source_target_pairs={{0,12},{4,8},{8,4},{12,0},{1,13},{5,9},{9,5},{13,1},{2,14},{6,10},... | collective-permute-start | bytes 147464 | tf_op jit(solution)/shard_map/ppermute | solution.py:22
  72.6 2.5 %collective-permute-done.13.refs_2_ = bf16[48,512]{1,0:T(8,128)(2,1)S(1)} collective-permute-done((bf16[48,512]{1,0:T(8,128)(2,1)S(1)}, bf16[48,512]{1,0:T(8,128)(2,1)S(1)}, u32[]{:S(2)}, u32[]{:S(2)}) %collective-permute-start.13) | collective-permute-done | bytes 49184 | tf_op jit(solution)/shard_map/ppermute | solution.py:22
  75.1 1.2 %collective-permute-done.14.refs_3_ = bf16[48,512]{1,0:T(8,128)(2,1)S(1)} collective-permute-done((bf16[48,512]{1,0:T(8,128)(2,1)S(1)}, bf16[48,512]{1,0:T(8,128)(2,1)S(1)}, u32[]{:S(2)}, u32[]{:S(2)}) %collective-permute-start.14) | collective-permute-done | bytes 49184 | tf_op jit(solution)/shard_map/ppermute | solution.py:22
  77.0 1.2 %shard_map.123 = (f32[320,512]{1,0:T(8,128)}, f32[320,576]{1,0:T(8,128)}) custom-call(bf16[160,256]{1,0:T(8,128)(2,1)S(1)} %add_convert_fusion.2.refs_0_, bf16[160,256]{1,0:T(8,128)(2,1)S(1)} %collective-permute-done.20.refs_1_, bf16[160,896]{1,0:T(8,128)(2,1)S(1)} %add_convert_fusion.refs_2_, bf16[160,896]{1,0:T(8,128)(2,1)S(1)} %collective-permute-done.26.refs_3_), custom_call_target="tpu_custom_call" | custom-call | flops 16777216 | bytes 2129920 | tf_op jit(solution)/shard_map/pallas_call | solution.py:517
  (46 shorter events, 8.5 us)
Async XLA Ops:
  0.6 29.3 %copy-start = (bf16[512,512]{1,0:T(8,128)(2,1)S(1)}, bf16[512,512]{1,0:T(8,128)(2,1)}, u32[]{:S(2)}) copy-start(bf16[512,512]{1,0:T(8,128)(2,1)} %mix_ref.3) | copy-start | bytes 1572868
  0.6 29.8 %copy-start.2 = (f32[9,512]{1,0:T(8,128)S(1)}, f32[9,512]{1,0:T(8,128)}, u32[]{:S(2)}) copy-start(f32[9,512]{1,0:T(8,128)} %depth_ref.3) | copy-start | bytes 55300
  2.1 5.5 %collective-permute-start.3 = (bf16[5,32,256]{2,1,0:T(8,128)(2,1)S(1)}, bf16[5,32,256]{2,1,0:T(8,128)(2,1)S(1)}, u32[]{:S(2)}, u32[]{:S(2)}) collective-permute-start(bf16[5,32,256]{2,1,0:T(8,128)(2,1)S(1)} %get-tuple-element.62), channel_id=1, source_target_pairs={{0,2},{2,0},{1,3},{3,1},{4,6},{6,4},{5,7},{7,5},{8,10},{10,8},{9,1... | collective-permute-start | bytes 245768 | tf_op jit(solution)/shard_map/ppermute | solution.py:30
  9.3 19.3 %collective-permute-start.4 = (bf16[216,256]{1,0:T(8,128)(2,1)S(1)}, bf16[216,256]{1,0:T(8,128)(2,1)S(1)}, u32[]{:S(2)}, u32[]{:S(2)}) collective-permute-start(bf16[216,256]{1,0:T(8,128)(2,1)S(1)} %get-tuple-element.64), channel_id=1, source_target_pairs={{0,4},{4,0},{8,12},{12,8},{1,5},{5,1},{9,13},{13,9},{2,6},{6,2},{1... | collective-permute-start | bytes 331784 | tf_op jit(solution)/shard_map/ppermute | solution.py:22
  11.4 19.0 %collective-permute-start.5 = (bf16[216,256]{1,0:T(8,128)(2,1)S(1)}, bf16[216,256]{1,0:T(8,128)(2,1)S(1)}, u32[]{:S(2)}, u32[]{:S(2)}) collective-permute-start(bf16[216,256]{1,0:T(8,128)(2,1)S(1)} %get-tuple-element.65), channel_id=1, source_target_pairs={{0,8},{4,12},{8,0},{12,4},{1,9},{5,13},{9,1},{13,5},{2,10},{6,14},... | collective-permute-start | bytes 331784 | tf_op jit(solution)/shard_map/ppermute | solution.py:22
  14.0 16.4 %collective-permute-start.6 = (bf16[216,256]{1,0:T(8,128)(2,1)S(1)}, bf16[216,256]{1,0:T(8,128)(2,1)S(1)}, u32[]{:S(2)}, u32[]{:S(2)}) collective-permute-start(bf16[216,256]{1,0:T(8,128)(2,1)S(1)} %get-tuple-element.66), channel_id=1, source_target_pairs={{0,12},{4,8},{8,4},{12,0},{1,13},{5,9},{9,5},{13,1},{2,14},{6,10},... | collective-permute-start | bytes 331784 | tf_op jit(solution)/shard_map/ppermute | solution.py:22
  14.0 4.8 %collective-permute-start = (bf16[16,512]{1,0:T(8,128)(2,1)S(1)}, bf16[16,512]{1,0:T(8,128)(2,1)S(1)}, u32[]{:S(2)}, u32[]{:S(2)}) collective-permute-start(bf16[16,512]{1,0:T(8,128)(2,1)S(1)} %get-tuple-element.53), channel_id=1, source_target_pairs={{0,4},{8,12},{4,0},{12,8},{1,5},{9,13},{5,1},{13,9},{2,6},{10,14},... | collective-permute-start | bytes 49160 | tf_op jit(solution)/shard_map/ppermute | solution.py:30
  14.9 3.9 %collective-permute-start.1 = (bf16[16,512]{1,0:T(8,128)(2,1)S(1)}, bf16[16,512]{1,0:T(8,128)(2,1)S(1)}, u32[]{:S(2)}, u32[]{:S(2)}) collective-permute-start(bf16[16,512]{1,0:T(8,128)(2,1)S(1)} %get-tuple-element.54), channel_id=1, source_target_pairs={{4,8},{8,4},{5,9},{9,5},{6,10},{10,6},{7,11},{11,7},{20,24},{24,20... | collective-permute-start | bytes 49160 | tf_op jit(solution)/shard_map/ppermute | solution.py:30
  18.8 6.5 %collective-permute-start.2 = (bf16[16,512]{1,0:T(8,128)(2,1)S(1)}, bf16[16,512]{1,0:T(8,128)(2,1)S(1)}, u32[]{:S(2)}, u32[]{:S(2)}) collective-permute-start(bf16[16,512]{1,0:T(8,128)(2,1)S(1)} %get-tuple-element.58), channel_id=1, source_target_pairs={{0,2},{2,0},{1,3},{3,1},{4,6},{6,4},{5,7},{7,5},{8,10},{10,8},{9,1... | collective-permute-start | bytes 49160 | tf_op jit(solution)/shard_map/ppermute | solution.py:30
  20.4 14.2 %collective-permute-start.7 = (bf16[216,256]{1,0:T(8,128)(2,1)S(1)}, bf16[216,256]{1,0:T(8,128)(2,1)S(1)}, u32[]{:S(2)}, u32[]{:S(2)}) collective-permute-start(bf16[216,256]{1,0:T(8,128)(2,1)S(1)} %get-tuple-element.69), channel_id=1, source_target_pairs={{0,4},{4,0},{8,12},{12,8},{1,5},{5,1},{9,13},{13,9},{2,6},{6,2},{1... | collective-permute-start | bytes 331784 | tf_op jit(solution)/shard_map/ppermute | solution.py:22
  25.3 11.9 %collective-permute-start.8 = (bf16[216,256]{1,0:T(8,128)(2,1)S(1)}, bf16[216,256]{1,0:T(8,128)(2,1)S(1)}, u32[]{:S(2)}, u32[]{:S(2)}) collective-permute-start(bf16[216,256]{1,0:T(8,128)(2,1)S(1)} %get-tuple-element.70), channel_id=1, source_target_pairs={{0,8},{4,12},{8,0},{12,4},{1,9},{5,13},{9,1},{13,5},{2,10},{6,14},... | collective-permute-start | bytes 331784 | tf_op jit(solution)/shard_map/ppermute | solution.py:22
  28.6 8.6 %collective-permute-start.9 = (bf16[216,256]{1,0:T(8,128)(2,1)S(1)}, bf16[216,256]{1,0:T(8,128)(2,1)S(1)}, u32[]{:S(2)}, u32[]{:S(2)}) collective-permute-start(bf16[216,256]{1,0:T(8,128)(2,1)S(1)} %get-tuple-element.71), channel_id=1, source_target_pairs={{0,12},{4,8},{8,4},{12,0},{1,13},{5,9},{9,5},{13,1},{2,14},{6,10},... | collective-permute-start | bytes 331784 | tf_op jit(solution)/shard_map/ppermute | solution.py:22
  30.4 20.5 %copy-start.1 = (bf16[320,512]{1,0:T(8,128)(2,1)S(1)}, bf16[320,512]{1,0:T(8,128)(2,1)}, u32[]{:S(2)}) copy-start(bf16[320,512]{1,0:T(8,128)(2,1)} %weight_ref.1) | copy-start | bytes 983044
  31.5 13.3 %collective-permute-start.15 = (bf16[128,256]{1,0:T(8,128)(2,1)S(1)}, bf16[128,256]{1,0:T(8,128)(2,1)S(1)}, u32[]{:S(2)}, u32[]{:S(2)}) collective-permute-start(bf16[128,256]{1,0:T(8,128)(2,1)S(1)} %bitcast.16), channel_id=1, source_target_pairs={{0,4},{4,0},{8,12},{12,8},{1,5},{5,1},{9,13},{13,9},{2,6},{6,2},{1... | collective-permute-start | bytes 196616 | tf_op jit(solution)/shard_map/ppermute | solution.py:22
  31.6 15.9 %collective-permute-start.16 = (bf16[128,256]{1,0:T(8,128)(2,1)S(1)}, bf16[128,256]{1,0:T(8,128)(2,1)S(1)}, u32[]{:S(2)}, u32[]{:S(2)}) collective-permute-start(bf16[128,256]{1,0:T(8,128)(2,1)S(1)} %bitcast.17), channel_id=1, source_target_pairs={{0,8},{4,12},{8,0},{12,4},{1,9},{5,13},{9,1},{13,5},{2,10},{6,14},... | collective-permute-start | bytes 196616 | tf_op jit(solution)/shard_map/ppermute | solution.py:22
  34.6 12.9 %collective-permute-start.17 = (bf16[128,256]{1,0:T(8,128)(2,1)S(1)}, bf16[128,256]{1,0:T(8,128)(2,1)S(1)}, u32[]{:S(2)}, u32[]{:S(2)}) collective-permute-start(bf16[128,256]{1,0:T(8,128)(2,1)S(1)} %bitcast.18), channel_id=1, source_target_pairs={{0,12},{4,8},{8,4},{12,0},{1,13},{5,9},{9,5},{13,1},{2,14},{6,10},... | collective-permute-start | bytes 196616 | tf_op jit(solution)/shard_map/ppermute | solution.py:22
  38.2 9.7 %collective-permute-start.21 = (bf16[128,256]{1,0:T(8,128)(2,1)S(1)}, bf16[128,256]{1,0:T(8,128)(2,1)S(1)}, u32[]{:S(2)}, u32[]{:S(2)}) collective-permute-start(bf16[128,256]{1,0:T(8,128)(2,1)S(1)} %bitcast.12), channel_id=1, source_target_pairs={{0,4},{4,0},{8,12},{12,8},{1,5},{5,1},{9,13},{13,9},{2,6},{6,2},{1... | collective-permute-start | bytes 196616 | tf_op jit(solution)/shard_map/ppermute | solution.py:22
  44.0 5.8 %collective-permute-start.22 = (bf16[128,256]{1,0:T(8,128)(2,1)S(1)}, bf16[128,256]{1,0:T(8,128)(2,1)S(1)}, u32[]{:S(2)}, u32[]{:S(2)}) collective-permute-start(bf16[128,256]{1,0:T(8,128)(2,1)S(1)} %bitcast.13), channel_id=1, source_target_pairs={{0,8},{4,12},{8,0},{12,4},{1,9},{5,13},{9,1},{13,5},{2,10},{6,14},... | collective-permute-start | bytes 196616 | tf_op jit(solution)/shard_map/ppermute | solution.py:22
  44.8 6.2 %collective-permute-start.23 = (bf16[128,256]{1,0:T(8,128)(2,1)S(1)}, bf16[128,256]{1,0:T(8,128)(2,1)S(1)}, u32[]{:S(2)}, u32[]{:S(2)}) collective-permute-start(bf16[128,256]{1,0:T(8,128)(2,1)S(1)} %bitcast.14), channel_id=1, source_target_pairs={{0,12},{4,8},{8,4},{12,0},{1,13},{5,9},{9,5},{13,1},{2,14},{6,10},... | collective-permute-start | bytes 196616 | tf_op jit(solution)/shard_map/ppermute | solution.py:22
  52.5 1.6 %collective-permute-start.24 = (bf16[160,896]{1,0:T(8,128)(2,1)S(1)}, bf16[160,896]{1,0:T(8,128)(2,1)S(1)}, u32[]{:S(2)}, u32[]{:S(2)}) collective-permute-start(bf16[160,896]{1,0:T(8,128)(2,1)S(1)} %get-tuple-element.96), channel_id=1, source_target_pairs={{0,1},{1,0},{2,3},{3,2},{4,5},{5,4},{6,7},{7,6},{8,9},{9,8},{10,11... | collective-permute-start | bytes 860168 | tf_op jit(solution)/shard_map/ppermute | solution.py:22
  52.6 3.7 %collective-permute-start.18 = (bf16[160,256]{1,0:T(8,128)(2,1)S(1)}, bf16[160,256]{1,0:T(8,128)(2,1)S(1)}, u32[]{:S(2)}, u32[]{:S(2)}) collective-permute-start(bf16[160,256]{1,0:T(8,128)(2,1)S(1)} %get-tuple-element.91), channel_id=1, source_target_pairs={{0,1},{1,0},{2,3},{3,2},{4,5},{5,4},{6,7},{7,6},{8,9},{9,8},{10,11... | collective-permute-start | bytes 245768 | tf_op jit(solution)/shard_map/ppermute | solution.py:22
  54.2 9.8 %collective-permute-start.25 = (bf16[160,896]{1,0:T(8,128)(2,1)S(1)}, bf16[160,896]{1,0:T(8,128)(2,1)S(1)}, u32[]{:S(2)}, u32[]{:S(2)}) collective-permute-start(bf16[160,896]{1,0:T(8,128)(2,1)S(1)} %add_convert_fusion.1), channel_id=1, source_target_pairs={{0,2},{2,0},{1,3},{3,1},{4,6},{6,4},{5,7},{7,5},{8,10},{10,8},{9,1... | collective-permute-start | bytes 860168 | tf_op jit(solution)/shard_map/ppermute | solution.py:22
  56.2 1.7 %collective-permute-start.10 = (bf16[272,512]{1,0:T(8,128)(2,1)S(1)}, bf16[272,512]{1,0:T(8,128)(2,1)S(1)}, u32[]{:S(2)}, u32[]{:S(2)}) collective-permute-start(bf16[272,512]{1,0:T(8,128)(2,1)S(1)} %get-tuple-element.79), channel_id=1, source_target_pairs={{0,1},{1,0},{2,3},{3,2},{4,5},{5,4},{6,7},{7,6},{8,9},{9,8},{10,11... | collective-permute-start | bytes 835592 | tf_op jit(solution)/shard_map/ppermute | solution.py:22
  56.3 9.5 %collective-permute-start.19 = (bf16[160,256]{1,0:T(8,128)(2,1)S(1)}, bf16[160,256]{1,0:T(8,128)(2,1)S(1)}, u32[]{:S(2)}, u32[]{:S(2)}) collective-permute-start(bf16[160,256]{1,0:T(8,128)(2,1)S(1)} %add_convert_fusion.3), channel_id=1, source_target_pairs={{0,2},{2,0},{1,3},{3,1},{4,6},{6,4},{5,7},{7,5},{8,10},{10,8},{9,1... | collective-permute-start | bytes 245768 | tf_op jit(solution)/shard_map/ppermute | solution.py:22
  58.0 10.0 %collective-permute-start.11 = (bf16[144,512]{1,0:T(8,128)(2,1)S(1)}, bf16[144,512]{1,0:T(8,128)(2,1)S(1)}, u32[]{:S(2)}, u32[]{:S(2)}) collective-permute-start(bf16[144,512]{1,0:T(8,128)(2,1)S(1)} %get-tuple-element.81), channel_id=1, source_target_pairs={{0,2},{2,0},{1,3},{3,1},{4,6},{6,4},{5,7},{7,5},{8,10},{10,8},{9,1... | collective-permute-start | bytes 442376 | tf_op jit(solution)/shard_map/ppermute | solution.py:22
  64.0 12.9 %collective-permute-start.26 = (bf16[160,896]{1,0:T(8,128)(2,1)S(1)}, bf16[160,896]{1,0:T(8,128)(2,1)S(1)}, u32[]{:S(2)}, u32[]{:S(2)}) collective-permute-start(bf16[160,896]{1,0:T(8,128)(2,1)S(1)} %add_convert_fusion.refs_2_), channel_id=1, source_target_pairs={{0,1},{1,0},{2,3},{3,2},{4,5},{5,4},{6,7},{7,6},{8,9},{9,8},{10,11... | collective-permute-start | bytes 860168 | tf_op jit(solution)/shard_map/ppermute | solution.py:22
  65.7 11.2 %collective-permute-start.20 = (bf16[160,256]{1,0:T(8,128)(2,1)S(1)}, bf16[160,256]{1,0:T(8,128)(2,1)S(1)}, u32[]{:S(2)}, u32[]{:S(2)}) collective-permute-start(bf16[160,256]{1,0:T(8,128)(2,1)S(1)} %add_convert_fusion.2.refs_0_), channel_id=1, source_target_pairs={{0,1},{1,0},{2,3},{3,2},{4,5},{5,4},{6,7},{7,6},{8,9},{9,8},{10,11... | collective-permute-start | bytes 245768 | tf_op jit(solution)/shard_map/ppermute | solution.py:22
  68.1 4.5 %collective-permute-start.12 = (bf16[48,512]{1,0:T(8,128)(2,1)S(1)}, bf16[48,512]{1,0:T(8,128)(2,1)S(1)}, u32[]{:S(2)}, u32[]{:S(2)}) collective-permute-start(bf16[48,512]{1,0:T(8,128)(2,1)S(1)} %get-tuple-element.83), channel_id=1, source_target_pairs={{0,4},{4,0},{8,12},{12,8},{1,5},{5,1},{9,13},{13,9},{2,6},{6,2},{1... | collective-permute-start | bytes 147464 | tf_op jit(solution)/shard_map/ppermute | solution.py:22
  69.0 6.0 %collective-permute-start.13 = (bf16[48,512]{1,0:T(8,128)(2,1)S(1)}, bf16[48,512]{1,0:T(8,128)(2,1)S(1)}, u32[]{:S(2)}, u32[]{:S(2)}) collective-permute-start(bf16[48,512]{1,0:T(8,128)(2,1)S(1)} %get-tuple-element.84), channel_id=1, source_target_pairs={{0,8},{4,12},{8,0},{12,4},{1,9},{5,13},{9,1},{13,5},{2,10},{6,14},... | collective-permute-start | bytes 147464 | tf_op jit(solution)/shard_map/ppermute | solution.py:22
  70.4 5.9 %collective-permute-start.14 = (bf16[48,512]{1,0:T(8,128)(2,1)S(1)}, bf16[48,512]{1,0:T(8,128)(2,1)S(1)}, u32[]{:S(2)}, u32[]{:S(2)}) collective-permute-start(bf16[48,512]{1,0:T(8,128)(2,1)S(1)} %get-tuple-element.85), channel_id=1, source_target_pairs={{0,12},{4,8},{8,4},{12,0},{1,13},{5,9},{9,5},{13,1},{2,14},{6,10},... | collective-permute-start | bytes 147464 | tf_op jit(solution)/shard_map/ppermute | solution.py:22

commit v3 on v2

--- a/solution.py
+++ b/solution.py
@@ -38,17 +38,22 @@
 
 
 def full_sum(keep, send):
-    total = (keep.astype(F32) + swap(send, "rep", 1).astype(F32)).astype(BF16)
+    def add(first, second):
+        return (first.astype(F32) + second.astype(F32)).astype(BF16)
+
+    total = add(keep, swap(send, "rep", 1))
     step = 1
     while step < lax.axis_size("col"):
-        total = (total.astype(F32) + swap(total, "col", step).astype(F32)).astype(BF16)
+        total = add(total, swap(total, "col", step))
         step *= 2
-    remote = swap(total, "rep", 1)
-    return total, remote
+    return total, swap(total, "rep", 1)
 
 
 def join_kernel(parts, *refs):
-    in_refs, (in_out, group_out) = refs[:-2], refs[-2:]
+    in_refs, mix_refs, (in_out, group_out, mix_out, depth_out) = refs[: 2 * parts], refs[2 * parts : -4], refs[-4:]
+    total = tree_sum([ref[...].astype(F32) for ref in mix_refs])
+    mix_out[...] = total[: mix_out.shape[0]]
+    depth_out[...] = total[mix_out.shape[0] : mix_out.shape[0] + depth_out.shape[0]]
     rows = in_refs[0].shape[0]
     rep = lax.axis_index("rep")
     for i in range(parts):
@@ -293,6 +298,17 @@
 TAPS = [(a, b) for a in range(3) for b in range(3)]
 
 
+def by_groups(count, most, step):
+    group = max(g for g in range(1, most + 1) if count % g == 0)
+
+    def body(i, carry):
+        for j in range(group):
+            step(i * group + j)
+        return carry
+
+    lax.fori_loop(0, count // group, body, 0)
+
+
 def middle_kernel(tiles, lane, grad_ref, depth_ref, *refs):
     term_refs, (act_grad_ref, hidden_ref, act, inner) = refs[:tiles], refs[tiles:]
     width = grad_ref.shape[0] - 2
@@ -318,7 +334,7 @@
             for half in range(2):
                 act[n, lax.rem(before_block + width + 2, width + 4) + half] = jnp.zeros(act.shape[2:], F32)
 
-    def forward(column, carry):
+    def forward(column):
         for n, here, whole in chunks:
             terms = [
                 depth_ref[3 * a + b : 3 * a + b + 1, whole] * act[n, column + b, a : a + ROWS + 2, :] for a, b in TAPS
@@ -329,11 +345,10 @@
             grad = grad_ref[column, 0 : ROWS + 2, whole] * slope
             inner[n, column, 0 : ROWS + 2, :] = grad.astype(BF16).astype(F32)
             hidden_ref[column, :, here] = (before * sig)[1 : ROWS + 1]
-        return carry
-
-    lax.fori_loop(0, width + 2, forward, 0)
-
-    def backward(column, carry):
+
+    by_groups(width + 2, 3, forward)
+
+    def backward(column):
         place = lax.shift_right_logical(column, 1) + (column & 1) * (width // 2)
         for n, here, whole in chunks:
             terms = [
@@ -341,9 +356,8 @@
                 for a, b in TAPS
             ]
             act_grad_ref[place, :, here] = tree_sum(terms).astype(BF16)
-        return carry
-
-    lax.fori_loop(0, width, backward, 0)
+
+    by_groups(width, 4, backward)
 
 
 def finish_kernel(parts, upstream_ref, mix_ref, *refs):
@@ -403,14 +417,6 @@
             start = pl.multiple_of(g * size * block + part * block, 16)
             out[g * block : (g + 1) * block, :] = held[pl.ds(start, block), :]
         out[rows:, :] = held[held.shape[0] - 16 :, :]
-
-
-def total_kernel(count, *refs):
-    in_refs, (mix_ref, depth_ref) = refs[:count], refs[count:]
-    total = tree_sum([ref[...].astype(F32) for ref in in_refs])
-    rows = mix_ref.shape[0]
-    mix_ref[...] = total[:rows]
-    depth_ref[...] = total[rows : rows + depth_ref.shape[0]]
 
 
 def corner_kernel(ends, sides, *refs):
@@ -640,10 +646,6 @@
             [pltpu.VMEM(arrived[0].shape, BF16)],
         )
         arrived = [swap(dealt[step], axis, step) if step else dealt[0] for step in range(size)]
-    mix_grad, depth_grad = call(
-        functools.partial(total_kernel, tiles), [((rows, hidden), F32), ((9, hidden), F32)], arrived
-    )
-
     half = slots * channels // 2
     joined, wholes = [], []
     for h in range(parts - 1):
@@ -664,8 +666,10 @@
         flops=1 << 28,
     )
     joined += full_sum(keep, send)
-    in_grad, group_grad = call(
-        functools.partial(join_kernel, parts), [((2 * half, hidden), F32), ((2 * half, 9 * channels), F32)], joined
+    in_grad, group_grad, mix_grad, depth_grad = call(
+        functools.partial(join_kernel, parts),
+        [((2 * half, hidden), F32), ((2 * half, 9 * channels), F32), ((rows, hidden), F32), ((9, hidden), F32)],
+        [*joined, *arrived],
     )
     group_grad = jnp.swapaxes(group_grad.reshape(slots, channels, -1), 1, 2)
     return (adjusted.reshape(cotangent.shape), mix_grad, depth_grad, in_grad, group_grad)

time: 78.3 us -> 77.4 us (0.989)
  Pallas kernels: 12.1 us -> 10.7 us
  waiting for transfers between devices: 22.3 us -> 23.2 us
    pallas_call x14 -> x13, Pallas kernels: 12.1 us -> 10.7 us  [call(): pl.pallas_call(kernel, out_shape=shapes, in_specs=specs or [SMEM if jnp.i...]
    ppermute x23, waiting for transfers between devices: 17.3 us -> 18.1 us  [swap(): lax.ppermute(value, axis, [(i, i ^ step) for i in range(lax.axis_size(axi...]
  transfers between devices with their start and end apart: 27 -> 27, of which waited for: 11 -> 12; matrix products, arithmetic and copies ran while one was open for 0% -> 0% of each run, Pallas kernels for 8% -> 6%
where the time goes in v3:
time: 77.4 us; the launch traced here: 77.2 us
  starting transfers between devices  41.7 us (54%)
  waiting for transfers between devices  23.2 us (30%)
  Pallas kernels  10.7 us (14%)
  between operations  1.49 us (2%)
    ppermute x23, starting transfers between devices, swap(): lax.ppermute(value, axis, [(i, i ^ step) for i in range(lax.axis_size(axi...  35.5 us
    ppermute x23, waiting for transfers between devices, swap(): lax.ppermute(value, axis, [(i, i ^ step) for i in range(lax.axis_size(axi...  18.1 us
    pallas_call x13, Pallas kernels, call(): pl.pallas_call(kernel, out_shape=shapes, in_specs=specs or [SMEM if jnp.i...  10.7 us
    ppermute x4, starting transfers between devices, with_neighbours(): lax.ppermute(value, axis, pairs + [(b, a) for a, b in pairs])  6.19 us
    ppermute x4, waiting for transfers between devices, with_neighbours(): lax.ppermute(value, axis, pairs + [(b, a) for a, b in pairs])  5.01 us
  transfers between devices with their start and end apart: 27, of which 12 were waited for; matrix products, arithmetic and copies ran while one was open for 0% of the time, Pallas kernels for 6%

profile of v3, /device:TPU:0, one launch (start us, length us, event | category | flops | bytes accessed | tf_op | source)
XLA Modules:
  0.0 77.2 jit_solution(7018467444383257886)
XLA Ops:
  0.7 1.4 %shard_map.110 = (bf16[5,32,1024]{2,1,0:T(8,128)(2,1)S(1)}, bf16[5,128,768]{2,1,0:T(8,128)(2,1)S(1)}, bf16[384,512]{1,0:T(8,128)(2,1)S(1)}, bf16[8,16,512]{2,1,0...) custom-call(bf16[5,32,1024]{2,1,0:T(8,128)(2,1)} %bitcast.21, ...), custom_call_target="tpu_custom_call" | custom-call | flops 16777216 | bytes 3112960 | tf_op jit(solution)/shard_map/pallas_call | solution.py:523
  2.1 3.0 %collective-permute-start.3 = (bf16[5,32,256]{2,1,0:T(8,128)(2,1)S(1)}, bf16[5,32,256]{2,1,0:T(8,128)(2,1)S(1)}, u32[]{:S(2)}, u32[]{:S(2)}) collective-permute-start(bf16[5,32,256]{2,1,0:T(8,128)(2,1)S(1)} %get-tuple-element.62), channel_id=1, source_target_pairs={{0,2},{2,0},{1,3},{3,1},{4,6},{6,4},{5,7},{7,5},{8,10},{10,8},{9,1... | collective-permute-start | bytes 245768 | tf_op jit(solution)/shard_map/ppermute | solution.py:30
  5.8 1.8 %collective-permute-done.3.refs_0_ = bf16[5,32,256]{2,1,0:T(8,128)(2,1)S(1)} collective-permute-done((bf16[5,32,256]{2,1,0:T(8,128)(2,1)S(1)}, bf16[5,32,256]{2,1,0:T(8,128)(2,1)S(1)}, u32[]{:S(2)}, u32[]{:S(2)}) %collective-permute-start.3) | collective-permute-done | bytes 81952 | tf_op jit(solution)/shard_map/ppermute | solution.py:30
  7.6 1.7 %shard_map.113 = (bf16[216,256]{1,0:T(8,128)(2,1)S(1)}, bf16[216,256]{1,0:T(8,128)(2,1)S(1)}, bf16[216,256]{1,0:T(8,128)(2,1)S(1)}, bf16[216,256]{1,0:T(8,128)(2...) custom-call(s32[1]{0:T(128)S(6)} %copy.12.count_ref, ...), custom_call_target="tpu_custom_call" | custom-call | flops 268435456 | bytes 2670596 | tf_op jit(solution)/shard_map/pallas_call | solution.py:523
  9.3 2.2 %collective-permute-start.4 = (bf16[216,256]{1,0:T(8,128)(2,1)S(1)}, bf16[216,256]{1,0:T(8,128)(2,1)S(1)}, u32[]{:S(2)}, u32[]{:S(2)}) collective-permute-start(bf16[216,256]{1,0:T(8,128)(2,1)S(1)} %get-tuple-element.64), channel_id=1, source_target_pairs={{0,4},{4,0},{8,12},{12,8},{1,5},{5,1},{9,13},{13,9},{2,6},{6,2},{1... | collective-permute-start | bytes 331784 | tf_op jit(solution)/shard_map/ppermute | solution.py:22
  11.4 2.6 %collective-permute-start.5 = (bf16[216,256]{1,0:T(8,128)(2,1)S(1)}, bf16[216,256]{1,0:T(8,128)(2,1)S(1)}, u32[]{:S(2)}, u32[]{:S(2)}) collective-permute-start(bf16[216,256]{1,0:T(8,128)(2,1)S(1)} %get-tuple-element.65), channel_id=1, source_target_pairs={{0,8},{4,12},{8,0},{12,4},{1,9},{5,13},{9,1},{13,5},{2,10},{6,14},... | collective-permute-start | bytes 331784 | tf_op jit(solution)/shard_map/ppermute | solution.py:22
  15.6 3.2 %collective-permute-done.refs_0_ = bf16[16,512]{1,0:T(8,128)(2,1)S(1)} collective-permute-done((bf16[16,512]{1,0:T(8,128)(2,1)S(1)}, bf16[16,512]{1,0:T(8,128)(2,1)S(1)}, u32[]{:S(2)}, u32[]{:S(2)}) %collective-permute-start) | collective-permute-done | bytes 16416 | tf_op jit(solution)/shard_map/ppermute | solution.py:30
  18.8 1.6 %collective-permute-start.2 = (bf16[16,512]{1,0:T(8,128)(2,1)S(1)}, bf16[16,512]{1,0:T(8,128)(2,1)S(1)}, u32[]{:S(2)}, u32[]{:S(2)}) collective-permute-start(bf16[16,512]{1,0:T(8,128)(2,1)S(1)} %get-tuple-element.58), channel_id=1, source_target_pairs={{0,2},{2,0},{1,3},{3,1},{4,6},{6,4},{5,7},{7,5},{8,10},{10,8},{9,1... | collective-permute-start | bytes 49160 | tf_op jit(solution)/shard_map/ppermute | solution.py:30
  20.4 4.9 %collective-permute-start.7 = (bf16[216,256]{1,0:T(8,128)(2,1)S(1)}, bf16[216,256]{1,0:T(8,128)(2,1)S(1)}, u32[]{:S(2)}, u32[]{:S(2)}) collective-permute-start(bf16[216,256]{1,0:T(8,128)(2,1)S(1)} %get-tuple-element.69), channel_id=1, source_target_pairs={{0,4},{4,0},{8,12},{12,8},{1,5},{5,1},{9,13},{13,9},{2,6},{6,2},{1... | collective-permute-start | bytes 331784 | tf_op jit(solution)/shard_map/ppermute | solution.py:22
  25.3 3.3 %collective-permute-start.8 = (bf16[216,256]{1,0:T(8,128)(2,1)S(1)}, bf16[216,256]{1,0:T(8,128)(2,1)S(1)}, u32[]{:S(2)}, u32[]{:S(2)}) collective-permute-start(bf16[216,256]{1,0:T(8,128)(2,1)S(1)} %get-tuple-element.70), channel_id=1, source_target_pairs={{0,8},{4,12},{8,0},{12,4},{1,9},{5,13},{9,1},{13,5},{2,10},{6,14},... | collective-permute-start | bytes 331784 | tf_op jit(solution)/shard_map/ppermute | solution.py:22
  28.6 1.4 %collective-permute-start.9 = (bf16[216,256]{1,0:T(8,128)(2,1)S(1)}, bf16[216,256]{1,0:T(8,128)(2,1)S(1)}, u32[]{:S(2)}, u32[]{:S(2)}) collective-permute-start(bf16[216,256]{1,0:T(8,128)(2,1)S(1)} %get-tuple-element.71), channel_id=1, source_target_pairs={{0,12},{4,8},{8,4},{12,0},{1,13},{5,9},{9,5},{13,1},{2,14},{6,10},... | collective-permute-start | bytes 331784 | tf_op jit(solution)/shard_map/ppermute | solution.py:22
  31.1 3.0 %collective-permute-start.11 = (bf16[128,256]{1,0:T(8,128)(2,1)S(1)}, bf16[128,256]{1,0:T(8,128)(2,1)S(1)}, u32[]{:S(2)}, u32[]{:S(2)}) collective-permute-start(bf16[128,256]{1,0:T(8,128)(2,1)S(1)} %bitcast.17), channel_id=1, source_target_pairs={{0,8},{4,12},{8,0},{12,4},{1,9},{5,13},{9,1},{13,5},{2,10},{6,14},... | collective-permute-start | bytes 196616 | tf_op jit(solution)/shard_map/ppermute | solution.py:22
  34.2 1.4 %collective-permute-start.12 = (bf16[128,256]{1,0:T(8,128)(2,1)S(1)}, bf16[128,256]{1,0:T(8,128)(2,1)S(1)}, u32[]{:S(2)}, u32[]{:S(2)}) collective-permute-start(bf16[128,256]{1,0:T(8,128)(2,1)S(1)} %bitcast.18), channel_id=1, source_target_pairs={{0,12},{4,8},{8,4},{12,0},{1,13},{5,9},{9,5},{13,1},{2,14},{6,10},... | collective-permute-start | bytes 196616 | tf_op jit(solution)/shard_map/ppermute | solution.py:22
  35.5 1.7 %collective-permute-done.8.refs_2_ = bf16[216,256]{1,0:T(8,128)(2,1)S(1)} collective-permute-done((bf16[216,256]{1,0:T(8,128)(2,1)S(1)}, bf16[216,256]{1,0:T(8,128)(2,1)S(1)}, u32[]{:S(2)}, u32[]{:S(2)}) %collective-permute-start.8) | collective-permute-done | bytes 110624 | tf_op jit(solution)/shard_map/ppermute | solution.py:22
  37.9 5.8 %collective-permute-start.16 = (bf16[128,256]{1,0:T(8,128)(2,1)S(1)}, bf16[128,256]{1,0:T(8,128)(2,1)S(1)}, u32[]{:S(2)}, u32[]{:S(2)}) collective-permute-start(bf16[128,256]{1,0:T(8,128)(2,1)S(1)} %bitcast.12), channel_id=1, source_target_pairs={{0,4},{4,0},{8,12},{12,8},{1,5},{5,1},{9,13},{13,9},{2,6},{6,2},{1... | collective-permute-start | bytes 196616 | tf_op jit(solution)/shard_map/ppermute | solution.py:22
  44.4 1.7 %collective-permute-start.18 = (bf16[128,256]{1,0:T(8,128)(2,1)S(1)}, bf16[128,256]{1,0:T(8,128)(2,1)S(1)}, u32[]{:S(2)}, u32[]{:S(2)}) collective-permute-start(bf16[128,256]{1,0:T(8,128)(2,1)S(1)} %bitcast.14), channel_id=1, source_target_pairs={{0,12},{4,8},{8,4},{12,0},{1,13},{5,9},{9,5},{13,1},{2,14},{6,10},... | collective-permute-start | bytes 196616 | tf_op jit(solution)/shard_map/ppermute | solution.py:22
  46.1 1.1 %shard_map.117 = (bf16[5,256,896]{2,1,0:T(8,128)(2,1)S(1)}, bf16[512,384]{1,0:T(8,128)(2,1)S(1)}) custom-call(s32[1]{0:T(128)S(6)} %copy.12.count_ref, bf16[5,32,1024]{2,1,0:T(8,128)(2,1)S(1)} %get-tuple-element.59.field_ref, bf16[5,128,768]{2,1,0:T(8,128)(2,1)S(1)} %get-tuple-element.60.kernel_ref, bf16[5,32,256]{2,1,0:T(8,128)(2,1)S(1)} %collective-permute-done.3.refs_0_), custom_call_target="tpu_custom_call" | custom-call | flops 268435456 | bytes 4079620 | tf_op jit(solution)/shard_map/pallas_call | solution.py:523
  47.5 1.9 %collective-permute-done.17.refs_3_ = bf16[128,256]{1,0:T(8,128)(2,1)S(1)} collective-permute-done((bf16[128,256]{1,0:T(8,128)(2,1)S(1)}, bf16[128,256]{1,0:T(8,128)(2,1)S(1)}, u32[]{:S(2)}, u32[]{:S(2)}) %collective-permute-start.17) | collective-permute-done | bytes 65568 | tf_op jit(solution)/shard_map/ppermute | solution.py:22
  49.4 1.1 %collective-permute-done.18.refs_4_ = bf16[128,256]{1,0:T(8,128)(2,1)S(1)} collective-permute-done((bf16[128,256]{1,0:T(8,128)(2,1)S(1)}, bf16[128,256]{1,0:T(8,128)(2,1)S(1)}, u32[]{:S(2)}, u32[]{:S(2)}) %collective-permute-start.18) | collective-permute-done | bytes 65568 | tf_op jit(solution)/shard_map/ppermute | solution.py:22
  50.6 1.6 %shard_map.119 = (bf16[160,896]{1,0:T(8,128)(2,1)S(1)}, bf16[160,896]{1,0:T(8,128)(2,1)S(1)}) custom-call(bf16[512,384]{1,0:T(8,128)(2,1)S(1)} %get-tuple-element.78.own_ref, bf16[320,512]{1,0:T(8,128)(2,1)S(1)} %copy-done.1, bf16[5,256,896]{2,1,0:T(8,128)(2,1)S(1)} %get-tuple-element.82.patch_ref, bf16[512,256]{1,0:T(8,128)(2,1)S(1)} %get-tuple-element.83.refs_0_, ...), custom_call_target="tpu_custom_call" | custom-call | flops 268435456 | bytes 4112384 | tf_op jit(solution)/shard_map/pallas_call | solution.py:523
  52.7 1.1 %collective-permute-done.19 = bf16[160,896]{1,0:T(8,128)(2,1)S(1)} collective-permute-done((bf16[160,896]{1,0:T(8,128)(2,1)S(1)}, bf16[160,896]{1,0:T(8,128)(2,1)S(1)}, u32[]{:S(2)}, u32[]{:S(2)}) %collective-permute-start.19) | collective-permute-done | bytes 286752 | tf_op jit(solution)/shard_map/ppermute | solution.py:22
  54.8 1.5 %shard_map.116 = (bf16[128,512]{1,0:T(8,128)(2,1)}, bf16[272,512]{1,0:T(8,128)(2,1)S(1)}, bf16[272,512]{1,0:T(8,128)(2,1)S(1)}) custom-call(bf16[128,512]{1,0:T(8,128)(2,1)S(1)} %bitcast.11, bf16[512,512]{1,0:T(8,128)(2,1)S(1)} %copy-done, f32[18,8,256]{2,1,0:T(8,128)S(1)} %get-tuple-element.67.refs_0_, f32[18,8,256]{2,1,0:T(8,128)S(1)} %get-tuple-element.72.refs_1_, ...), custom_call_target="tpu_custom_call" | custom-call | flops 16777216 | bytes 2883584 | tf_op jit(solution)/shard_map/pallas_call | solution.py:523
  56.3 1.2 %collective-permute-start.14 = (bf16[160,256]{1,0:T(8,128)(2,1)S(1)}, bf16[160,256]{1,0:T(8,128)(2,1)S(1)}, u32[]{:S(2)}, u32[]{:S(2)}) collective-permute-start(bf16[160,256]{1,0:T(8,128)(2,1)S(1)} %add_convert_fusion.3), channel_id=1, source_target_pairs={{0,2},{2,0},{1,3},{3,1},{4,6},{6,4},{5,7},{7,5},{8,10},{10,8},{9,1... | collective-permute-start | bytes 245768 | tf_op jit(solution)/shard_map/ppermute | solution.py:22
  58.0 1.2 %collective-permute-start.23 = (bf16[144,512]{1,0:T(8,128)(2,1)S(1)}, bf16[144,512]{1,0:T(8,128)(2,1)S(1)}, u32[]{:S(2)}, u32[]{:S(2)}) collective-permute-start(bf16[144,512]{1,0:T(8,128)(2,1)S(1)} %get-tuple-element.90), channel_id=1, source_target_pairs={{0,2},{2,0},{1,3},{3,1},{4,6},{6,4},{5,7},{7,5},{8,10},{10,8},{9,1... | collective-permute-start | bytes 442376 | tf_op jit(solution)/shard_map/ppermute | solution.py:22
  59.2 4.4 %collective-permute-done.20 = bf16[160,896]{1,0:T(8,128)(2,1)S(1)} collective-permute-done((bf16[160,896]{1,0:T(8,128)(2,1)S(1)}, bf16[160,896]{1,0:T(8,128)(2,1)S(1)}, u32[]{:S(2)}, u32[]{:S(2)}) %collective-permute-start.20) | collective-permute-done | bytes 286752 | tf_op jit(solution)/shard_map/ppermute | solution.py:22
  63.8 1.6 %collective-permute-done.14 = bf16[160,256]{1,0:T(8,128)(2,1)S(1)} collective-permute-done((bf16[160,256]{1,0:T(8,128)(2,1)S(1)}, bf16[160,256]{1,0:T(8,128)(2,1)S(1)}, u32[]{:S(2)}, u32[]{:S(2)}) %collective-permute-start.14) | collective-permute-done | bytes 81952 | tf_op jit(solution)/shard_map/ppermute | solution.py:22
  65.4 2.2 %collective-permute-done.23.refs_1_ = bf16[144,512]{1,0:T(8,128)(2,1)S(1)} collective-permute-done((bf16[144,512]{1,0:T(8,128)(2,1)S(1)}, bf16[144,512]{1,0:T(8,128)(2,1)S(1)}, u32[]{:S(2)}, u32[]{:S(2)}) %collective-permute-start.23) | collective-permute-done | bytes 147488 | tf_op jit(solution)/shard_map/ppermute | solution.py:22
  68.6 1.5 %collective-permute-start.25 = (bf16[48,512]{1,0:T(8,128)(2,1)S(1)}, bf16[48,512]{1,0:T(8,128)(2,1)S(1)}, u32[]{:S(2)}, u32[]{:S(2)}) collective-permute-start(bf16[48,512]{1,0:T(8,128)(2,1)S(1)} %get-tuple-element.93), channel_id=1, source_target_pairs={{0,8},{4,12},{8,0},{12,4},{1,9},{5,13},{9,1},{13,5},{2,10},{6,14},... | collective-permute-start | bytes 147464 | tf_op jit(solution)/shard_map/ppermute | solution.py:22
  70.1 2.1 %collective-permute-start.26 = (bf16[48,512]{1,0:T(8,128)(2,1)S(1)}, bf16[48,512]{1,0:T(8,128)(2,1)S(1)}, u32[]{:S(2)}, u32[]{:S(2)}) collective-permute-start(bf16[48,512]{1,0:T(8,128)(2,1)S(1)} %get-tuple-element.94), channel_id=1, source_target_pairs={{0,12},{4,8},{8,4},{12,0},{1,13},{5,9},{9,5},{13,1},{2,14},{6,10},... | collective-permute-start | bytes 147464 | tf_op jit(solution)/shard_map/ppermute | solution.py:22
  72.2 2.5 %collective-permute-done.25.refs_6_ = bf16[48,512]{1,0:T(8,128)(2,1)S(1)} collective-permute-done((bf16[48,512]{1,0:T(8,128)(2,1)S(1)}, bf16[48,512]{1,0:T(8,128)(2,1)S(1)}, u32[]{:S(2)}, u32[]{:S(2)}) %collective-permute-start.25) | collective-permute-done | bytes 49184 | tf_op jit(solution)/shard_map/ppermute | solution.py:22
  74.7 1.3 %collective-permute-done.26.refs_7_ = bf16[48,512]{1,0:T(8,128)(2,1)S(1)} collective-permute-done((bf16[48,512]{1,0:T(8,128)(2,1)S(1)}, bf16[48,512]{1,0:T(8,128)(2,1)S(1)}, u32[]{:S(2)}, u32[]{:S(2)}) %collective-permute-start.26) | collective-permute-done | bytes 49184 | tf_op jit(solution)/shard_map/ppermute | solution.py:22
  76.0 1.2 %shard_map.122 = (f32[320,512]{1,0:T(8,128)}, f32[320,576]{1,0:T(8,128)}, f32[32,512]{1,0:T(8,128)}, f32[9,512]{1,0:T(8,128)}) custom-call(bf16[160,256]{1,0:T(8,128)(2,1)S(1)} %add_convert_fusion.2.refs_0_, bf16[160,256]{1,0:T(8,128)(2,1)S(1)} %collective-permute-done.15.refs_1_, bf16[160,896]{1,0:T(8,128)(2,1)S(1)} %add_convert_fusion.refs_2_, ...), custom_call_target="tpu_custom_call" | custom-call | flops 16777216 | bytes 2410496 | tf_op jit(solution)/shard_map/pallas_call | solution.py:523
  (45 shorter events, 7.7 us)
Async XLA Ops:
  0.6 29.3 %copy-start = (bf16[512,512]{1,0:T(8,128)(2,1)S(1)}, bf16[512,512]{1,0:T(8,128)(2,1)}, u32[]{:S(2)}) copy-start(bf16[512,512]{1,0:T(8,128)(2,1)} %mix_ref.3) | copy-start | bytes 1572868
  0.6 29.8 %copy-start.2 = (f32[9,512]{1,0:T(8,128)S(1)}, f32[9,512]{1,0:T(8,128)}, u32[]{:S(2)}) copy-start(f32[9,512]{1,0:T(8,128)} %depth_ref.3) | copy-start | bytes 55300
  2.1 5.5 %collective-permute-start.3 = (bf16[5,32,256]{2,1,0:T(8,128)(2,1)S(1)}, bf16[5,32,256]{2,1,0:T(8,128)(2,1)S(1)}, u32[]{:S(2)}, u32[]{:S(2)}) collective-permute-start(bf16[5,32,256]{2,1,0:T(8,128)(2,1)S(1)} %get-tuple-element.62), channel_id=1, source_target_pairs={{0,2},{2,0},{1,3},{3,1},{4,6},{6,4},{5,7},{7,5},{8,10},{10,8},{9,1... | collective-permute-start | bytes 245768 | tf_op jit(solution)/shard_map/ppermute | solution.py:30
  9.3 19.3 %collective-permute-start.4 = (bf16[216,256]{1,0:T(8,128)(2,1)S(1)}, bf16[216,256]{1,0:T(8,128)(2,1)S(1)}, u32[]{:S(2)}, u32[]{:S(2)}) collective-permute-start(bf16[216,256]{1,0:T(8,128)(2,1)S(1)} %get-tuple-element.64), channel_id=1, source_target_pairs={{0,4},{4,0},{8,12},{12,8},{1,5},{5,1},{9,13},{13,9},{2,6},{6,2},{1... | collective-permute-start | bytes 331784 | tf_op jit(solution)/shard_map/ppermute | solution.py:22
  11.4 19.0 %collective-permute-start.5 = (bf16[216,256]{1,0:T(8,128)(2,1)S(1)}, bf16[216,256]{1,0:T(8,128)(2,1)S(1)}, u32[]{:S(2)}, u32[]{:S(2)}) collective-permute-start(bf16[216,256]{1,0:T(8,128)(2,1)S(1)} %get-tuple-element.65), channel_id=1, source_target_pairs={{0,8},{4,12},{8,0},{12,4},{1,9},{5,13},{9,1},{13,5},{2,10},{6,14},... | collective-permute-start | bytes 331784 | tf_op jit(solution)/shard_map/ppermute | solution.py:22
  14.0 16.4 %collective-permute-start.6 = (bf16[216,256]{1,0:T(8,128)(2,1)S(1)}, bf16[216,256]{1,0:T(8,128)(2,1)S(1)}, u32[]{:S(2)}, u32[]{:S(2)}) collective-permute-start(bf16[216,256]{1,0:T(8,128)(2,1)S(1)} %get-tuple-element.66), channel_id=1, source_target_pairs={{0,12},{4,8},{8,4},{12,0},{1,13},{5,9},{9,5},{13,1},{2,14},{6,10},... | collective-permute-start | bytes 331784 | tf_op jit(solution)/shard_map/ppermute | solution.py:22
  14.0 4.8 %collective-permute-start = (bf16[16,512]{1,0:T(8,128)(2,1)S(1)}, bf16[16,512]{1,0:T(8,128)(2,1)S(1)}, u32[]{:S(2)}, u32[]{:S(2)}) collective-permute-start(bf16[16,512]{1,0:T(8,128)(2,1)S(1)} %get-tuple-element.53), channel_id=1, source_target_pairs={{0,4},{8,12},{4,0},{12,8},{1,5},{9,13},{5,1},{13,9},{2,6},{10,14},... | collective-permute-start | bytes 49160 | tf_op jit(solution)/shard_map/ppermute | solution.py:30
  14.9 3.9 %collective-permute-start.1 = (bf16[16,512]{1,0:T(8,128)(2,1)S(1)}, bf16[16,512]{1,0:T(8,128)(2,1)S(1)}, u32[]{:S(2)}, u32[]{:S(2)}) collective-permute-start(bf16[16,512]{1,0:T(8,128)(2,1)S(1)} %get-tuple-element.54), channel_id=1, source_target_pairs={{4,8},{8,4},{5,9},{9,5},{6,10},{10,6},{7,11},{11,7},{20,24},{24,20... | collective-permute-start | bytes 49160 | tf_op jit(solution)/shard_map/ppermute | solution.py:30
  18.8 6.5 %collective-permute-start.2 = (bf16[16,512]{1,0:T(8,128)(2,1)S(1)}, bf16[16,512]{1,0:T(8,128)(2,1)S(1)}, u32[]{:S(2)}, u32[]{:S(2)}) collective-permute-start(bf16[16,512]{1,0:T(8,128)(2,1)S(1)} %get-tuple-element.58), channel_id=1, source_target_pairs={{0,2},{2,0},{1,3},{3,1},{4,6},{6,4},{5,7},{7,5},{8,10},{10,8},{9,1... | collective-permute-start | bytes 49160 | tf_op jit(solution)/shard_map/ppermute | solution.py:30
  20.4 13.8 %collective-permute-start.7 = (bf16[216,256]{1,0:T(8,128)(2,1)S(1)}, bf16[216,256]{1,0:T(8,128)(2,1)S(1)}, u32[]{:S(2)}, u32[]{:S(2)}) collective-permute-start(bf16[216,256]{1,0:T(8,128)(2,1)S(1)} %get-tuple-element.69), channel_id=1, source_target_pairs={{0,4},{4,0},{8,12},{12,8},{1,5},{5,1},{9,13},{13,9},{2,6},{6,2},{1... | collective-permute-start | bytes 331784 | tf_op jit(solution)/shard_map/ppermute | solution.py:22
  25.3 12.0 %collective-permute-start.8 = (bf16[216,256]{1,0:T(8,128)(2,1)S(1)}, bf16[216,256]{1,0:T(8,128)(2,1)S(1)}, u32[]{:S(2)}, u32[]{:S(2)}) collective-permute-start(bf16[216,256]{1,0:T(8,128)(2,1)S(1)} %get-tuple-element.70), channel_id=1, source_target_pairs={{0,8},{4,12},{8,0},{12,4},{1,9},{5,13},{9,1},{13,5},{2,10},{6,14},... | collective-permute-start | bytes 331784 | tf_op jit(solution)/shard_map/ppermute | solution.py:22
  28.6 8.7 %collective-permute-start.9 = (bf16[216,256]{1,0:T(8,128)(2,1)S(1)}, bf16[216,256]{1,0:T(8,128)(2,1)S(1)}, u32[]{:S(2)}, u32[]{:S(2)}) collective-permute-start(bf16[216,256]{1,0:T(8,128)(2,1)S(1)} %get-tuple-element.71), channel_id=1, source_target_pairs={{0,12},{4,8},{8,4},{12,0},{1,13},{5,9},{9,5},{13,1},{2,14},{6,10},... | collective-permute-start | bytes 331784 | tf_op jit(solution)/shard_map/ppermute | solution.py:22
  30.4 20.2 %copy-start.1 = (bf16[320,512]{1,0:T(8,128)(2,1)S(1)}, bf16[320,512]{1,0:T(8,128)(2,1)}, u32[]{:S(2)}) copy-start(bf16[320,512]{1,0:T(8,128)(2,1)} %weight_ref.1) | copy-start | bytes 983044
  31.1 13.3 %collective-permute-start.10 = (bf16[128,256]{1,0:T(8,128)(2,1)S(1)}, bf16[128,256]{1,0:T(8,128)(2,1)S(1)}, u32[]{:S(2)}, u32[]{:S(2)}) collective-permute-start(bf16[128,256]{1,0:T(8,128)(2,1)S(1)} %bitcast.16), channel_id=1, source_target_pairs={{0,4},{4,0},{8,12},{12,8},{1,5},{5,1},{9,13},{13,9},{2,6},{6,2},{1... | collective-permute-start | bytes 196616 | tf_op jit(solution)/shard_map/ppermute | solution.py:22
  31.1 16.0 %collective-permute-start.11 = (bf16[128,256]{1,0:T(8,128)(2,1)S(1)}, bf16[128,256]{1,0:T(8,128)(2,1)S(1)}, u32[]{:S(2)}, u32[]{:S(2)}) collective-permute-start(bf16[128,256]{1,0:T(8,128)(2,1)S(1)} %bitcast.17), channel_id=1, source_target_pairs={{0,8},{4,12},{8,0},{12,4},{1,9},{5,13},{9,1},{13,5},{2,10},{6,14},... | collective-permute-start | bytes 196616 | tf_op jit(solution)/shard_map/ppermute | solution.py:22
  34.2 13.0 %collective-permute-start.12 = (bf16[128,256]{1,0:T(8,128)(2,1)S(1)}, bf16[128,256]{1,0:T(8,128)(2,1)S(1)}, u32[]{:S(2)}, u32[]{:S(2)}) collective-permute-start(bf16[128,256]{1,0:T(8,128)(2,1)S(1)} %bitcast.18), channel_id=1, source_target_pairs={{0,12},{4,8},{8,4},{12,0},{1,13},{5,9},{9,5},{13,1},{2,14},{6,10},... | collective-permute-start | bytes 196616 | tf_op jit(solution)/shard_map/ppermute | solution.py:22
  37.9 9.7 %collective-permute-start.16 = (bf16[128,256]{1,0:T(8,128)(2,1)S(1)}, bf16[128,256]{1,0:T(8,128)(2,1)S(1)}, u32[]{:S(2)}, u32[]{:S(2)}) collective-permute-start(bf16[128,256]{1,0:T(8,128)(2,1)S(1)} %bitcast.12), channel_id=1, source_target_pairs={{0,4},{4,0},{8,12},{12,8},{1,5},{5,1},{9,13},{13,9},{2,6},{6,2},{1... | collective-permute-start | bytes 196616 | tf_op jit(solution)/shard_map/ppermute | solution.py:22
  43.7 5.7 %collective-permute-start.17 = (bf16[128,256]{1,0:T(8,128)(2,1)S(1)}, bf16[128,256]{1,0:T(8,128)(2,1)S(1)}, u32[]{:S(2)}, u32[]{:S(2)}) collective-permute-start(bf16[128,256]{1,0:T(8,128)(2,1)S(1)} %bitcast.13), channel_id=1, source_target_pairs={{0,8},{4,12},{8,0},{12,4},{1,9},{5,13},{9,1},{13,5},{2,10},{6,14},... | collective-permute-start | bytes 196616 | tf_op jit(solution)/shard_map/ppermute | solution.py:22
  44.4 6.2 %collective-permute-start.18 = (bf16[128,256]{1,0:T(8,128)(2,1)S(1)}, bf16[128,256]{1,0:T(8,128)(2,1)S(1)}, u32[]{:S(2)}, u32[]{:S(2)}) collective-permute-start(bf16[128,256]{1,0:T(8,128)(2,1)S(1)} %bitcast.14), channel_id=1, source_target_pairs={{0,12},{4,8},{8,4},{12,0},{1,13},{5,9},{9,5},{13,1},{2,14},{6,10},... | collective-permute-start | bytes 196616 | tf_op jit(solution)/shard_map/ppermute | solution.py:22
  52.1 1.6 %collective-permute-start.19 = (bf16[160,896]{1,0:T(8,128)(2,1)S(1)}, bf16[160,896]{1,0:T(8,128)(2,1)S(1)}, u32[]{:S(2)}, u32[]{:S(2)}) collective-permute-start(bf16[160,896]{1,0:T(8,128)(2,1)S(1)} %get-tuple-element.86), channel_id=1, source_target_pairs={{0,1},{1,0},{2,3},{3,2},{4,5},{5,4},{6,7},{7,6},{8,9},{9,8},{10,11... | collective-permute-start | bytes 860168 | tf_op jit(solution)/shard_map/ppermute | solution.py:22
  52.2 4.1 %collective-permute-start.13 = (bf16[160,256]{1,0:T(8,128)(2,1)S(1)}, bf16[160,256]{1,0:T(8,128)(2,1)S(1)}, u32[]{:S(2)}, u32[]{:S(2)}) collective-permute-start(bf16[160,256]{1,0:T(8,128)(2,1)S(1)} %get-tuple-element.81), channel_id=1, source_target_pairs={{0,1},{1,0},{2,3},{3,2},{4,5},{5,4},{6,7},{7,6},{8,9},{9,8},{10,11... | collective-permute-start | bytes 245768 | tf_op jit(solution)/shard_map/ppermute | solution.py:22
  53.8 9.8 %collective-permute-start.20 = (bf16[160,896]{1,0:T(8,128)(2,1)S(1)}, bf16[160,896]{1,0:T(8,128)(2,1)S(1)}, u32[]{:S(2)}, u32[]{:S(2)}) collective-permute-start(bf16[160,896]{1,0:T(8,128)(2,1)S(1)} %add_convert_fusion.1), channel_id=1, source_target_pairs={{0,2},{2,0},{1,3},{3,1},{4,6},{6,4},{5,7},{7,5},{8,10},{10,8},{9,1... | collective-permute-start | bytes 860168 | tf_op jit(solution)/shard_map/ppermute | solution.py:22
  56.3 1.6 %collective-permute-start.22 = (bf16[272,512]{1,0:T(8,128)(2,1)S(1)}, bf16[272,512]{1,0:T(8,128)(2,1)S(1)}, u32[]{:S(2)}, u32[]{:S(2)}) collective-permute-start(bf16[272,512]{1,0:T(8,128)(2,1)S(1)} %get-tuple-element.88), channel_id=1, source_target_pairs={{0,1},{1,0},{2,3},{3,2},{4,5},{5,4},{6,7},{7,6},{8,9},{9,8},{10,11... | collective-permute-start | bytes 835592 | tf_op jit(solution)/shard_map/ppermute | solution.py:22
  56.3 9.0 %collective-permute-start.14 = (bf16[160,256]{1,0:T(8,128)(2,1)S(1)}, bf16[160,256]{1,0:T(8,128)(2,1)S(1)}, u32[]{:S(2)}, u32[]{:S(2)}) collective-permute-start(bf16[160,256]{1,0:T(8,128)(2,1)S(1)} %add_convert_fusion.3), channel_id=1, source_target_pairs={{0,2},{2,0},{1,3},{3,1},{4,6},{6,4},{5,7},{7,5},{8,10},{10,8},{9,1... | collective-permute-start | bytes 245768 | tf_op jit(solution)/shard_map/ppermute | solution.py:22
  58.0 9.7 %collective-permute-start.23 = (bf16[144,512]{1,0:T(8,128)(2,1)S(1)}, bf16[144,512]{1,0:T(8,128)(2,1)S(1)}, u32[]{:S(2)}, u32[]{:S(2)}) collective-permute-start(bf16[144,512]{1,0:T(8,128)(2,1)S(1)} %get-tuple-element.90), channel_id=1, source_target_pairs={{0,2},{2,0},{1,3},{3,1},{4,6},{6,4},{5,7},{7,5},{8,10},{10,8},{9,1... | collective-permute-start | bytes 442376 | tf_op jit(solution)/shard_map/ppermute | solution.py:22
  63.7 12.3 %collective-permute-start.21 = (bf16[160,896]{1,0:T(8,128)(2,1)S(1)}, bf16[160,896]{1,0:T(8,128)(2,1)S(1)}, u32[]{:S(2)}, u32[]{:S(2)}) collective-permute-start(bf16[160,896]{1,0:T(8,128)(2,1)S(1)} %add_convert_fusion.refs_2_), channel_id=1, source_target_pairs={{0,1},{1,0},{2,3},{3,2},{4,5},{5,4},{6,7},{7,6},{8,9},{9,8},{10,11... | collective-permute-start | bytes 860168 | tf_op jit(solution)/shard_map/ppermute | solution.py:22
  65.4 6.8 %collective-permute-start.15 = (bf16[160,256]{1,0:T(8,128)(2,1)S(1)}, bf16[160,256]{1,0:T(8,128)(2,1)S(1)}, u32[]{:S(2)}, u32[]{:S(2)}) collective-permute-start(bf16[160,256]{1,0:T(8,128)(2,1)S(1)} %add_convert_fusion.2.refs_0_), channel_id=1, source_target_pairs={{0,1},{1,0},{2,3},{3,2},{4,5},{5,4},{6,7},{7,6},{8,9},{9,8},{10,11... | collective-permute-start | bytes 245768 | tf_op jit(solution)/shard_map/ppermute | solution.py:22
  67.7 4.5 %collective-permute-start.24 = (bf16[48,512]{1,0:T(8,128)(2,1)S(1)}, bf16[48,512]{1,0:T(8,128)(2,1)S(1)}, u32[]{:S(2)}, u32[]{:S(2)}) collective-permute-start(bf16[48,512]{1,0:T(8,128)(2,1)S(1)} %get-tuple-element.92), channel_id=1, source_target_pairs={{0,4},{4,0},{8,12},{12,8},{1,5},{5,1},{9,13},{13,9},{2,6},{6,2},{1... | collective-permute-start | bytes 147464 | tf_op jit(solution)/shard_map/ppermute | solution.py:22
  68.6 6.0 %collective-permute-start.25 = (bf16[48,512]{1,0:T(8,128)(2,1)S(1)}, bf16[48,512]{1,0:T(8,128)(2,1)S(1)}, u32[]{:S(2)}, u32[]{:S(2)}) collective-permute-start(bf16[48,512]{1,0:T(8,128)(2,1)S(1)} %get-tuple-element.93), channel_id=1, source_target_pairs={{0,8},{4,12},{8,0},{12,4},{1,9},{5,13},{9,1},{13,5},{2,10},{6,14},... | collective-permute-start | bytes 147464 | tf_op jit(solution)/shard_map/ppermute | solution.py:22
  70.1 5.9 %collective-permute-start.26 = (bf16[48,512]{1,0:T(8,128)(2,1)S(1)}, bf16[48,512]{1,0:T(8,128)(2,1)S(1)}, u32[]{:S(2)}, u32[]{:S(2)}) collective-permute-start(bf16[48,512]{1,0:T(8,128)(2,1)S(1)} %get-tuple-element.94), channel_id=1, source_target_pairs={{0,12},{4,8},{8,4},{12,0},{1,13},{5,9},{9,5},{13,1},{2,14},{6,10},... | collective-permute-start | bytes 147464 | tf_op jit(solution)/shard_map/ppermute | solution.py:22
